TPU v7x, 512 devices: a whole 4x4x16 slice. The times are simulated.
512 devices in a mesh: seq: 128 (over z, y, core), head: 4 (over x).
Axes of the slice: x: 4, y: 4, z: 16, core: 2. Of those that a mesh axis runs over, the one named last changes fastest.
Arguments:
- query: bfloat16 [6144, 1536], P('seq', 'head'), may hold values from -64 to 64
- new_kv: bfloat16 [2, 6144, 1536], P(None, 'seq', 'head'), may hold values from -6 to 6
- cache_kv: bfloat16 [2, 16384, 1536], P(None, 'seq', 'head'), may hold values from -6 to 6
- text_kv: bfloat16 [2, 512, 1536], P(None, None, 'head'), may hold values from -8 to 8
- active: int32 [6144], P('seq'), may hold values from 0 to 16383, as said below
- counts: int32 [128], P('seq'), may hold values from 0 to 48, as said below
- hidden: bfloat16 [6144, 3072], P('seq', 'head'), may hold values from -64 to 64
- w_out: bfloat16 [1536, 3072], P('head'), may hold values from -0.4375 to 0.4375
- mod_shift: float32 [3072], P('head'), may hold values from -3 to 3
- mod_scale: float32 [3072], P('head'), may hold values from -3 to 3
- w_final: float32 [3072, 64], P('head'), may hold values from -0.109375 to 0.109375
- latent: float32 [16384, 64], P('seq'), may hold values from -6 to 6
- cached_velocity: float32 [16384, 64], P('seq'), may hold values from -6 to 6
- step_size: float32 [1], replicated, may hold values from -0.6 to -0.1
Outputs:
- velocity: float32 [16384, 64], P('seq')
- latent_next: float32 [16384, 64], P('seq')
Inputs may be any that keep to these rules, and one draw needn't show every extreme that they name: `active`: for shard k, the entries k * 48 to k * 48 + counts[k] - 1 are distinct image tokens of that shard (k * 128 to (k + 1) * 128 - 1); the later entries of the shard are tokens of the same shard and carry no meaning. The counts sum to exactly 24 times the number of shards; some shard has 48 and some shard has 0.
All inputs are finite; a program needn't handle non-finite values.
Results may differ from a plain program's by a relative error of at most 0.0035.
Values may be sent and summed in bfloat16 or wider, within the bound.
No kernel may reach another device: no remote copies, remote signals or barrier semaphores. Data moves between devices by JAX's collectives and lax.ppermute only.
A program may use at most 128 MiB of HBM per device.

v0:
```python
import functools

import jax
import jax.numpy as jnp
from jax import lax
from jax.experimental import pallas as pl
from jax.experimental.pallas import tpu as pltpu
from jax.sharding import PartitionSpec as P


D = 3072
HD = 128
EPS = 1e-06
LOG2E = 1.4426950408889634
SCALE = HD ** (-0.5)
SEQ = ("zb", "za", "y", "core")
STAT = 8


f32 = jnp.float32
bf16 = jnp.bfloat16
VM = pl.BlockSpec(memory_space=pltpu.VMEM)
SM = pl.BlockSpec(memory_space=pltpu.SMEM)


def one_hot(pos_ref, info_ref, rows, cols):
    local = pos_ref[...] - info_ref[0]
    slot = lax.broadcasted_iota(jnp.int32, (1, cols), 1)
    local = jnp.where(slot < info_ref[1], local, -1)
    return lax.broadcasted_iota(jnp.int32, (rows, cols), 0) == local


def fill_kernel(info_ref, pos_ref, new_ref, cache_ref, out_ref):
    rows, cols = cache_ref.shape[1], new_ref.shape[1]
    matched = one_hot(pos_ref, info_ref, rows, cols)
    pick = matched.astype(f32)
    keep = jnp.max(pick, axis=1, keepdims=True) < 0.5
    pick = pick.astype(bf16)
    for s in range(2):
        placed = jnp.dot(pick, new_ref[s], preferred_element_type=f32)
        merged = jnp.where(keep, cache_ref[s].astype(f32), placed).astype(bf16)
        for y in range(out_ref.shape[0]):
            out_ref[y, s] = merged


def fill(info, pos, new_kv, cache_kv, copies):
    return pl.pallas_call(
        fill_kernel,
        out_shape=jax.ShapeDtypeStruct((copies,) + cache_kv.shape, bf16),
        in_specs=[SM, VM, VM, VM],
        out_specs=VM,
    )(info, pos, new_kv, cache_kv)


def attend_kernel(part_ref, q_ref, a_ref, b_ref, t_ref, out_ref, *, chunk):
    del part_ref
    slots = out_ref.shape[1] - STAT
    keys, values = [], []
    for ref in (a_ref, b_ref):
        n = ref.shape[0] * ref.shape[2]
        keys.append(ref[:, 0].reshape(n, HD))
        values.append(ref[:, 1].reshape(n, HD))
    keys.append(t_ref[0])
    values.append(t_ref[1])
    lane = lax.broadcasted_iota(jnp.int32, (slots, HD), 1)
    eye = lax.broadcasted_iota(jnp.int32, (slots, HD), 0) == lane
    row = lax.broadcasted_iota(jnp.int32, (STAT, HD), 0)
    for start in range(0, q_ref.shape[0], chunk):
        q = q_ref[pl.ds(start, chunk), :]
        scores = [
            lax.dot_general(q, k, (((1,), (1,)), ((), ())), preferred_element_type=f32)
            for k in keys
        ]
        top = functools.reduce(
            jnp.maximum, [jnp.max(s, axis=1, keepdims=True) for s in scores]
        )
        weights = [jnp.exp2((s - top) * (SCALE * LOG2E)) for s in scores]
        total = sum(jnp.sum(w, axis=1, keepdims=True) for w in weights)
        mixed = sum(
            jnp.dot(w.astype(bf16), v, preferred_element_type=f32)
            for w, v in zip(weights, values)
        )
        mixed = mixed / total
        spread = top * SCALE + jnp.log(total)
        for i in range(chunk // slots):
            d = start // slots + i
            out_ref[d, 0:slots, :] = mixed[i * slots : (i + 1) * slots].astype(bf16)
            column = spread[i * slots : (i + 1) * slots]
            line = jnp.sum(jnp.where(eye, column, 0.0), axis=0, keepdims=True)
            first = line.astype(bf16).astype(f32)
            second = (line - first).astype(bf16).astype(f32)
            third = line - first - second
            pieces = jnp.where(row == 0, first, jnp.where(row == 1, second, third))
            out_ref[d, slots : slots + STAT, :] = pieces.astype(bf16)


def attend(part, parts, queries, near, far, text_kv, slots, chunk):
    rows, width = queries.shape
    text_rows = text_kv.shape[1] // parts
    kv_spec = pl.BlockSpec(near.shape[:3] + (HD,), lambda h, part: (0, 0, 0, h))
    return pl.pallas_call(
        functools.partial(attend_kernel, chunk=chunk),
        out_shape=jax.ShapeDtypeStruct((parts, slots + STAT, width), bf16),
        grid_spec=pltpu.PrefetchScalarGridSpec(
            num_scalar_prefetch=1,
            grid=(width // HD,),
            in_specs=[
                pl.BlockSpec((rows, HD), lambda h, part: (0, h)),
                kv_spec,
                kv_spec,
                pl.BlockSpec((2, text_rows, HD), lambda h, part: (0, part[0], h)),
            ],
            out_specs=pl.BlockSpec((parts, slots + STAT, HD), lambda h, part: (0, 0, h)),
        ),
    )(part, queries, near, far, text_kv)


def merge_kernel(got_ref, w_ref, out_ref):
    parts, rows, width = got_ref.shape
    slots = rows - STAT
    heads = []
    for h in range(width // HD):
        cols = slice(h * HD, (h + 1) * HD)
        stat = got_ref[:, slots:rows, cols].astype(f32)
        spread = stat[:, 0] + stat[:, 1] + stat[:, 2]
        share = jnp.exp(spread - jnp.max(spread, axis=0, keepdims=True))
        share = share / jnp.sum(share, axis=0, keepdims=True)
        share = jnp.concatenate([share, jnp.zeros((HD - parts, HD), f32)], axis=0).T
        total = jnp.zeros((slots, HD), f32)
        for s in range(parts):
            total += got_ref[s, 0:slots, cols].astype(f32) * share[0:slots, s : s + 1]
        heads.append(total.astype(bf16))
    attended = jnp.concatenate(heads, axis=1)
    piece = out_ref.shape[2]
    for k in range(out_ref.shape[0]):
        out_ref[k] = jnp.dot(
            attended, w_ref[:, k * piece : (k + 1) * piece], preferred_element_type=f32
        ).astype(bf16)


def merge(got, w_out, groups):
    return pl.pallas_call(
        merge_kernel,
        out_shape=jax.ShapeDtypeStruct(
            (groups, got.shape[1] - STAT, w_out.shape[1] // groups), bf16
        ),
        in_specs=[VM, VM],
        out_specs=VM,
    )(got, w_out)


def norm_kernel(got_ref, hidden_ref, scale_ref, shift_ref, w_ref, out_ref):
    slots, width = hidden_ref.shape
    summed = hidden_ref[...].astype(f32)
    for k in range(got_ref.shape[0]):
        summed += got_ref[k].astype(f32)
    mean = jnp.sum(summed, axis=1, keepdims=True) * (1.0 / width)
    centred = summed - mean
    squares = jnp.sum(centred * centred, axis=1, keepdims=True)
    lifted = 1.0 + scale_ref[...]
    tail = lax.broadcasted_iota(jnp.int32, (STAT, width), 0)
    tail = jnp.where(tail == 0, lifted, jnp.where(tail == 1, shift_ref[...], 0.0))
    rows = jnp.concatenate([centred * lifted, tail], axis=0)
    mapped = lax.dot_general(
        rows,
        w_ref[...],
        (((1,), (1,)), ((), ())),
        precision=lax.Precision.HIGHEST,
        preferred_element_type=f32,
    )
    lane = lax.broadcasted_iota(jnp.int32, (slots, 64), 1)
    stat = jnp.where(lane == 0, mean, jnp.where(lane == 1, squares, 0.0))
    stat = jnp.concatenate([stat, jnp.zeros((STAT, 64), f32)], axis=0)
    block = jnp.concatenate([mapped, stat], axis=1)
    for k in range(out_ref.shape[0]):
        out_ref[k] = block


def norm(got, hidden, scale, shift, w_final):
    return pl.pallas_call(
        norm_kernel,
        out_shape=jax.ShapeDtypeStruct(
            (got.shape[0], hidden.shape[0] + STAT, 2 * w_final.shape[1]), f32
        ),
        in_specs=[VM] * 5,
        out_specs=VM,
    )(got, hidden, scale, shift, w_final.T)


def finish_kernel(
    info_ref, step_ref, pos_ref, got_ref, latent_ref, old_ref, velocity_ref, next_ref
):
    groups, rows, _ = got_ref.shape
    slots = rows - STAT
    ch = latent_ref.shape[0]
    blocks = [got_ref[k] for k in range(groups)]
    means = [b[0:slots, ch : ch + 1] for b in blocks]
    mean = sum(means) * (1.0 / groups)
    width = D // groups
    var = sum(b[0:slots, ch + 1 : ch + 2] for b in blocks)
    var = (var + width * sum((m - mean) * (m - mean) for m in means)) * (1.0 / D)
    mapped = sum(
        b[0:slots, 0:ch] + (m - mean) * b[slots : slots + 1, 0:ch]
        for b, m in zip(blocks, means)
    )
    base = sum(b[slots + 1 : slots + 2, 0:ch] for b in blocks)
    fresh = mapped * lax.rsqrt(var + EPS) + base
    tokens = latent_ref.shape[1]
    pick = one_hot(pos_ref, info_ref, tokens, slots).astype(f32)
    keep = lax.dot_general(
        jnp.ones((8, slots), f32),
        pick,
        (((1,), (1,)), ((), ())),
        preferred_element_type=f32,
    )[0:1]
    chosen = lax.dot_general(
        fresh,
        pick,
        (((0,), (1,)), ((), ())),
        precision=lax.Precision.HIGHEST,
        preferred_element_type=f32,
    )
    velocity = jnp.where(keep < 0.5, old_ref[...], chosen)
    velocity_ref[...] = velocity
    next_ref[...] = latent_ref[...] + step_ref[0] * velocity


def finish(info, step_size, pos, got, latent, cached_velocity):
    velocity, following = pl.pallas_call(
        finish_kernel,
        out_shape=(
            jax.ShapeDtypeStruct(latent.shape[::-1], f32),
            jax.ShapeDtypeStruct(latent.shape[::-1], f32),
        ),
        in_specs=[SM, SM, VM, VM, VM, VM],
        out_specs=(VM, VM),
    )(info, step_size, pos, got, latent.T, cached_velocity.T)
    return velocity.T, following.T


def on_device(
    query,
    new_kv,
    cache_kv,
    text_kv,
    active,
    counts,
    hidden,
    w_out,
    mod_shift,
    mod_scale,
    w_final,
    latent,
    cached_velocity,
    step_size,
):
    groups = lax.axis_size("head")
    planes = lax.axis_size("zb")
    block = lax.axis_index("zb")
    own = lax.axis_index(SEQ)
    slots = query.shape[0]
    tokens = cache_kv.shape[1]
    near_axes = ("za", "y")
    copies = lax.axis_size(near_axes)

    info = jnp.stack([own * tokens, counts[0]]).astype(jnp.int32)
    pos = active.reshape(1, slots)
    gathered = lax.all_gather(query, "zb", axis=0, tiled=True)
    filled = fill(info, pos, new_kv, cache_kv, copies)
    near = lax.all_to_all(filled, near_axes, 0, 0, tiled=True)
    far = lax.ppermute(near, "core", [(0, 1), (1, 0)])
    part = block.reshape(1).astype(jnp.int32)
    partial = attend(part, planes, gathered, near, far, text_kv, slots, 192)
    returned = lax.all_to_all(partial, "zb", 0, 0, tiled=True)
    terms = merge(returned, w_out, groups)
    terms = lax.all_to_all(terms, "head", 0, 0, tiled=True)
    stats = norm(
        terms, hidden, mod_scale.reshape(1, -1), mod_shift.reshape(1, -1), w_final
    )
    stats = lax.all_to_all(stats, "head", 0, 0, tiled=True)
    return finish(info, step_size, pos, stats, latent, cached_velocity)


def solution(mesh):
    in_specs = (
        P(SEQ, "head"),
        P(None, SEQ, "head"),
        P(None, SEQ, "head"),
        P(None, None, "head"),
        P(SEQ),
        P(SEQ),
        P(SEQ, "head"),
        P("head", None),
        P("head"),
        P("head"),
        P("head", None),
        P(SEQ, None),
        P(SEQ, None),
        P(),
    )
    out_specs = (P(SEQ, None), P(SEQ, None))
    split = jax.sharding.Mesh(
        mesh.devices.reshape(8, 2, 4, 2, mesh.shape["head"]), SEQ + ("head",)
    )

    return jax.shard_map(
        on_device, mesh=split, in_specs=in_specs, out_specs=out_specs, check_vma=False
    )
```

profile of v0, /device:TPU:24, one launch (start us, length us, event | category | flops | bytes accessed | tf_op | source)
XLA Modules:
  0.0 132.9 jit_solution(2742862676868982095)
XLA Ops:
  1.3 0.6 pad_add_fusion.info_ref
  1.9 2.5 %shard_map.149 = bf16[8,2,128,384]{3,2,1,0:T(8,128)(2,1)} custom-call(s32[2]{0:T(128)} %pad_add_fusion.info_ref, s32[1,48]{1,0:T(1,128)} %bitcast.11, bf16[2,48,384]{2,1,0:T(8,128)(2,1)} %new_ref.1, bf16[2,128,384]{2,1,0:T(8,128)(2,1)} %cache_ref.1), custom_call_target="tpu_custom_call" | custom-call | tf_op jit(solution)/shard_map/pallas_call | solution.py:47
  4.3 0.0 copy-start.4
  4.3 25.1 %all_to_all.20.a_ref = bf16[8,2,128,384]{3,2,1,0:T(8,128)(2,1)S(1)} all-to-all(bf16[8,2,128,384]{3,2,1,0:T(8,128)(2,1)} %shard_map.149), channel_id=1, replica_groups=mesh['zb'=8,'za'=2,'y'=4,'core'=2,'head'=4] {'za','y'}, dimensions={0} | all-to-all | bytes 3145728 | tf_op jit(solution)/shard_map/all_to_all | solution.py:270
  29.5 0.0 copy-start
  29.5 1.9 %collective-permute-start = (bf16[8,2,128,384]{3,2,1,0:T(8,128)(2,1)S(1)}, bf16[8,2,128,384]{3,2,1,0:T(8,128)(2,1)S(1)}, u32[]{:S(2)}, u32[]{:S(2)}) collective-permute-start(bf16[8,2,128,384]{3,2,1,0:T(8,128)(2,1)S(1)} %all_to_all.20.a_ref), channel_id=1, source_target_pairs={{0,4},{4,0},{1,5},{5,1},{2,6},{6,2},{3,7},{7,3},{8,12},{12,8},{9,1... | collective-permute-start | bytes 4718600 | tf_op jit(solution)/shard_map/ppermute | solution.py:271
  31.4 0.0 copy-done.4
  31.4 37.4 %all_gather.3.q_ref = bf16[384,384]{1,0:T(8,128)(2,1)} all-gather(bf16[48,384]{1,0:T(8,128)(2,1)S(1)} %copy-done.4), channel_id=1, replica_groups=mesh['zb'=8,'za'=2,'y'=4,'core'=2,'head'=4] {'zb'}, dimensions={0}, use_global_device_ids=true | all-gather | bytes 331776 | tf_op jit(solution)/shard_map/all_gather | solution.py:268
  68.8 0.0 collective-permute-done.b_ref
  68.8 0.0 copy-start.1
  68.8 0.0 copy-done
  68.8 1.1 copy-done.1
  70.0 6.9 %shard_map.150 = bf16[8,56,384]{2,1,0:T(8,128)(2,1)} custom-call(s32[1]{0:T(128)} %bitcast.2.part_ref, bf16[384,384]{1,0:T(8,128)(2,1)} %all_gather.3.q_ref, bf16[8,2,128,384]{3,2,1,0:T(8,128)(2,1)} %copy-done, bf16[8,2,128,384]{3,2,1,0:T(8,128)(2,1)} %copy-done.1, bf16[2,512,384]{2,1,0:T(8,128)(2,1)} %t_ref.1), custom_call_target="tpu_custom_call" | custom-call | tf_op jit(solution)/shard_map/pallas_call | solution.py:101
  76.9 26.7 %all_to_all.21.got_ref = bf16[8,56,384]{2,1,0:T(8,128)(2,1)} all-to-all(bf16[8,56,384]{2,1,0:T(8,128)(2,1)} %shard_map.150), channel_id=1, replica_groups=mesh['zb'=8,'za'=2,'y'=4,'core'=2,'head'=4] {'zb'}, dimensions={0} | all-to-all | bytes 688128 | tf_op jit(solution)/shard_map/all_to_all | solution.py:274
  103.6 0.0 copy-start.5
  103.6 0.0 copy-start.6
  103.6 3.3 %shard_map.151 = bf16[4,48,768]{2,1,0:T(8,128)(2,1)} custom-call(bf16[8,56,384]{2,1,0:T(8,128)(2,1)} %all_to_all.21.got_ref, bf16[384,3072]{1,0:T(8,128)(2,1)} %w_ref.1), custom_call_target="tpu_custom_call" | custom-call | tf_op jit(solution)/shard_map/pallas_call | solution.py:142
  106.9 4.4 %all-to-all-start.2 = ((bf16[4,48,768]{2,1,0:T(8,128)(2,1)}), bf16[4,48,768]{2,1,0:T(8,128)(2,1)S(1)}, u32[]{:S(2)}, u32[]{:S(2)}) async-start(bf16[4,48,768]{2,1,0:T(8,128)(2,1)} %shard_map.151), calls=%async_computation.2 | async-start | bytes 589824 | tf_op jit(solution)/shard_map/all_to_all | solution.py:276
  111.4 0.0 copy-done.5
  111.4 0.6 reshape.18.scale_ref
  111.9 0.0 copy-done.6
  111.9 0.6 reshape.19.shift_ref
  112.5 5.7 %all-to-all-done.2.got_ref = bf16[4,48,768]{2,1,0:T(8,128)(2,1)S(1)} async-done(((bf16[4,48,768]{2,1,0:T(8,128)(2,1)}), bf16[4,48,768]{2,1,0:T(8,128)(2,1)S(1)}, u32[]{:S(2)}, u32[]{:S(2)}) %all-to-all-start.2) | async-done | bytes 294944 | tf_op jit(solution)/shard_map/all_to_all | solution.py:276
  118.2 0.0 copy-start.2
  118.2 0.7 copy-done.2
  118.9 2.1 %shard_map.152 = f32[4,56,128]{2,1,0:T(8,128)} custom-call(bf16[4,48,768]{2,1,0:T(8,128)(2,1)} %copy-done.2, bf16[48,768]{1,0:T(8,128)(2,1)} %hidden_ref.1, f32[1,768]{1,0:T(1,128)} %reshape.18.scale_ref, f32[1,768]{1,0:T(1,128)} %reshape.19.shift_ref, f32[64,768]{1,0:T(8,128)} %bitcast.8), custom_call_target="tpu_custom_call" | custom-call | tf_op jit(solution)/shard_map/pallas_call | solution.py:180
  121.1 3.3 %all-to-all-start.3 = ((f32[4,56,128]{2,1,0:T(8,128)}), f32[4,56,128]{2,1,0:T(8,128)S(1)}, u32[]{:S(2)}, u32[]{:S(2)}) async-start(f32[4,56,128]{2,1,0:T(8,128)} %shard_map.152), calls=%async_computation.3 | async-start | bytes 229376 | tf_op jit(solution)/shard_map/all_to_all | solution.py:280
  125.0 5.2 %all-to-all-done.3.got_ref = f32[4,56,128]{2,1,0:T(8,128)S(1)} async-done(((f32[4,56,128]{2,1,0:T(8,128)}), f32[4,56,128]{2,1,0:T(8,128)S(1)}, u32[]{:S(2)}, u32[]{:S(2)}) %all-to-all-start.3) | async-done | bytes 114720 | tf_op jit(solution)/shard_map/all_to_all | solution.py:280
  130.2 0.0 copy-start.3
  130.2 0.6 copy-done.3
  130.9 2.0 %shard_map.153 = (f32[64,128]{1,0:T(8,128)}, f32[64,128]{1,0:T(8,128)}) custom-call(s32[2]{0:T(128)} %pad_add_fusion.info_ref, f32[1]{0:T(128)S(6)} %copy.17.step_ref, s32[1,48]{1,0:T(1,128)} %bitcast.12, f32[4,56,128]{2,1,0:T(8,128)} %copy-done.3, f32[64,128]{1,0:T(8,128)} %bitcast.9, f32[64,128]{1,0:T(8,128)} %bitcast.10), custom_call_target="tpu_custom_call" | custom-call | tf_op jit(solution)/shard_map/pallas_call | solution.py:229
Async XLA Ops:
  4.3 27.1 %copy-start.4 = (bf16[48,384]{1,0:T(8,128)(2,1)S(1)}, bf16[48,384]{1,0:T(8,128)(2,1)}, u32[]{:S(2)}) copy-start(bf16[48,384]{1,0:T(8,128)(2,1)} %param.14) | copy-start | bytes 110596
  29.5 39.4 %copy-start = (bf16[8,2,128,384]{3,2,1,0:T(8,128)(2,1)}, bf16[8,2,128,384]{3,2,1,0:T(8,128)(2,1)S(1)}, u32[]{:S(2)}) copy-start(bf16[8,2,128,384]{3,2,1,0:T(8,128)(2,1)S(1)} %all_to_all.20.a_ref) | copy-start | bytes 4718596
  29.5 39.3 %collective-permute-start = (bf16[8,2,128,384]{3,2,1,0:T(8,128)(2,1)S(1)}, bf16[8,2,128,384]{3,2,1,0:T(8,128)(2,1)S(1)}, u32[]{:S(2)}, u32[]{:S(2)}) collective-permute-start(bf16[8,2,128,384]{3,2,1,0:T(8,128)(2,1)S(1)} %all_to_all.20.a_ref), channel_id=1, source_target_pairs={{0,4},{4,0},{1,5},{5,1},{2,6},{6,2},{3,7},{7,3},{8,12},{12,8},{9,1... | collective-permute-start | bytes 4718600 | tf_op jit(solution)/shard_map/ppermute | solution.py:271
  68.8 1.2 copy-start.1
  103.6 7.8 %copy-start.5 = (f32[768]{0:T(1024)S(1)}, f32[768]{0:T(1024)}, u32[]{:S(2)}) copy-start(f32[768]{0:T(1024)} %param.23) | copy-start | bytes 9220
  103.6 8.3 %copy-start.6 = (f32[768]{0:T(1024)S(1)}, f32[768]{0:T(1024)}, u32[]{:S(2)}) copy-start(f32[768]{0:T(1024)} %param.22) | copy-start | bytes 9220
  106.9 11.3 %all-to-all-start.2 = ((bf16[4,48,768]{2,1,0:T(8,128)(2,1)}), bf16[4,48,768]{2,1,0:T(8,128)(2,1)S(1)}, u32[]{:S(2)}, u32[]{:S(2)}) async-start(bf16[4,48,768]{2,1,0:T(8,128)(2,1)} %shard_map.151), calls=%async_computation.2 | async-start | bytes 589824 | tf_op jit(solution)/shard_map/all_to_all | solution.py:276
  118.2 0.7 copy-start.2
  121.1 9.2 %all-to-all-start.3 = ((f32[4,56,128]{2,1,0:T(8,128)}), f32[4,56,128]{2,1,0:T(8,128)S(1)}, u32[]{:S(2)}, u32[]{:S(2)}) async-start(f32[4,56,128]{2,1,0:T(8,128)} %shard_map.152), calls=%async_computation.3 | async-start | bytes 229376 | tf_op jit(solution)/shard_map/all_to_all | solution.py:280
  130.2 0.6 copy-start.3
where the time goes:
time: 135 us; the launch traced here: 133 us
  blocking collectives  89.2 us (66%)
  Pallas kernels  16.9 us (13%)
  waiting for transfers between devices  10.9 us (8%)
  starting transfers between devices  9.63 us (7%)
  local copies, waits for them, and re-layouts  3.67 us (3%)
  between operations  1.97 us (1%)
    all_gather x1, blocking collectives, on_device(): gathered = lax.all_gather(query, 'zb', axis=0, tiled=True)  37.4 us
    all_to_all x1, blocking collectives, on_device(): returned = lax.all_to_all(partial, 'zb', 0, 0, tiled=True)  26.7 us
    all_to_all x1, blocking collectives, on_device(): near = lax.all_to_all(filled, near_axes, 0, 0, tiled=True)  25.1 us
    pallas_call x1, Pallas kernels, attend(): pl.pallas_call(functools.partial(attend_kernel, chunk=chunk), out_shape=j...  6.93 us
    all_to_all x1, waiting for transfers between devices, on_device(): terms = lax.all_to_all(terms, 'head', 0, 0, tiled=True)  5.69 us
    all_to_all x1, waiting for transfers between devices, on_device(): stats = lax.all_to_all(stats, 'head', 0, 0, tiled=True)  5.21 us
    all_to_all x1, starting transfers between devices, on_device(): terms = lax.all_to_all(terms, 'head', 0, 0, tiled=True)  4.41 us
    pallas_call x1, Pallas kernels, merge(): pl.pallas_call(merge_kernel, out_shape=jax.ShapeDtypeStruct((groups, got....  3.35 us
  transfers between devices with their start and end apart: 3, of which 2 were waited for; matrix products, arithmetic and copies ran while one was open for 1% of the time, Pallas kernels for 0%

commit v1 on v0

--- a/solution.py
+++ b/solution.py
@@ -13,7 +13,7 @@
 EPS = 1e-06
 LOG2E = 1.4426950408889634
 SCALE = HD ** (-0.5)
-SEQ = ("zb", "za", "y", "core")
+SEQ = ("zh", "zl", "y", "core")
 STAT = 8
 
 
@@ -39,14 +39,13 @@
     for s in range(2):
         placed = jnp.dot(pick, new_ref[s], preferred_element_type=f32)
         merged = jnp.where(keep, cache_ref[s].astype(f32), placed).astype(bf16)
-        for y in range(out_ref.shape[0]):
-            out_ref[y, s] = merged
-
-
-def fill(info, pos, new_kv, cache_kv, copies):
+        out_ref[s] = merged
+
+
+def fill(info, pos, new_kv, cache_kv):
     return pl.pallas_call(
         fill_kernel,
-        out_shape=jax.ShapeDtypeStruct((copies,) + cache_kv.shape, bf16),
+        out_shape=jax.ShapeDtypeStruct(cache_kv.shape, bf16),
         in_specs=[SM, VM, VM, VM],
         out_specs=VM,
     )(info, pos, new_kv, cache_kv)
@@ -255,23 +254,23 @@
     step_size,
 ):
     groups = lax.axis_size("head")
-    planes = lax.axis_size("zb")
-    block = lax.axis_index("zb")
+    around = ("zl", "y")
+    parts = lax.axis_size(around)
     own = lax.axis_index(SEQ)
     slots = query.shape[0]
     tokens = cache_kv.shape[1]
-    near_axes = ("za", "y")
-    copies = lax.axis_size(near_axes)
 
     info = jnp.stack([own * tokens, counts[0]]).astype(jnp.int32)
     pos = active.reshape(1, slots)
-    gathered = lax.all_gather(query, "zb", axis=0, tiled=True)
-    filled = fill(info, pos, new_kv, cache_kv, copies)
-    near = lax.all_to_all(filled, near_axes, 0, 0, tiled=True)
+    filled = fill(info, pos, new_kv, cache_kv)
+    near = lax.all_gather(filled, "zh", axis=0, tiled=False)
     far = lax.ppermute(near, "core", [(0, 1), (1, 0)])
-    part = block.reshape(1).astype(jnp.int32)
-    partial = attend(part, planes, gathered, near, far, text_kv, slots, 192)
-    returned = lax.all_to_all(partial, "zb", 0, 0, tiled=True)
+    asked = jnp.broadcast_to(query[None], (parts,) + query.shape)
+    gathered = lax.all_to_all(asked, around, 0, 0, tiled=True)
+    gathered = gathered.reshape(parts * slots, -1)
+    part = lax.axis_index(around).reshape(1).astype(jnp.int32)
+    partial = attend(part, parts, gathered, near, far, text_kv, slots, 192)
+    returned = lax.all_to_all(partial, around, 0, 0, tiled=True)
     terms = merge(returned, w_out, groups)
     terms = lax.all_to_all(terms, "head", 0, 0, tiled=True)
     stats = norm(
@@ -300,7 +299,7 @@
     )
     out_specs = (P(SEQ, None), P(SEQ, None))
     split = jax.sharding.Mesh(
-        mesh.devices.reshape(8, 2, 4, 2, mesh.shape["head"]), SEQ + ("head",)
+        mesh.devices.reshape(4, 4, 4, 2, mesh.shape["head"]), SEQ + ("head",)
     )
 
     return jax.shard_map(

time: 135 us -> 132 us (0.978)
  blocking collectives: 89.2 us -> 73 us
  starting transfers between devices: 9.63 us -> 18.3 us
  waiting for transfers between devices: 10.9 us -> 13.1 us
  local copies, waits for them, and re-layouts: 3.67 us -> 5.29 us
    all_to_all x2 -> x1, blocking collectives: 51.8 us -> 37.2 us  [on_device(): returned = lax.all_to_all(partial, around, 0, 0, tiled=True)]
    all_to_all x0 -> x1, starting transfers between devices: none -> 8.95 us  [on_device(): gathered = lax.all_to_all(asked, around, 0, 0, tiled=True)]
    ppermute x1, waiting for transfers between devices: 0.01 us -> 2.24 us  [on_device(): far = lax.ppermute(near, 'core', [(0, 1), (1, 0)])]
    broadcast_in_dim x0 -> x1, local copies, waits for them, and re-layouts: none -> 1.65 us  [on_device(): asked = jnp.broadcast_to(query[None], (parts,) + query.shape)]
    all_gather x1, blocking collectives: 37.4 us -> 35.8 us  [on_device(): near = lax.all_gather(filled, 'zh', axis=0, tiled=False)]
  transfers between devices with their start and end apart: 3 -> 4, of which waited for: 2 -> 3; matrix products, arithmetic and copies ran while one was open for 1% -> 1% of each run, Pallas kernels for 0% -> 1%
where the time goes in v1:
time: 132 us; the launch traced here: 130 us
  blocking collectives  73 us (55%)
  starting transfers between devices  18.3 us (14%)
  Pallas kernels  17.8 us (13%)
  waiting for transfers between devices  13.1 us (10%)
  local copies, waits for them, and re-layouts  5.29 us (4%)
  between operations  1.97 us (1%)
    all_to_all x1, blocking collectives, on_device(): returned = lax.all_to_all(partial, around, 0, 0, tiled=True)  37.2 us
    all_gather x1, blocking collectives, on_device(): near = lax.all_gather(filled, 'zh', axis=0, tiled=False)  35.8 us
    all_to_all x1, starting transfers between devices, on_device(): gathered = lax.all_to_all(asked, around, 0, 0, tiled=True)  8.95 us
    pallas_call x1, Pallas kernels, attend(): pl.pallas_call(functools.partial(attend_kernel, chunk=chunk), out_shape=j...  8.1 us
    all_to_all x1, waiting for transfers between devices, on_device(): terms = lax.all_to_all(terms, 'head', 0, 0, tiled=True)  5.69 us
    all_to_all x1, waiting for transfers between devices, on_device(): stats = lax.all_to_all(stats, 'head', 0, 0, tiled=True)  5.21 us
    all_to_all x1, starting transfers between devices, on_device(): terms = lax.all_to_all(terms, 'head', 0, 0, tiled=True)  4.14 us
    pallas_call x1, Pallas kernels, merge(): pl.pallas_call(merge_kernel, out_shape=jax.ShapeDtypeStruct((groups, got....  3.68 us
  transfers between devices with their start and end apart: 4, of which 3 were waited for; matrix products, arithmetic and copies ran while one was open for 1% of the time, Pallas kernels for 1%

profile of v1, /device:TPU:24, one launch (start us, length us, event | category | flops | bytes accessed | tf_op | source)
XLA Modules:
  0.0 130.1 jit_solution(12618283289863244243)
XLA Ops:
  0.6 1.7 %broadcast_in_dim.2 = bf16[16,48,384]{2,1,0:T(8,128)(2,1)} broadcast(bf16[48,384]{1,0:T(8,128)(2,1)} %param.14), dimensions={1,2} | broadcast | bytes 626688 | tf_op jit(solution)/shard_map/broadcast_in_dim | solution.py:268
  2.3 9.0 %all-to-all-start = ((bf16[16,48,384]{2,1,0:T(8,128)(2,1)}), bf16[16,48,384]{2,1,0:T(8,128)(2,1)S(1)}, u32[]{:S(2)}, u32[]{:S(2)}) async-start(bf16[16,48,384]{2,1,0:T(8,128)(2,1)} %broadcast_in_dim.2), calls=%async_computation | async-start | bytes 1179648 | tf_op jit(solution)/shard_map/all_to_all | solution.py:269
  11.9 0.7 pad_add_fusion.info_ref
  12.5 1.9 %shard_map.149 = bf16[2,128,384]{2,1,0:T(8,128)(2,1)} custom-call(s32[2]{0:T(128)} %pad_add_fusion.info_ref, s32[1,48]{1,0:T(1,128)} %bitcast.16, bf16[2,48,384]{2,1,0:T(8,128)(2,1)} %new_ref.1, bf16[2,128,384]{2,1,0:T(8,128)(2,1)} %cache_ref.1), custom_call_target="tpu_custom_call" | custom-call | tf_op jit(solution)/shard_map/pallas_call | solution.py:46
  14.4 35.8 %all-gather = bf16[8,128,384]{2,1,0:T(8,128)(2,1)S(1)} all-gather(bf16[2,128,384]{2,1,0:T(8,128)(2,1)} %shard_map.149), channel_id=2, replica_groups=mesh['zh'=4,'zl'=4,'y'=4,'core'=2,'head'=4] {'zh'}, dimensions={0}, use_global_device_ids=true | all-gather | bytes 983040 | tf_op jit(solution)/shard_map/all_gather | solution.py:266
  50.2 0.0 copy-start
  50.2 1.9 %collective-permute-start = (bf16[4,2,128,384]{3,2,1,0:T(8,128)(2,1)S(1)}, bf16[4,2,128,384]{3,2,1,0:T(8,128)(2,1)S(1)}, u32[]{:S(2)}, u32[]{:S(2)}) collective-permute-start(bf16[4,2,128,384]{3,2,1,0:T(8,128)(2,1)S(1)} %bitcast.10), channel_id=1, source_target_pairs={{0,4},{4,0},{1,5},{5,1},{2,6},{6,2},{3,7},{7,3},{8,12},{12,8},{9,1... | collective-permute-start | bytes 2359304 | tf_op jit(solution)/shard_map/ppermute | solution.py:267
  52.2 2.2 %collective-permute-done.b_ref = bf16[4,2,128,384]{3,2,1,0:T(8,128)(2,1)S(1)} collective-permute-done((bf16[4,2,128,384]{3,2,1,0:T(8,128)(2,1)S(1)}, bf16[4,2,128,384]{3,2,1,0:T(8,128)(2,1)S(1)}, u32[]{:S(2)}, u32[]{:S(2)}) %collective-permute-start) | collective-permute-done | bytes 786464 | tf_op jit(solution)/shard_map/ppermute | solution.py:267
  54.4 0.0 copy-start.3
  54.4 0.0 all-to-all-done
  54.4 0.0 copy-start.1
  54.4 0.0 copy-done
  54.4 0.9 copy-done.3
  55.3 0.2 copy-done.1
  55.5 8.1 %shard_map.150 = bf16[16,56,384]{2,1,0:T(8,128)(2,1)} custom-call(s32[1]{0:T(128)} %bitcast.2.part_ref, bf16[768,384]{1,0:T(8,128)(2,1)} %bitcast.12, bf16[4,2,128,384]{3,2,1,0:T(8,128)(2,1)} %bitcast.11, bf16[4,2,128,384]{3,2,1,0:T(8,128)(2,1)} %copy-done.3, bf16[2,512,384]{2,1,0:T(8,128)(2,1)} %t_ref.1), custom_call_target="tpu_custom_call" | custom-call | tf_op jit(solution)/shard_map/pallas_call | solution.py:100
  63.6 0.0 copy-start.5
  63.6 0.0 copy-start.6
  63.6 37.2 %all_to_all.20.got_ref = bf16[16,56,384]{2,1,0:T(8,128)(2,1)} all-to-all(bf16[16,56,384]{2,1,0:T(8,128)(2,1)} %shard_map.150), channel_id=1, replica_groups=mesh['zh'=4,'zl'=4,'y'=4,'core'=2,'head'=4] {'zl','y'}, dimensions={0} | all-to-all | bytes 1376256 | tf_op jit(solution)/shard_map/all_to_all | solution.py:273
  100.8 3.7 %shard_map.151 = bf16[4,48,768]{2,1,0:T(8,128)(2,1)} custom-call(bf16[16,56,384]{2,1,0:T(8,128)(2,1)} %all_to_all.20.got_ref, bf16[384,3072]{1,0:T(8,128)(2,1)} %w_ref.1), custom_call_target="tpu_custom_call" | custom-call | tf_op jit(solution)/shard_map/pallas_call | solution.py:141
  104.5 4.1 %all-to-all-start.2 = ((bf16[4,48,768]{2,1,0:T(8,128)(2,1)}), bf16[4,48,768]{2,1,0:T(8,128)(2,1)S(1)}, u32[]{:S(2)}, u32[]{:S(2)}) async-start(bf16[4,48,768]{2,1,0:T(8,128)(2,1)} %shard_map.151), calls=%async_computation.2 | async-start | bytes 589824 | tf_op jit(solution)/shard_map/all_to_all | solution.py:275
  108.6 0.0 copy-done.5
  108.7 0.6 reshape.23.scale_ref
  109.2 0.0 copy-done.6
  109.2 0.6 reshape.24.shift_ref
  109.8 5.7 %all-to-all-done.2.got_ref = bf16[4,48,768]{2,1,0:T(8,128)(2,1)S(1)} async-done(((bf16[4,48,768]{2,1,0:T(8,128)(2,1)}), bf16[4,48,768]{2,1,0:T(8,128)(2,1)S(1)}, u32[]{:S(2)}, u32[]{:S(2)}) %all-to-all-start.2) | async-done | bytes 294944 | tf_op jit(solution)/shard_map/all_to_all | solution.py:275
  115.5 0.0 copy-start.2
  115.5 0.7 copy-done.2
  116.2 2.1 %shard_map.152 = f32[4,56,128]{2,1,0:T(8,128)} custom-call(bf16[4,48,768]{2,1,0:T(8,128)(2,1)} %copy-done.2, bf16[48,768]{1,0:T(8,128)(2,1)} %hidden_ref.1, f32[1,768]{1,0:T(1,128)} %reshape.23.scale_ref, f32[1,768]{1,0:T(1,128)} %reshape.24.shift_ref, f32[64,768]{1,0:T(8,128)} %bitcast.13), custom_call_target="tpu_custom_call" | custom-call | tf_op jit(solution)/shard_map/pallas_call | solution.py:179
  118.3 3.3 %all-to-all-start.3 = ((f32[4,56,128]{2,1,0:T(8,128)}), f32[4,56,128]{2,1,0:T(8,128)S(1)}, u32[]{:S(2)}, u32[]{:S(2)}) async-start(f32[4,56,128]{2,1,0:T(8,128)} %shard_map.152), calls=%async_computation.3 | async-start | bytes 229376 | tf_op jit(solution)/shard_map/all_to_all | solution.py:279
  122.3 5.2 %all-to-all-done.3.got_ref = f32[4,56,128]{2,1,0:T(8,128)S(1)} async-done(((f32[4,56,128]{2,1,0:T(8,128)}), f32[4,56,128]{2,1,0:T(8,128)S(1)}, u32[]{:S(2)}, u32[]{:S(2)}) %all-to-all-start.3) | async-done | bytes 114720 | tf_op jit(solution)/shard_map/all_to_all | solution.py:279
  127.5 0.0 copy-start.4
  127.5 0.6 copy-done.4
  128.2 2.0 %shard_map.153 = (f32[64,128]{1,0:T(8,128)}, f32[64,128]{1,0:T(8,128)}) custom-call(s32[2]{0:T(128)} %pad_add_fusion.info_ref, f32[1]{0:T(128)S(6)} %copy.17.step_ref, s32[1,48]{1,0:T(1,128)} %bitcast.17, f32[4,56,128]{2,1,0:T(8,128)} %copy-done.4, f32[64,128]{1,0:T(8,128)} %bitcast.14, f32[64,128]{1,0:T(8,128)} %bitcast.15), custom_call_target="tpu_custom_call" | custom-call | tf_op jit(solution)/shard_map/pallas_call | solution.py:228
Async XLA Ops:
  2.3 52.1 %all-to-all-start = ((bf16[16,48,384]{2,1,0:T(8,128)(2,1)}), bf16[16,48,384]{2,1,0:T(8,128)(2,1)S(1)}, u32[]{:S(2)}, u32[]{:S(2)}) async-start(bf16[16,48,384]{2,1,0:T(8,128)(2,1)} %broadcast_in_dim.2), calls=%async_computation | async-start | bytes 1179648 | tf_op jit(solution)/shard_map/all_to_all | solution.py:269
  50.2 4.2 %copy-start = (bf16[8,128,384]{2,1,0:T(8,128)(2,1)}, bf16[8,128,384]{2,1,0:T(8,128)(2,1)S(1)}, u32[]{:S(2)}) copy-start(bf16[8,128,384]{2,1,0:T(8,128)(2,1)S(1)} %all-gather) | copy-start | bytes 2359300
  50.2 4.2 %collective-permute-start = (bf16[4,2,128,384]{3,2,1,0:T(8,128)(2,1)S(1)}, bf16[4,2,128,384]{3,2,1,0:T(8,128)(2,1)S(1)}, u32[]{:S(2)}, u32[]{:S(2)}) collective-permute-start(bf16[4,2,128,384]{3,2,1,0:T(8,128)(2,1)S(1)} %bitcast.10), channel_id=1, source_target_pairs={{0,4},{4,0},{1,5},{5,1},{2,6},{6,2},{3,7},{7,3},{8,12},{12,8},{9,1... | collective-permute-start | bytes 2359304 | tf_op jit(solution)/shard_map/ppermute | solution.py:267
  54.4 0.9 copy-start.3
  54.4 1.1 copy-start.1
  63.6 45.0 %copy-start.5 = (f32[768]{0:T(1024)S(1)}, f32[768]{0:T(1024)}, u32[]{:S(2)}) copy-start(f32[768]{0:T(1024)} %param.23) | copy-start | bytes 9220
  63.6 45.6 %copy-start.6 = (f32[768]{0:T(1024)S(1)}, f32[768]{0:T(1024)}, u32[]{:S(2)}) copy-start(f32[768]{0:T(1024)} %param.22) | copy-start | bytes 9220
  104.5 11.0 %all-to-all-start.2 = ((bf16[4,48,768]{2,1,0:T(8,128)(2,1)}), bf16[4,48,768]{2,1,0:T(8,128)(2,1)S(1)}, u32[]{:S(2)}, u32[]{:S(2)}) async-start(bf16[4,48,768]{2,1,0:T(8,128)(2,1)} %shard_map.151), calls=%async_computation.2 | async-start | bytes 589824 | tf_op jit(solution)/shard_map/all_to_all | solution.py:275
  115.5 0.7 copy-start.2
  118.3 9.2 %all-to-all-start.3 = ((f32[4,56,128]{2,1,0:T(8,128)}), f32[4,56,128]{2,1,0:T(8,128)S(1)}, u32[]{:S(2)}, u32[]{:S(2)}) async-start(f32[4,56,128]{2,1,0:T(8,128)} %shard_map.152), calls=%async_computation.3 | async-start | bytes 229376 | tf_op jit(solution)/shard_map/all_to_all | solution.py:279
  127.5 0.6 copy-start.4

commit v2 on v1

--- a/solution.py
+++ b/solution.py
@@ -20,19 +20,20 @@
 f32 = jnp.float32
 bf16 = jnp.bfloat16
 VM = pl.BlockSpec(memory_space=pltpu.VMEM)
-SM = pl.BlockSpec(memory_space=pltpu.SMEM)
-
-
-def one_hot(pos_ref, info_ref, rows, cols):
-    local = pos_ref[...] - info_ref[0]
+
+
+def one_hot(pos_ref, count_ref, rows, cols):
+    local = pos_ref[...] - lax.axis_index(SEQ) * rows
     slot = lax.broadcasted_iota(jnp.int32, (1, cols), 1)
-    local = jnp.where(slot < info_ref[1], local, -1)
+    local = jnp.where(slot < count_ref[...], local, -1)
     return lax.broadcasted_iota(jnp.int32, (rows, cols), 0) == local
 
 
-def fill_kernel(info_ref, pos_ref, new_ref, cache_ref, out_ref):
+def fill_kernel(
+    count_ref, step_ref, pos_ref, q_ref, new_ref, cache_ref, out_ref, asked_ref, row_ref
+):
     rows, cols = cache_ref.shape[1], new_ref.shape[1]
-    matched = one_hot(pos_ref, info_ref, rows, cols)
+    matched = one_hot(pos_ref, count_ref, rows, cols)
     pick = matched.astype(f32)
     keep = jnp.max(pick, axis=1, keepdims=True) < 0.5
     pick = pick.astype(bf16)
@@ -40,27 +41,50 @@
         placed = jnp.dot(pick, new_ref[s], preferred_element_type=f32)
         merged = jnp.where(keep, cache_ref[s].astype(f32), placed).astype(bf16)
         out_ref[s] = merged
-
-
-def fill(info, pos, new_kv, cache_kv):
+    for d in range(asked_ref.shape[0]):
+        asked_ref[d] = q_ref[...]
+    row_ref[...] = jnp.broadcast_to(step_ref[...], row_ref.shape)
+
+
+def fill(count, step_size, pos, query, new_kv, cache_kv, copies):
     return pl.pallas_call(
         fill_kernel,
-        out_shape=jax.ShapeDtypeStruct(cache_kv.shape, bf16),
-        in_specs=[SM, VM, VM, VM],
-        out_specs=VM,
-    )(info, pos, new_kv, cache_kv)
-
-
-def attend_kernel(part_ref, q_ref, a_ref, b_ref, t_ref, out_ref, *, chunk):
-    del part_ref
+        out_shape=(
+            jax.ShapeDtypeStruct(cache_kv.shape, bf16),
+            jax.ShapeDtypeStruct((copies,) + query.shape, bf16),
+            jax.ShapeDtypeStruct((8, 128), f32),
+        ),
+        in_specs=[VM] * 6,
+        out_specs=(VM, VM, VM),
+    )(count, step_size, pos, query, new_kv, cache_kv)
+
+
+def touch_kernel(in_ref, out_ref):
+    del in_ref, out_ref
+
+
+def touch(x):
+    any_space = pl.BlockSpec(memory_space=pl.ANY)
+    return pl.pallas_call(
+        touch_kernel,
+        out_shape=jax.ShapeDtypeStruct(x.shape, x.dtype),
+        in_specs=[any_space],
+        out_specs=any_space,
+        input_output_aliases={0: 0},
+    )(x)
+
+
+def attend_kernel(q_ref, a_ref, b_ref, t_ref, out_ref, *, chunk, around):
     slots = out_ref.shape[1] - STAT
     keys, values = [], []
     for ref in (a_ref, b_ref):
         n = ref.shape[0] * ref.shape[2]
         keys.append(ref[:, 0].reshape(n, HD))
         values.append(ref[:, 1].reshape(n, HD))
-    keys.append(t_ref[0])
-    values.append(t_ref[1])
+    share = t_ref.shape[1] // out_ref.shape[0]
+    own_text = pl.ds(pl.multiple_of(lax.axis_index(around) * share, share), share)
+    keys.append(t_ref[0, own_text, :])
+    values.append(t_ref[1, own_text, :])
     lane = lax.broadcasted_iota(jnp.int32, (slots, HD), 1)
     eye = lax.broadcasted_iota(jnp.int32, (slots, HD), 0) == lane
     row = lax.broadcasted_iota(jnp.int32, (STAT, HD), 0)
@@ -93,25 +117,21 @@
             out_ref[d, slots : slots + STAT, :] = pieces.astype(bf16)
 
 
-def attend(part, parts, queries, near, far, text_kv, slots, chunk):
+def attend(parts, around, queries, near, far, text_kv, slots, chunk):
     rows, width = queries.shape
-    text_rows = text_kv.shape[1] // parts
-    kv_spec = pl.BlockSpec(near.shape[:3] + (HD,), lambda h, part: (0, 0, 0, h))
-    return pl.pallas_call(
-        functools.partial(attend_kernel, chunk=chunk),
+    kv_spec = pl.BlockSpec(near.shape[:3] + (HD,), lambda h: (0, 0, 0, h))
+    return pl.pallas_call(
+        functools.partial(attend_kernel, chunk=chunk, around=around),
         out_shape=jax.ShapeDtypeStruct((parts, slots + STAT, width), bf16),
-        grid_spec=pltpu.PrefetchScalarGridSpec(
-            num_scalar_prefetch=1,
-            grid=(width // HD,),
-            in_specs=[
-                pl.BlockSpec((rows, HD), lambda h, part: (0, h)),
-                kv_spec,
-                kv_spec,
-                pl.BlockSpec((2, text_rows, HD), lambda h, part: (0, part[0], h)),
-            ],
-            out_specs=pl.BlockSpec((parts, slots + STAT, HD), lambda h, part: (0, 0, h)),
-        ),
-    )(part, queries, near, far, text_kv)
+        grid=(width // HD,),
+        in_specs=[
+            pl.BlockSpec((rows, HD), lambda h: (0, h)),
+            kv_spec,
+            kv_spec,
+            pl.BlockSpec(text_kv.shape[:2] + (HD,), lambda h: (0, 0, h)),
+        ],
+        out_specs=pl.BlockSpec((parts, slots + STAT, HD), lambda h: (0, 0, h)),
+    )(queries, near, far, text_kv)
 
 
 def merge_kernel(got_ref, w_ref, out_ref):
@@ -148,6 +168,10 @@
     )(got, w_out)
 
 
+def flat(ref):
+    return jnp.concatenate([ref[i : i + 1, :] for i in range(ref.shape[0])], axis=1)
+
+
 def norm_kernel(got_ref, hidden_ref, scale_ref, shift_ref, w_ref, out_ref):
     slots, width = hidden_ref.shape
     summed = hidden_ref[...].astype(f32)
@@ -156,9 +180,9 @@
     mean = jnp.sum(summed, axis=1, keepdims=True) * (1.0 / width)
     centred = summed - mean
     squares = jnp.sum(centred * centred, axis=1, keepdims=True)
-    lifted = 1.0 + scale_ref[...]
+    lifted = 1.0 + flat(scale_ref)
     tail = lax.broadcasted_iota(jnp.int32, (STAT, width), 0)
-    tail = jnp.where(tail == 0, lifted, jnp.where(tail == 1, shift_ref[...], 0.0))
+    tail = jnp.where(tail == 0, lifted, jnp.where(tail == 1, flat(shift_ref), 0.0))
     rows = jnp.concatenate([centred * lifted, tail], axis=0)
     mapped = lax.dot_general(
         rows,
@@ -187,7 +211,7 @@
 
 
 def finish_kernel(
-    info_ref, step_ref, pos_ref, got_ref, latent_ref, old_ref, velocity_ref, next_ref
+    count_ref, step_ref, pos_ref, got_ref, latent_ref, old_ref, velocity_ref, next_ref
 ):
     groups, rows, _ = got_ref.shape
     slots = rows - STAT
@@ -205,7 +229,7 @@
     base = sum(b[slots + 1 : slots + 2, 0:ch] for b in blocks)
     fresh = mapped * lax.rsqrt(var + EPS) + base
     tokens = latent_ref.shape[1]
-    pick = one_hot(pos_ref, info_ref, tokens, slots).astype(f32)
+    pick = one_hot(pos_ref, count_ref, tokens, slots).astype(f32)
     keep = lax.dot_general(
         jnp.ones((8, slots), f32),
         pick,
@@ -221,19 +245,19 @@
     )
     velocity = jnp.where(keep < 0.5, old_ref[...], chosen)
     velocity_ref[...] = velocity
-    next_ref[...] = latent_ref[...] + step_ref[0] * velocity
-
-
-def finish(info, step_size, pos, got, latent, cached_velocity):
+    next_ref[...] = latent_ref[...] + step_ref[0:1, :] * velocity
+
+
+def finish(count, step_size, pos, got, latent, cached_velocity):
     velocity, following = pl.pallas_call(
         finish_kernel,
         out_shape=(
             jax.ShapeDtypeStruct(latent.shape[::-1], f32),
             jax.ShapeDtypeStruct(latent.shape[::-1], f32),
         ),
-        in_specs=[SM, SM, VM, VM, VM, VM],
+        in_specs=[VM] * 6,
         out_specs=(VM, VM),
-    )(info, step_size, pos, got, latent.T, cached_velocity.T)
+    )(count, step_size, pos, got, latent.T, cached_velocity.T)
     return velocity.T, following.T
 
 
@@ -256,28 +280,27 @@
     groups = lax.axis_size("head")
     around = ("zl", "y")
     parts = lax.axis_size(around)
-    own = lax.axis_index(SEQ)
     slots = query.shape[0]
-    tokens = cache_kv.shape[1]
-
-    info = jnp.stack([own * tokens, counts[0]]).astype(jnp.int32)
+
+    count = counts.reshape(1, 1)
     pos = active.reshape(1, slots)
-    filled = fill(info, pos, new_kv, cache_kv)
+    filled, asked, step_row = fill(
+        count, step_size.reshape(1, 1), pos, query, new_kv, cache_kv, parts
+    )
     near = lax.all_gather(filled, "zh", axis=0, tiled=False)
     far = lax.ppermute(near, "core", [(0, 1), (1, 0)])
-    asked = jnp.broadcast_to(query[None], (parts,) + query.shape)
     gathered = lax.all_to_all(asked, around, 0, 0, tiled=True)
+    gathered = touch(gathered)
     gathered = gathered.reshape(parts * slots, -1)
-    part = lax.axis_index(around).reshape(1).astype(jnp.int32)
-    partial = attend(part, parts, gathered, near, far, text_kv, slots, 192)
+    partial = attend(parts, around, gathered, near, far, text_kv, slots, 192)
     returned = lax.all_to_all(partial, around, 0, 0, tiled=True)
     terms = merge(returned, w_out, groups)
     terms = lax.all_to_all(terms, "head", 0, 0, tiled=True)
     stats = norm(
-        terms, hidden, mod_scale.reshape(1, -1), mod_shift.reshape(1, -1), w_final
+        terms, hidden, mod_scale.reshape(-1, 128), mod_shift.reshape(-1, 128), w_final
     )
     stats = lax.all_to_all(stats, "head", 0, 0, tiled=True)
-    return finish(info, step_size, pos, stats, latent, cached_velocity)
+    return finish(count, step_row, pos, stats, latent, cached_velocity)
 
 
 def solution(mesh):

time: 132 us -> 133 us (level)
  blocking collectives: 73 us -> 97.9 us
  waiting for transfers between devices: 13.1 us -> 1.43 us
  starting transfers between devices: 18.3 us -> 10.9 us
  local copies, waits for them, and re-layouts: 5.29 us -> 1.71 us
    all_to_all x0 -> x2, blocking collectives: none -> 21.1 us  [the longest x1 11.3 us: on_device(): terms = lax.all_to_all(terms, 'head', 0, 0, tiled=True)]
    all_to_all x2 -> x0, waiting for transfers between devices: 10.9 us -> none  [the longest x1 5.69 us: on_device(): terms = lax.all_to_all(terms, 'head', 0, 0, tiled=True)]
    all_to_all x2 -> x0, starting transfers between devices: 7.45 us -> none  [the longest x1 4.14 us: on_device(): terms = lax.all_to_all(terms, 'head', 0, 0, tiled=True)]
    all_gather x1, blocking collectives: 35.8 us -> 38.8 us  [on_device(): near = lax.all_gather(filled, 'zh', axis=0, tiled=False)]
    broadcast_in_dim x1 -> x0, local copies, waits for them, and re-layouts: 1.65 us -> none  [on_device(): asked = jnp.broadcast_to(query[None], (parts,) + query.shape)]
    pallas_call x2 -> x3, Pallas kernels: 9.96 us -> 10.2 us  [the longest x1 8.12 us: attend(): pl.pallas_call(functools.partial(attend_kernel, chunk=chunk, around=aroun...]
  transfers between devices with their start and end apart: 4 -> 2, of which waited for: 3 -> 1; matrix products, arithmetic and copies ran while one was open for 1% -> 0% of each run, Pallas kernels for 1% -> 0%
where the time goes in v2:
time: 133 us; the launch traced here: 132 us
  blocking collectives  97.9 us (74%)
  Pallas kernels  18 us (14%)
  starting transfers between devices  10.9 us (8%)
  between operations  1.95 us (1%)
  local copies, waits for them, and re-layouts  1.71 us (1%)
  waiting for transfers between devices  1.43 us (1%)
    all_gather x1, blocking collectives, on_device(): near = lax.all_gather(filled, 'zh', axis=0, tiled=False)  38.8 us
    all_to_all x1, blocking collectives, on_device(): returned = lax.all_to_all(partial, around, 0, 0, tiled=True)  37.9 us
    all_to_all x1, blocking collectives, on_device(): terms = lax.all_to_all(terms, 'head', 0, 0, tiled=True)  11.3 us
    all_to_all x1, blocking collectives, on_device(): stats = lax.all_to_all(stats, 'head', 0, 0, tiled=True)  9.87 us
    all_to_all x1, starting transfers between devices, on_device(): gathered = lax.all_to_all(asked, around, 0, 0, tiled=True)  8.95 us
    pallas_call x1, Pallas kernels, attend(): pl.pallas_call(functools.partial(attend_kernel, chunk=chunk, around=aroun...  8.12 us
    pallas_call x1, Pallas kernels, merge(): pl.pallas_call(merge_kernel, out_shape=jax.ShapeDtypeStruct((groups, got....  3.68 us
  transfers between devices with their start and end apart: 2, of which 1 were waited for; matrix products, arithmetic and copies ran while one was open for 0% of the time, Pallas kernels for 0%

profile of v2, /device:TPU:24, one launch (start us, length us, event | category | flops | bytes accessed | tf_op | source)
XLA Modules:
  0.0 131.8 jit_solution(16877366559383923830)
XLA Ops:
  1.9 2.0 %shard_map.149 = (bf16[2,128,384]{2,1,0:T(8,128)(2,1)}, bf16[16,48,384]{2,1,0:T(8,128)(2,1)}, f32[8,128]{1,0:T(8,128)}) custom-call(s32[1,1]{1,0:T(1,128)} %bitcast.12.count_ref, f32[1,1]{1,0:T(1,128)} %bitcast.14.step_ref, s32[1,48]{1,0:T(1,128)} %bitcast.23, bf16[48,384]{1,0:T(8,128)(2,1)} %q_ref.1, bf16[2,48,384]{2,1,0:T(8,128)(2,1)} %new_ref.1, ...), custom_call_target="tpu_custom_call" | custom-call | tf_op jit(solution)/shard_map/pallas_call | solution.py:50
  4.0 9.0 %all-to-all-start = ((bf16[16,48,384]{2,1,0:T(8,128)(2,1)}), bf16[16,48,384]{2,1,0:T(8,128)(2,1)S(1)}, u32[]{:S(2)}, u32[]{:S(2)}) async-start(bf16[16,48,384]{2,1,0:T(8,128)(2,1)} %get-tuple-element.8), calls=%async_computation | async-start | bytes 1179648 | tf_op jit(solution)/shard_map/all_to_all | solution.py:292
  12.9 38.8 %all-gather = bf16[8,128,384]{2,1,0:T(8,128)(2,1)S(1)} all-gather(bf16[2,128,384]{2,1,0:T(8,128)(2,1)} %get-tuple-element.9), channel_id=2, replica_groups=mesh['zh'=4,'zl'=4,'y'=4,'core'=2,'head'=4] {'zh'}, dimensions={0}, use_global_device_ids=true | all-gather | bytes 983040 | tf_op jit(solution)/shard_map/all_gather | solution.py:290
  51.8 0.0 copy-start.1
  51.8 1.9 %collective-permute-start = (bf16[4,2,128,384]{3,2,1,0:T(8,128)(2,1)S(1)}, bf16[4,2,128,384]{3,2,1,0:T(8,128)(2,1)S(1)}, u32[]{:S(2)}, u32[]{:S(2)}) collective-permute-start(bf16[4,2,128,384]{3,2,1,0:T(8,128)(2,1)S(1)} %bitcast.16), channel_id=1, source_target_pairs={{0,4},{4,0},{1,5},{5,1},{2,6},{6,2},{3,7},{7,3},{8,12},{12,8},{9,1... | collective-permute-start | bytes 2359304 | tf_op jit(solution)/shard_map/ppermute | solution.py:291
  53.7 0.0 all-to-all-done.in_ref
  53.7 0.0 copy-start
  53.7 0.8 copy-done
  54.5 1.4 %collective-permute-done.b_ref = bf16[4,2,128,384]{3,2,1,0:T(8,128)(2,1)S(1)} collective-permute-done((bf16[4,2,128,384]{3,2,1,0:T(8,128)(2,1)S(1)}, bf16[4,2,128,384]{3,2,1,0:T(8,128)(2,1)S(1)}, u32[]{:S(2)}, u32[]{:S(2)}) %collective-permute-start) | collective-permute-done | bytes 786464 | tf_op jit(solution)/shard_map/ppermute | solution.py:291
  55.9 0.0 copy-start.2
  55.9 0.0 copy-done.1
  55.9 0.9 copy-done.2
  56.8 8.1 %shard_map.151 = bf16[16,56,384]{2,1,0:T(8,128)(2,1)} custom-call(bf16[768,384]{1,0:T(8,128)(2,1)} %bitcast.15, bf16[4,2,128,384]{3,2,1,0:T(8,128)(2,1)} %bitcast.17, bf16[4,2,128,384]{3,2,1,0:T(8,128)(2,1)} %copy-done.2, bf16[2,512,384]{2,1,0:T(8,128)(2,1)} %t_ref.1), custom_call_target="tpu_custom_call" | custom-call | tf_op jit(solution)/shard_map/pallas_call | solution.py:123
  65.0 37.9 %all_to_all.20.got_ref = bf16[16,56,384]{2,1,0:T(8,128)(2,1)} all-to-all(bf16[16,56,384]{2,1,0:T(8,128)(2,1)} %shard_map.151), channel_id=1, replica_groups=mesh['zh'=4,'zl'=4,'y'=4,'core'=2,'head'=4] {'zl','y'}, dimensions={0} | all-to-all | bytes 1376256 | tf_op jit(solution)/shard_map/all_to_all | solution.py:296
  102.9 3.7 %shard_map.152 = bf16[4,48,768]{2,1,0:T(8,128)(2,1)} custom-call(bf16[16,56,384]{2,1,0:T(8,128)(2,1)} %all_to_all.20.got_ref, bf16[384,3072]{1,0:T(8,128)(2,1)} %w_ref.1), custom_call_target="tpu_custom_call" | custom-call | tf_op jit(solution)/shard_map/pallas_call | solution.py:161
  106.5 11.3 %all_to_all.21.got_ref = bf16[4,48,768]{2,1,0:T(8,128)(2,1)} all-to-all(bf16[4,48,768]{2,1,0:T(8,128)(2,1)} %shard_map.152), channel_id=1, replica_groups=mesh['zh'=4,'zl'=4,'y'=4,'core'=2,'head'=4] {'head'}, dimensions={0} | all-to-all | bytes 589824 | tf_op jit(solution)/shard_map/all_to_all | solution.py:298
  117.8 2.1 %shard_map.153 = f32[4,56,128]{2,1,0:T(8,128)} custom-call(bf16[4,48,768]{2,1,0:T(8,128)(2,1)} %all_to_all.21.got_ref, bf16[48,768]{1,0:T(8,128)(2,1)} %hidden_ref.1, f32[6,128]{1,0:T(8,128)} %bitcast.21, f32[6,128]{1,0:T(8,128)} %bitcast.22, f32[64,768]{1,0:T(8,128)} %bitcast.18), custom_call_target="tpu_custom_call" | custom-call | tf_op jit(solution)/shard_map/pallas_call | solution.py:203
  119.9 9.9 %all_to_all.22.got_ref = f32[4,56,128]{2,1,0:T(8,128)} all-to-all(f32[4,56,128]{2,1,0:T(8,128)} %shard_map.153), channel_id=1, replica_groups=mesh['zh'=4,'zl'=4,'y'=4,'core'=2,'head'=4] {'head'}, dimensions={0} | all-to-all | bytes 229376 | tf_op jit(solution)/shard_map/all_to_all | solution.py:302
  129.8 2.0 %shard_map.154 = (f32[64,128]{1,0:T(8,128)}, f32[64,128]{1,0:T(8,128)}) custom-call(s32[1,1]{1,0:T(1,128)} %bitcast.13.count_ref, f32[8,128]{1,0:T(8,128)} %get-tuple-element.7.step_ref, s32[1,48]{1,0:T(1,128)} %bitcast.24, f32[4,56,128]{2,1,0:T(8,128)} %all_to_all.22.got_ref, f32[64,128]{1,0:T(8,128)} %bitcast.19, f32[64,128]{1,0:T(8,128)} %bitcast.20), custom_call_target="tpu_custom_call" | custom-call | tf_op jit(solution)/shard_map/pallas_call | solution.py:252
  (1 shorter events, 0.0 us)
Async XLA Ops:
  4.0 49.7 %all-to-all-start = ((bf16[16,48,384]{2,1,0:T(8,128)(2,1)}), bf16[16,48,384]{2,1,0:T(8,128)(2,1)S(1)}, u32[]{:S(2)}, u32[]{:S(2)}) async-start(bf16[16,48,384]{2,1,0:T(8,128)(2,1)} %get-tuple-element.8), calls=%async_computation | async-start | bytes 1179648 | tf_op jit(solution)/shard_map/all_to_all | solution.py:292
  51.8 4.2 %copy-start.1 = (bf16[8,128,384]{2,1,0:T(8,128)(2,1)}, bf16[8,128,384]{2,1,0:T(8,128)(2,1)S(1)}, u32[]{:S(2)}) copy-start(bf16[8,128,384]{2,1,0:T(8,128)(2,1)S(1)} %all-gather) | copy-start | bytes 2359300
  51.8 4.2 %collective-permute-start = (bf16[4,2,128,384]{3,2,1,0:T(8,128)(2,1)S(1)}, bf16[4,2,128,384]{3,2,1,0:T(8,128)(2,1)S(1)}, u32[]{:S(2)}, u32[]{:S(2)}) collective-permute-start(bf16[4,2,128,384]{3,2,1,0:T(8,128)(2,1)S(1)} %bitcast.16), channel_id=1, source_target_pairs={{0,4},{4,0},{1,5},{5,1},{2,6},{6,2},{3,7},{7,3},{8,12},{12,8},{9,1... | collective-permute-start | bytes 2359304 | tf_op jit(solution)/shard_map/ppermute | solution.py:291
  53.7 0.8 copy-start
  55.9 0.9 copy-start.2

commit v3 on v2

--- a/solution.py
+++ b/solution.py
@@ -20,6 +20,14 @@
 f32 = jnp.float32
 bf16 = jnp.bfloat16
 VM = pl.BlockSpec(memory_space=pltpu.VMEM)
+
+
+def grant(mebibytes):
+    return pltpu.CompilerParams(vmem_limit_bytes=mebibytes * 2**20)
+
+
+def local(*arrays):
+    return [pltpu.with_memory_space_constraint(x, pltpu.VMEM) for x in arrays]
 
 
 def one_hot(pos_ref, count_ref, rows, cols):
@@ -50,12 +58,13 @@
     return pl.pallas_call(
         fill_kernel,
         out_shape=(
-            jax.ShapeDtypeStruct(cache_kv.shape, bf16),
-            jax.ShapeDtypeStruct((copies,) + query.shape, bf16),
-            jax.ShapeDtypeStruct((8, 128), f32),
+            pltpu.VMEM(cache_kv.shape, bf16),
+            pltpu.VMEM((copies,) + query.shape, bf16),
+            pltpu.VMEM((8, 128), f32),
         ),
         in_specs=[VM] * 6,
         out_specs=(VM, VM, VM),
+        compiler_params=grant(8),
     )(count, step_size, pos, query, new_kv, cache_kv)
 
 
@@ -64,74 +73,73 @@
 
 
 def touch(x):
-    any_space = pl.BlockSpec(memory_space=pl.ANY)
     return pl.pallas_call(
         touch_kernel,
-        out_shape=jax.ShapeDtypeStruct(x.shape, x.dtype),
-        in_specs=[any_space],
-        out_specs=any_space,
+        out_shape=pltpu.VMEM(x.shape, x.dtype),
+        in_specs=[VM],
+        out_specs=VM,
         input_output_aliases={0: 0},
-    )(x)
+        compiler_params=grant(2),
+    )(*local(x))
 
 
 def attend_kernel(q_ref, a_ref, b_ref, t_ref, out_ref, *, chunk, around):
     slots = out_ref.shape[1] - STAT
-    keys, values = [], []
-    for ref in (a_ref, b_ref):
-        n = ref.shape[0] * ref.shape[2]
-        keys.append(ref[:, 0].reshape(n, HD))
-        values.append(ref[:, 1].reshape(n, HD))
     share = t_ref.shape[1] // out_ref.shape[0]
     own_text = pl.ds(pl.multiple_of(lax.axis_index(around) * share, share), share)
-    keys.append(t_ref[0, own_text, :])
-    values.append(t_ref[1, own_text, :])
     lane = lax.broadcasted_iota(jnp.int32, (slots, HD), 1)
     eye = lax.broadcasted_iota(jnp.int32, (slots, HD), 0) == lane
     row = lax.broadcasted_iota(jnp.int32, (STAT, HD), 0)
-    for start in range(0, q_ref.shape[0], chunk):
-        q = q_ref[pl.ds(start, chunk), :]
-        scores = [
-            lax.dot_general(q, k, (((1,), (1,)), ((), ())), preferred_element_type=f32)
-            for k in keys
-        ]
-        top = functools.reduce(
-            jnp.maximum, [jnp.max(s, axis=1, keepdims=True) for s in scores]
-        )
-        weights = [jnp.exp2((s - top) * (SCALE * LOG2E)) for s in scores]
-        total = sum(jnp.sum(w, axis=1, keepdims=True) for w in weights)
-        mixed = sum(
-            jnp.dot(w.astype(bf16), v, preferred_element_type=f32)
-            for w, v in zip(weights, values)
-        )
-        mixed = mixed / total
-        spread = top * SCALE + jnp.log(total)
-        for i in range(chunk // slots):
-            d = start // slots + i
-            out_ref[d, 0:slots, :] = mixed[i * slots : (i + 1) * slots].astype(bf16)
-            column = spread[i * slots : (i + 1) * slots]
-            line = jnp.sum(jnp.where(eye, column, 0.0), axis=0, keepdims=True)
-            first = line.astype(bf16).astype(f32)
-            second = (line - first).astype(bf16).astype(f32)
-            third = line - first - second
-            pieces = jnp.where(row == 0, first, jnp.where(row == 1, second, third))
-            out_ref[d, slots : slots + STAT, :] = pieces.astype(bf16)
+    for h in range(q_ref.shape[1] // HD):
+        cols = slice(h * HD, (h + 1) * HD)
+        keys, values = [], []
+        for ref in (a_ref, b_ref):
+            n = ref.shape[0] * ref.shape[2]
+            keys.append(ref[:, 0, :, cols].reshape(n, HD))
+            values.append(ref[:, 1, :, cols].reshape(n, HD))
+        keys.append(t_ref[0, own_text, cols])
+        values.append(t_ref[1, own_text, cols])
+        for start in range(0, q_ref.shape[0], chunk):
+            q = q_ref[pl.ds(start, chunk), cols]
+            scores = [
+                lax.dot_general(
+                    q, k, (((1,), (1,)), ((), ())), preferred_element_type=f32
+                )
+                for k in keys
+            ]
+            top = functools.reduce(
+                jnp.maximum, [jnp.max(s, axis=1, keepdims=True) for s in scores]
+            )
+            weights = [jnp.exp2((s - top) * (SCALE * LOG2E)) for s in scores]
+            total = sum(jnp.sum(w, axis=1, keepdims=True) for w in weights)
+            mixed = sum(
+                jnp.dot(w.astype(bf16), v, preferred_element_type=f32)
+                for w, v in zip(weights, values)
+            )
+            mixed = mixed / total
+            spread = top * SCALE + jnp.log(total)
+            for i in range(chunk // slots):
+                d = start // slots + i
+                part = slice(i * slots, (i + 1) * slots)
+                out_ref[d, 0:slots, cols] = mixed[part].astype(bf16)
+                line = jnp.sum(
+                    jnp.where(eye, spread[part], 0.0), axis=0, keepdims=True
+                )
+                first = line.astype(bf16).astype(f32)
+                second = (line - first).astype(bf16).astype(f32)
+                third = line - first - second
+                pieces = jnp.where(row == 0, first, jnp.where(row == 1, second, third))
+                out_ref[d, slots : slots + STAT, cols] = pieces.astype(bf16)
 
 
 def attend(parts, around, queries, near, far, text_kv, slots, chunk):
-    rows, width = queries.shape
-    kv_spec = pl.BlockSpec(near.shape[:3] + (HD,), lambda h: (0, 0, 0, h))
     return pl.pallas_call(
         functools.partial(attend_kernel, chunk=chunk, around=around),
-        out_shape=jax.ShapeDtypeStruct((parts, slots + STAT, width), bf16),
-        grid=(width // HD,),
-        in_specs=[
-            pl.BlockSpec((rows, HD), lambda h: (0, h)),
-            kv_spec,
-            kv_spec,
-            pl.BlockSpec(text_kv.shape[:2] + (HD,), lambda h: (0, 0, h)),
-        ],
-        out_specs=pl.BlockSpec((parts, slots + STAT, HD), lambda h: (0, 0, h)),
-    )(queries, near, far, text_kv)
+        out_shape=pltpu.VMEM((parts, slots + STAT, queries.shape[1]), bf16),
+        in_specs=[VM] * 4,
+        out_specs=VM,
+        compiler_params=grant(20),
+    )(*local(queries, near, far, text_kv))
 
 
 def merge_kernel(got_ref, w_ref, out_ref):
@@ -160,12 +168,13 @@
 def merge(got, w_out, groups):
     return pl.pallas_call(
         merge_kernel,
-        out_shape=jax.ShapeDtypeStruct(
+        out_shape=pltpu.VMEM(
             (groups, got.shape[1] - STAT, w_out.shape[1] // groups), bf16
         ),
         in_specs=[VM, VM],
         out_specs=VM,
-    )(got, w_out)
+        compiler_params=grant(8),
+    )(*local(got, w_out))
 
 
 def flat(ref):
@@ -202,12 +211,13 @@
 def norm(got, hidden, scale, shift, w_final):
     return pl.pallas_call(
         norm_kernel,
-        out_shape=jax.ShapeDtypeStruct(
+        out_shape=pltpu.VMEM(
             (got.shape[0], hidden.shape[0] + STAT, 2 * w_final.shape[1]), f32
         ),
         in_specs=[VM] * 5,
         out_specs=VM,
-    )(got, hidden, scale, shift, w_final.T)
+        compiler_params=grant(8),
+    )(*local(got, hidden, scale, shift, w_final.T))
 
 
 def finish_kernel(
@@ -257,7 +267,8 @@
         ),
         in_specs=[VM] * 6,
         out_specs=(VM, VM),
-    )(count, step_size, pos, got, latent.T, cached_velocity.T)
+        compiler_params=grant(8),
+    )(count, *local(step_size), pos, *local(got, latent.T, cached_velocity.T))
     return velocity.T, following.T
 
 

time: 133 us -> 125 us (0.940)
  Pallas kernels: 18 us -> 9.34 us
  blocking collectives: 97.9 us -> 96.1 us
  local copies, waits for them, and re-layouts: 1.71 us -> 3.27 us
    pallas_call x4, Pallas kernels: 7.84 us -> 2.45 us  [the longest x1 1.08 us: merge(): pl.pallas_call(merge_kernel, out_shape=pltpu.VMEM((groups, got.shape[1] -...]
    pallas_call x1, Pallas kernels: 8.12 us -> 5.8 us  [attend(): pl.pallas_call(functools.partial(attend_kernel, chunk=chunk, around=aroun...]
    all_to_all x1, blocking collectives: 9.87 us -> 8.27 us  [on_device(): stats = lax.all_to_all(stats, 'head', 0, 0, tiled=True)]
    unnamed x6 -> x26, local copies, waits for them, and re-layouts: 1.71 us -> 3.27 us
where the time goes in v3:
time: 125 us; the launch traced here: 124 us
  blocking collectives  96.1 us (77%)
  starting transfers between devices  10.9 us (9%)
  Pallas kernels  9.34 us (7%)
  local copies, waits for them, and re-layouts  3.27 us (3%)
  waiting for transfers between devices  2.23 us (2%)
  between operations  2.12 us (2%)
    all_gather x1, blocking collectives, on_device(): near = lax.all_gather(filled, 'zh', axis=0, tiled=False)  38.5 us
    all_to_all x1, blocking collectives, on_device(): returned = lax.all_to_all(partial, around, 0, 0, tiled=True)  38.4 us
    all_to_all x1, blocking collectives, on_device(): terms = lax.all_to_all(terms, 'head', 0, 0, tiled=True)  10.9 us
    all_to_all x1, starting transfers between devices, on_device(): gathered = lax.all_to_all(asked, around, 0, 0, tiled=True)  8.95 us
    all_to_all x1, blocking collectives, on_device(): stats = lax.all_to_all(stats, 'head', 0, 0, tiled=True)  8.27 us
    pallas_call x1, Pallas kernels, attend(): pl.pallas_call(functools.partial(attend_kernel, chunk=chunk, around=aroun...  5.8 us
    unnamed x26, local copies, waits for them, and re-layouts  3.27 us
  transfers between devices with their start and end apart: 2, of which 1 were waited for; matrix products, arithmetic and copies ran while one was open for 0% of the time, Pallas kernels for 0%

profile of v3, /device:TPU:24, one launch (start us, length us, event | category | flops | bytes accessed | tf_op | source)
XLA Modules:
  0.0 123.9 jit_solution(3026965241445205870)
XLA Ops:
  0.6 0.0 copy-start.1
  2.0 0.0 copy-start.2
  2.0 0.9 copy-done.2
  2.9 0.0 copy-start.4
  2.9 0.9 copy-done.4
  3.8 0.0 copy-start.6
  3.8 0.8 copy-done.6
  4.6 0.0 copy-start.11
  4.6 0.7 copy-done.11
  5.2 1.0 shard_map.149
  6.2 9.0 %all-to-all-start = ((bf16[16,48,384]{2,1,0:T(8,128)(2,1)}), bf16[16,48,384]{2,1,0:T(8,128)(2,1)S(1)}, u32[]{:S(2)}, u32[]{:S(2)}) async-start(bf16[16,48,384]{2,1,0:T(8,128)(2,1)} %get-tuple-element.8), calls=%async_computation | async-start | bytes 1179648 | tf_op jit(solution)/shard_map/all_to_all | solution.py:303
  15.2 38.5 %all-gather = bf16[8,128,384]{2,1,0:T(8,128)(2,1)S(1)} all-gather(bf16[2,128,384]{2,1,0:T(8,128)(2,1)S(1)} %get-tuple-element.9), channel_id=2, replica_groups=mesh['zh'=4,'zl'=4,'y'=4,'core'=2,'head'=4] {'zh'}, dimensions={0}, use_global_device_ids=true | all-gather | bytes 983040 | tf_op jit(solution)/shard_map/all_gather | solution.py:301
  53.7 1.9 %collective-permute-start = (bf16[4,2,128,384]{3,2,1,0:T(8,128)(2,1)S(1)}, bf16[4,2,128,384]{3,2,1,0:T(8,128)(2,1)S(1)}, u32[]{:S(2)}, u32[]{:S(2)}) collective-permute-start(bf16[4,2,128,384]{3,2,1,0:T(8,128)(2,1)S(1)} %bitcast.16), channel_id=1, source_target_pairs={{0,4},{4,0},{1,5},{5,1},{2,6},{6,2},{3,7},{7,3},{8,12},{12,8},{9,1... | collective-permute-start | bytes 2359304 | tf_op jit(solution)/shard_map/ppermute | solution.py:302
  55.6 0.0 all-to-all-done.in_ref
  55.6 2.2 %collective-permute-done.b_ref = bf16[4,2,128,384]{3,2,1,0:T(8,128)(2,1)S(1)} collective-permute-done((bf16[4,2,128,384]{3,2,1,0:T(8,128)(2,1)S(1)}, bf16[4,2,128,384]{3,2,1,0:T(8,128)(2,1)S(1)}, u32[]{:S(2)}, u32[]{:S(2)}) %collective-permute-start) | collective-permute-done | bytes 786464 | tf_op jit(solution)/shard_map/ppermute | solution.py:302
  57.8 0.0 copy-done.1
  57.9 0.0 copy-start
  57.9 5.8 %shard_map.151 = bf16[16,56,384]{2,1,0:T(8,128)(2,1)S(1)} custom-call(bf16[768,384]{1,0:T(8,128)(2,1)S(1)} %bitcast.15, bf16[4,2,128,384]{3,2,1,0:T(8,128)(2,1)S(1)} %bitcast.17, bf16[4,2,128,384]{3,2,1,0:T(8,128)(2,1)S(1)} %collective-permute-done.b_ref, bf16[2,512,384]{2,1,0:T(8,128)(2,1)S(1)} %copy-done.1), custom_call_target="tpu_custom_call" | custom-call | tf_op jit(solution)/shard_map/pallas_call | solution.py:136
  63.7 0.0 copy-start.3
  63.7 0.0 copy-start.5
  63.7 0.0 copy-start.9
  63.7 0.0 copy-start.10
  63.7 38.4 %all_to_all.20.got_ref = bf16[16,56,384]{2,1,0:T(8,128)(2,1)S(1)} all-to-all(bf16[16,56,384]{2,1,0:T(8,128)(2,1)S(1)} %shard_map.151), channel_id=1, replica_groups=mesh['zh'=4,'zl'=4,'y'=4,'core'=2,'head'=4] {'zl','y'}, dimensions={0} | all-to-all | bytes 1376256 | tf_op jit(solution)/shard_map/all_to_all | solution.py:307
  102.1 0.0 copy-done
  102.1 0.0 copy-start.7
  102.1 0.0 copy-start.8
  102.1 0.0 copy-start.12
  102.1 1.1 shard_map.152
  103.2 10.9 %all_to_all.21.got_ref = bf16[4,48,768]{2,1,0:T(8,128)(2,1)S(1)} all-to-all(bf16[4,48,768]{2,1,0:T(8,128)(2,1)S(1)} %shard_map.152), channel_id=1, replica_groups=mesh['zh'=4,'zl'=4,'y'=4,'core'=2,'head'=4] {'head'}, dimensions={0} | all-to-all | bytes 589824 | tf_op jit(solution)/shard_map/all_to_all | solution.py:309
  114.2 0.0 copy-done.3
  114.2 0.0 copy-done.5
  114.2 0.0 copy-done.9
  114.2 0.0 copy-done.10
  114.2 0.4 shard_map.153
  114.6 8.3 %all_to_all.22.got_ref = f32[4,56,128]{2,1,0:T(8,128)S(1)} all-to-all(f32[4,56,128]{2,1,0:T(8,128)S(1)} %shard_map.153), channel_id=1, replica_groups=mesh['zh'=4,'zl'=4,'y'=4,'core'=2,'head'=4] {'head'}, dimensions={0} | all-to-all | bytes 229376 | tf_op jit(solution)/shard_map/all_to_all | solution.py:313
  122.9 0.0 copy-done.7
  122.9 0.0 copy-done.8
  122.9 0.0 copy-done.12
  122.9 1.1 shard_map.154
  (1 shorter events, 0.0 us)
Async XLA Ops:
  0.6 57.2 %copy-start.1 = (bf16[2,512,384]{2,1,0:T(8,128)(2,1)S(1)}, bf16[2,512,384]{2,1,0:T(8,128)(2,1)}, u32[]{:S(2)}) copy-start(bf16[2,512,384]{2,1,0:T(8,128)(2,1)} %t_ref.1) | copy-start | bytes 2359300
  2.0 0.9 copy-start.2
  2.9 0.9 copy-start.4
  3.8 0.8 copy-start.6
  4.6 0.7 copy-start.11
  6.2 49.4 %all-to-all-start = ((bf16[16,48,384]{2,1,0:T(8,128)(2,1)}), bf16[16,48,384]{2,1,0:T(8,128)(2,1)S(1)}, u32[]{:S(2)}, u32[]{:S(2)}) async-start(bf16[16,48,384]{2,1,0:T(8,128)(2,1)} %get-tuple-element.8), calls=%async_computation | async-start | bytes 1179648 | tf_op jit(solution)/shard_map/all_to_all | solution.py:303
  53.7 4.2 %collective-permute-start = (bf16[4,2,128,384]{3,2,1,0:T(8,128)(2,1)S(1)}, bf16[4,2,128,384]{3,2,1,0:T(8,128)(2,1)S(1)}, u32[]{:S(2)}, u32[]{:S(2)}) collective-permute-start(bf16[4,2,128,384]{3,2,1,0:T(8,128)(2,1)S(1)} %bitcast.16), channel_id=1, source_target_pairs={{0,4},{4,0},{1,5},{5,1},{2,6},{6,2},{3,7},{7,3},{8,12},{12,8},{9,1... | collective-permute-start | bytes 2359304 | tf_op jit(solution)/shard_map/ppermute | solution.py:302
  57.9 44.3 %copy-start = (bf16[384,3072]{1,0:T(8,128)(2,1)S(1)}, bf16[384,3072]{1,0:T(8,128)(2,1)}, u32[]{:S(2)}) copy-start(bf16[384,3072]{1,0:T(8,128)(2,1)} %w_ref.1) | copy-start | bytes 7077892
  63.7 50.5 %copy-start.3 = (f32[768,64]{0,1:T(8,128)S(1)}, f32[768,64]{0,1:T(8,128)}, u32[]{:S(2)}) copy-start(f32[768,64]{0,1:T(8,128)} %param.24) | copy-start | bytes 589828
  63.7 50.5 %copy-start.5 = (bf16[48,768]{1,0:T(8,128)(2,1)S(1)}, bf16[48,768]{1,0:T(8,128)(2,1)}, u32[]{:S(2)}) copy-start(bf16[48,768]{1,0:T(8,128)(2,1)} %hidden_ref.1) | copy-start | bytes 221188
  63.7 50.5 %copy-start.9 = (f32[768]{0:T(1024)S(1)}, f32[768]{0:T(1024)}, u32[]{:S(2)}) copy-start(f32[768]{0:T(1024)} %param.23) | copy-start | bytes 9220
  63.7 50.5 %copy-start.10 = (f32[768]{0:T(1024)S(1)}, f32[768]{0:T(1024)}, u32[]{:S(2)}) copy-start(f32[768]{0:T(1024)} %param.22) | copy-start | bytes 9220
  102.1 20.7 %copy-start.7 = (f32[128,64]{0,1:T(8,128)S(1)}, f32[128,64]{0,1:T(8,128)}, u32[]{:S(2)}) copy-start(f32[128,64]{0,1:T(8,128)} %param.25) | copy-start | bytes 98308
  102.1 20.7 %copy-start.8 = (f32[128,64]{0,1:T(8,128)S(1)}, f32[128,64]{0,1:T(8,128)}, u32[]{:S(2)}) copy-start(f32[128,64]{0,1:T(8,128)} %param.26) | copy-start | bytes 98308
  102.1 20.7 %copy-start.12 = (s32[48]{0:T(128)S(1)}, s32[48]{0:T(128)}, u32[]{:S(2)}) copy-start(s32[48]{0:T(128)} %param.18) | copy-start | bytes 580

commit v4 on v3

--- a/solution.py
+++ b/solution.py
@@ -13,7 +13,7 @@
 EPS = 1e-06
 LOG2E = 1.4426950408889634
 SCALE = HD ** (-0.5)
-SEQ = ("zh", "zl", "y", "core")
+SEQ = ("zb", "za", "y", "core")
 STAT = 8
 
 
@@ -28,6 +28,10 @@
 
 def local(*arrays):
     return [pltpu.with_memory_space_constraint(x, pltpu.VMEM) for x in arrays]
+
+
+def remote(*arrays):
+    return [pltpu.with_memory_space_constraint(x, pltpu.HBM) for x in arrays]
 
 
 def one_hot(pos_ref, count_ref, rows, cols):
@@ -37,9 +41,7 @@
     return lax.broadcasted_iota(jnp.int32, (rows, cols), 0) == local
 
 
-def fill_kernel(
-    count_ref, step_ref, pos_ref, q_ref, new_ref, cache_ref, out_ref, asked_ref, row_ref
-):
+def fill_kernel(count_ref, step_ref, pos_ref, new_ref, cache_ref, out_ref, row_ref):
     rows, cols = cache_ref.shape[1], new_ref.shape[1]
     matched = one_hot(pos_ref, count_ref, rows, cols)
     pick = matched.astype(f32)
@@ -49,54 +51,57 @@
         placed = jnp.dot(pick, new_ref[s], preferred_element_type=f32)
         merged = jnp.where(keep, cache_ref[s].astype(f32), placed).astype(bf16)
         out_ref[s] = merged
-    for d in range(asked_ref.shape[0]):
-        asked_ref[d] = q_ref[...]
     row_ref[...] = jnp.broadcast_to(step_ref[...], row_ref.shape)
 
 
-def fill(count, step_size, pos, query, new_kv, cache_kv, copies):
+def fill(count, step_size, pos, new_kv, cache_kv):
     return pl.pallas_call(
         fill_kernel,
         out_shape=(
             pltpu.VMEM(cache_kv.shape, bf16),
-            pltpu.VMEM((copies,) + query.shape, bf16),
             pltpu.VMEM((8, 128), f32),
         ),
-        in_specs=[VM] * 6,
-        out_specs=(VM, VM, VM),
-        compiler_params=grant(8),
-    )(count, step_size, pos, query, new_kv, cache_kv)
-
-
-def touch_kernel(in_ref, out_ref):
-    del in_ref, out_ref
-
-
-def touch(x):
-    return pl.pallas_call(
-        touch_kernel,
-        out_shape=pltpu.VMEM(x.shape, x.dtype),
-        in_specs=[VM],
+        in_specs=[VM] * 5,
+        out_specs=(VM, VM),
+        compiler_params=grant(8),
+    )(count, step_size, *remote(pos, new_kv, cache_kv))
+
+
+def spread_kernel(own_ref, other_ref, out_ref):
+    for d in range(out_ref.shape[0]):
+        out_ref[d, 0] = own_ref[...]
+        out_ref[d, 1] = other_ref[...]
+
+
+def spread(own, other, copies):
+    return pl.pallas_call(
+        spread_kernel,
+        out_shape=pltpu.VMEM((copies, 2) + own.shape, bf16),
+        in_specs=[VM] * 2,
         out_specs=VM,
-        input_output_aliases={0: 0},
-        compiler_params=grant(2),
-    )(*local(x))
+        compiler_params=grant(8),
+    )(*local(own, other))
 
 
 def attend_kernel(q_ref, a_ref, b_ref, t_ref, out_ref, *, chunk, around):
-    slots = out_ref.shape[1] - STAT
-    share = t_ref.shape[1] // out_ref.shape[0]
+    parts = out_ref.shape[0]
+    slots = q_ref.shape[0] // parts
+    heads = q_ref.shape[1] // HD
+    share = t_ref.shape[1] // parts
     own_text = pl.ds(pl.multiple_of(lax.axis_index(around) * share, share), share)
     lane = lax.broadcasted_iota(jnp.int32, (slots, HD), 1)
-    eye = lax.broadcasted_iota(jnp.int32, (slots, HD), 0) == lane
+    slot = lax.broadcasted_iota(jnp.int32, (slots, HD), 0)
     row = lax.broadcasted_iota(jnp.int32, (STAT, HD), 0)
-    for h in range(q_ref.shape[1] // HD):
+    stats = [jnp.zeros((STAT, HD), f32)] * parts
+    for h in range(heads):
         cols = slice(h * HD, (h + 1) * HD)
+        eye = lane == slot + slots * (h % 2)
+        base = 3 * (h // 2)
         keys, values = [], []
         for ref in (a_ref, b_ref):
-            n = ref.shape[0] * ref.shape[2]
-            keys.append(ref[:, 0, :, cols].reshape(n, HD))
-            values.append(ref[:, 1, :, cols].reshape(n, HD))
+            n = ref.shape[0] * ref.shape[1] * ref.shape[3]
+            keys.append(ref[:, :, 0, :, cols].reshape(n, HD))
+            values.append(ref[:, :, 1, :, cols].reshape(n, HD))
         keys.append(t_ref[0, own_text, cols])
         values.append(t_ref[1, own_text, cols])
         for start in range(0, q_ref.shape[0], chunk):
@@ -117,25 +122,28 @@
                 for w, v in zip(weights, values)
             )
             mixed = mixed / total
-            spread = top * SCALE + jnp.log(total)
+            level = top * SCALE + jnp.log(total)
             for i in range(chunk // slots):
                 d = start // slots + i
                 part = slice(i * slots, (i + 1) * slots)
-                out_ref[d, 0:slots, cols] = mixed[part].astype(bf16)
+                out_ref[d, h * slots : (h + 1) * slots, :] = mixed[part].astype(bf16)
                 line = jnp.sum(
-                    jnp.where(eye, spread[part], 0.0), axis=0, keepdims=True
+                    jnp.where(eye, level[part], 0.0), axis=0, keepdims=True
                 )
                 first = line.astype(bf16).astype(f32)
                 second = (line - first).astype(bf16).astype(f32)
                 third = line - first - second
-                pieces = jnp.where(row == 0, first, jnp.where(row == 1, second, third))
-                out_ref[d, slots : slots + STAT, cols] = pieces.astype(bf16)
+                for p, piece in enumerate((first, second, third)):
+                    stats[d] = jnp.where(row == base + p, stats[d] + piece, stats[d])
+    for d in range(parts):
+        out_ref[d, heads * slots : heads * slots + STAT, :] = stats[d].astype(bf16)
 
 
 def attend(parts, around, queries, near, far, text_kv, slots, chunk):
+    heads = queries.shape[1] // HD
     return pl.pallas_call(
         functools.partial(attend_kernel, chunk=chunk, around=around),
-        out_shape=pltpu.VMEM((parts, slots + STAT, queries.shape[1]), bf16),
+        out_shape=pltpu.VMEM((parts, heads * slots + STAT, HD), bf16),
         in_specs=[VM] * 4,
         out_specs=VM,
         compiler_params=grant(20),
@@ -143,19 +151,24 @@
 
 
 def merge_kernel(got_ref, w_ref, out_ref):
-    parts, rows, width = got_ref.shape
-    slots = rows - STAT
+    parts, rows, _ = got_ref.shape
+    count = w_ref.shape[0] // HD
+    slots = (rows - STAT) // count
+    stat = got_ref[:, rows - STAT : rows, :].astype(f32)
+    shares = []
+    for base in range(0, 3 * ((count + 1) // 2), 3):
+        level = stat[:, base] + stat[:, base + 1] + stat[:, base + 2]
+        share = jnp.exp(level - jnp.max(level, axis=0, keepdims=True))
+        share = share / jnp.sum(share, axis=0, keepdims=True)
+        pad = jnp.zeros((HD - parts, HD), f32)
+        shares.append(jnp.concatenate([share, pad], axis=0).T)
     heads = []
-    for h in range(width // HD):
-        cols = slice(h * HD, (h + 1) * HD)
-        stat = got_ref[:, slots:rows, cols].astype(f32)
-        spread = stat[:, 0] + stat[:, 1] + stat[:, 2]
-        share = jnp.exp(spread - jnp.max(spread, axis=0, keepdims=True))
-        share = share / jnp.sum(share, axis=0, keepdims=True)
-        share = jnp.concatenate([share, jnp.zeros((HD - parts, HD), f32)], axis=0).T
+    for h in range(count):
+        share = shares[h // 2][slots * (h % 2) : slots * (h % 2 + 1)]
         total = jnp.zeros((slots, HD), f32)
         for s in range(parts):
-            total += got_ref[s, 0:slots, cols].astype(f32) * share[0:slots, s : s + 1]
+            block = got_ref[s, h * slots : (h + 1) * slots, :].astype(f32)
+            total += block * share[:, s : s + 1]
         heads.append(total.astype(bf16))
     attended = jnp.concatenate(heads, axis=1)
     piece = out_ref.shape[2]
@@ -166,10 +179,11 @@
 
 
 def merge(got, w_out, groups):
+    slots = (got.shape[1] - STAT) // (w_out.shape[0] // HD)
     return pl.pallas_call(
         merge_kernel,
         out_shape=pltpu.VMEM(
-            (groups, got.shape[1] - STAT, w_out.shape[1] // groups), bf16
+            (groups, slots, w_out.shape[1] // groups), bf16
         ),
         in_specs=[VM, VM],
         out_specs=VM,
@@ -289,22 +303,19 @@
     step_size,
 ):
     groups = lax.axis_size("head")
-    around = ("zl", "y")
-    parts = lax.axis_size(around)
+    parts = lax.axis_size("zb")
     slots = query.shape[0]
+    trade = [(0, 1), (1, 0)]
 
     count = counts.reshape(1, 1)
     pos = active.reshape(1, slots)
-    filled, asked, step_row = fill(
-        count, step_size.reshape(1, 1), pos, query, new_kv, cache_kv, parts
-    )
-    near = lax.all_gather(filled, "zh", axis=0, tiled=False)
-    far = lax.ppermute(near, "core", [(0, 1), (1, 0)])
-    gathered = lax.all_to_all(asked, around, 0, 0, tiled=True)
-    gathered = touch(gathered)
-    gathered = gathered.reshape(parts * slots, -1)
-    partial = attend(parts, around, gathered, near, far, text_kv, slots, 192)
-    returned = lax.all_to_all(partial, around, 0, 0, tiled=True)
+    filled, step_row = fill(count, step_size.reshape(1, 1), pos, new_kv, cache_kv)
+    pair = spread(filled, lax.ppermute(filled, "za", trade), lax.axis_size("y"))
+    near = lax.all_to_all(pair, "y", 0, 0, tiled=True)
+    gathered = lax.all_gather(query, "zb", axis=0, tiled=True)
+    far = lax.ppermute(near, "core", trade)
+    partial = attend(parts, "zb", gathered, near, far, text_kv, slots, 192)
+    returned = lax.all_to_all(partial, "zb", 0, 0, tiled=True)
     terms = merge(returned, w_out, groups)
     terms = lax.all_to_all(terms, "head", 0, 0, tiled=True)
     stats = norm(
@@ -333,7 +344,7 @@
     )
     out_specs = (P(SEQ, None), P(SEQ, None))
     split = jax.sharding.Mesh(
-        mesh.devices.reshape(4, 4, 4, 2, mesh.shape["head"]), SEQ + ("head",)
+        mesh.devices.reshape(8, 2, 4, 2, mesh.shape["head"]), SEQ + ("head",)
     )
 
     return jax.shard_map(

time: 125 us -> 127 us (1.016)
  blocking collectives: 96.1 us -> 104 us
  starting transfers between devices: 10.9 us -> 5.74 us
  local copies, waits for them, and re-layouts: 3.27 us -> 0.05 us
  waiting for transfers between devices: 2.23 us -> 4.89 us
    all_to_all x1 -> x2, blocking collectives: 38.4 us -> 49 us  [the longest x1 26.4 us: on_device(): returned = lax.all_to_all(partial, 'zb', 0, 0, tiled=True)]
    all_to_all x1 -> x0, starting transfers between devices: 8.95 us -> none  [on_device(): gathered = lax.all_to_all(asked, around, 0, 0, tiled=True)]
    ppermute x1 -> x2, starting transfers between devices: 1.91 us -> 5.74 us  [the longest x1 3.83 us: on_device(): pair = spread(filled, lax.ppermute(filled, 'za', trade), lax.axis_size('y'))]
    unnamed x26 -> x20, local copies, waits for them, and re-layouts: 3.27 us -> 0.05 us
    all_gather x1, blocking collectives: 38.5 us -> 35.8 us  [on_device(): gathered = lax.all_gather(query, 'zb', axis=0, tiled=True)]
    ppermute x1 -> x2, waiting for transfers between devices: 2.23 us -> 4.89 us  [the longest x1 4.89 us: on_device(): pair = spread(filled, lax.ppermute(filled, 'za', trade), lax.axis_size('y'))]
    pallas_call x1, Pallas kernels: 5.8 us -> 4.52 us  [attend(): pl.pallas_call(functools.partial(attend_kernel, chunk=chunk, around=aroun...]
where the time goes in v4:
time: 127 us; the launch traced here: 125 us
  blocking collectives  104 us (82%)
  Pallas kernels  8.21 us (6%)
  starting transfers between devices  5.74 us (5%)
  waiting for transfers between devices  4.89 us (4%)
  between operations  2.06 us (2%)
    all_gather x1, blocking collectives, on_device(): gathered = lax.all_gather(query, 'zb', axis=0, tiled=True)  35.8 us
    all_to_all x1, blocking collectives, on_device(): returned = lax.all_to_all(partial, 'zb', 0, 0, tiled=True)  26.4 us
    all_to_all x1, blocking collectives, on_device(): near = lax.all_to_all(pair, 'y', 0, 0, tiled=True)  22.6 us
    all_to_all x1, blocking collectives, on_device(): terms = lax.all_to_all(terms, 'head', 0, 0, tiled=True)  11.3 us
    all_to_all x1, blocking collectives, on_device(): stats = lax.all_to_all(stats, 'head', 0, 0, tiled=True)  8.27 us
    ppermute x1, waiting for transfers between devices, on_device(): pair = spread(filled, lax.ppermute(filled, 'za', trade), lax.axis_size('y'))  4.89 us
    pallas_call x1, Pallas kernels, attend(): pl.pallas_call(functools.partial(attend_kernel, chunk=chunk, around=aroun...  4.52 us
    ppermute x1, starting transfers between devices, on_device(): pair = spread(filled, lax.ppermute(filled, 'za', trade), lax.axis_size('y'))  3.83 us
  transfers between devices with their start and end apart: 2, of which 1 were waited for; matrix products, arithmetic and copies ran while one was open for 0% of the time, Pallas kernels for 0%

profile of v4, /device:TPU:24, one launch (start us, length us, event | category | flops | bytes accessed | tf_op | source)
XLA Modules:
  0.0 125.2 jit_solution(1881111137528055554)
XLA Ops:
  1.9 1.2 shard_map.149
  3.2 3.8 %collective-permute-start = (bf16[2,128,384]{2,1,0:T(8,128)(2,1)S(1)}, bf16[2,128,384]{2,1,0:T(8,128)(2,1)S(1)}, u32[]{:S(2)}, u32[]{:S(2)}) collective-permute-start(bf16[2,128,384]{2,1,0:T(8,128)(2,1)S(1)} %get-tuple-element.7.own_ref), channel_id=1, source_target_pairs={{0,32},{32,0},{1,33},{33,1},{2,34},{34,2},{3,35},{35,3},{4,36},{36... | collective-permute-start | bytes 589832 | tf_op jit(solution)/shard_map/ppermute | solution.py:313
  7.0 4.9 %collective-permute-done.other_ref = bf16[2,128,384]{2,1,0:T(8,128)(2,1)S(1)} collective-permute-done((bf16[2,128,384]{2,1,0:T(8,128)(2,1)S(1)}, bf16[2,128,384]{2,1,0:T(8,128)(2,1)S(1)}, u32[]{:S(2)}, u32[]{:S(2)}) %collective-permute-start) | collective-permute-done | bytes 196640 | tf_op jit(solution)/shard_map/ppermute | solution.py:313
  11.9 0.1 shard_map.150
  12.0 0.0 copy-start.9
  12.0 0.0 copy-start.1
  12.0 22.6 %all_to_all.20.a_ref = bf16[4,2,2,128,384]{4,3,2,1,0:T(8,128)(2,1)S(1)} all-to-all(bf16[4,2,2,128,384]{4,3,2,1,0:T(8,128)(2,1)S(1)} %shard_map.150), channel_id=1, replica_groups=mesh['zb'=8,'za'=2,'y'=4,'core'=2,'head'=4] {'y'}, dimensions={0} | all-to-all | bytes 3145728 | tf_op jit(solution)/shard_map/all_to_all | solution.py:314
  34.6 1.9 %collective-permute-start.1 = (bf16[4,2,2,128,384]{4,3,2,1,0:T(8,128)(2,1)S(1)}, bf16[4,2,2,128,384]{4,3,2,1,0:T(8,128)(2,1)S(1)}, u32[]{:S(2)}, u32[]{:S(2)}) collective-permute-start(bf16[4,2,2,128,384]{4,3,2,1,0:T(8,128)(2,1)S(1)} %all_to_all.20.a_ref), channel_id=1, source_target_pairs={{0,4},{4,0},{1,5},{5,1},{2,6},{6,2},{3,7},{7,3},{8,12},{12,8},{9,1... | collective-permute-start | bytes 4718600 | tf_op jit(solution)/shard_map/ppermute | solution.py:316
  36.6 0.0 copy-done.9
  36.6 35.8 %all_gather.3.q_ref = bf16[384,384]{1,0:T(8,128)(2,1)S(1)} all-gather(bf16[48,384]{1,0:T(8,128)(2,1)S(1)} %copy-done.9), channel_id=1, replica_groups=mesh['zb'=8,'za'=2,'y'=4,'core'=2,'head'=4] {'zb'}, dimensions={0}, use_global_device_ids=true | all-gather | bytes 331776 | tf_op jit(solution)/shard_map/all_gather | solution.py:315
  72.3 0.0 copy-start
  72.3 0.0 collective-permute-done.1.b_ref
  72.3 0.0 copy-done.1
  72.3 4.5 %shard_map.151 = bf16[8,152,128]{2,1,0:T(8,128)(2,1)S(1)} custom-call(bf16[384,384]{1,0:T(8,128)(2,1)S(1)} %all_gather.3.q_ref, bf16[4,2,2,128,384]{4,3,2,1,0:T(8,128)(2,1)S(1)} %all_to_all.20.a_ref, bf16[4,2,2,128,384]{4,3,2,1,0:T(8,128)(2,1)S(1)} %collective-permute-done.1.b_ref, bf16[2,512,384]{2,1,0:T(8,128)(2,1)S(1)} %copy-done.1), custom_call_target="tpu_custom_call" | custom-call | tf_op jit(solution)/shard_map/pallas_call | solution.py:144
  76.9 26.4 %all_to_all.21.got_ref = bf16[8,152,128]{2,1,0:T(8,128)(2,1)S(1)} all-to-all(bf16[8,152,128]{2,1,0:T(8,128)(2,1)S(1)} %shard_map.151), channel_id=1, replica_groups=mesh['zb'=8,'za'=2,'y'=4,'core'=2,'head'=4] {'zb'}, dimensions={0} | all-to-all | bytes 622592 | tf_op jit(solution)/shard_map/all_to_all | solution.py:318
  103.2 0.0 copy-done
  103.2 0.0 copy-start.2
  103.2 0.0 copy-start.3
  103.2 0.0 copy-start.6
  103.2 0.0 copy-start.7
  103.3 0.0 copy-start.4
  103.3 0.0 copy-start.5
  103.3 0.0 copy-start.8
  103.3 0.8 shard_map.152
  104.2 11.3 %all_to_all.22.got_ref = bf16[4,48,768]{2,1,0:T(8,128)(2,1)S(1)} all-to-all(bf16[4,48,768]{2,1,0:T(8,128)(2,1)S(1)} %shard_map.152), channel_id=1, replica_groups=mesh['zb'=8,'za'=2,'y'=4,'core'=2,'head'=4] {'head'}, dimensions={0} | all-to-all | bytes 589824 | tf_op jit(solution)/shard_map/all_to_all | solution.py:320
  115.4 0.0 copy-done.2
  115.4 0.0 copy-done.3
  115.4 0.0 copy-done.6
  115.4 0.0 copy-done.7
  115.4 0.4 shard_map.153
  115.8 8.3 %all_to_all.23.got_ref = f32[4,56,128]{2,1,0:T(8,128)S(1)} all-to-all(f32[4,56,128]{2,1,0:T(8,128)S(1)} %shard_map.153), channel_id=1, replica_groups=mesh['zb'=8,'za'=2,'y'=4,'core'=2,'head'=4] {'head'}, dimensions={0} | all-to-all | bytes 229376 | tf_op jit(solution)/shard_map/all_to_all | solution.py:324
  124.1 0.0 copy-done.4
  124.1 0.0 copy-done.5
  124.1 0.0 copy-done.8
  124.1 1.1 shard_map.154
Async XLA Ops:
  3.2 8.7 %collective-permute-start = (bf16[2,128,384]{2,1,0:T(8,128)(2,1)S(1)}, bf16[2,128,384]{2,1,0:T(8,128)(2,1)S(1)}, u32[]{:S(2)}, u32[]{:S(2)}) collective-permute-start(bf16[2,128,384]{2,1,0:T(8,128)(2,1)S(1)} %get-tuple-element.7.own_ref), channel_id=1, source_target_pairs={{0,32},{32,0},{1,33},{33,1},{2,34},{34,2},{3,35},{35,3},{4,36},{36... | collective-permute-start | bytes 589832 | tf_op jit(solution)/shard_map/ppermute | solution.py:313
  12.0 24.5 %copy-start.9 = (bf16[48,384]{1,0:T(8,128)(2,1)S(1)}, bf16[48,384]{1,0:T(8,128)(2,1)}, u32[]{:S(2)}) copy-start(bf16[48,384]{1,0:T(8,128)(2,1)} %param.14) | copy-start | bytes 110596
  12.0 60.3 %copy-start.1 = (bf16[2,512,384]{2,1,0:T(8,128)(2,1)S(1)}, bf16[2,512,384]{2,1,0:T(8,128)(2,1)}, u32[]{:S(2)}) copy-start(bf16[2,512,384]{2,1,0:T(8,128)(2,1)} %t_ref.1) | copy-start | bytes 2359300
  34.6 37.7 %collective-permute-start.1 = (bf16[4,2,2,128,384]{4,3,2,1,0:T(8,128)(2,1)S(1)}, bf16[4,2,2,128,384]{4,3,2,1,0:T(8,128)(2,1)S(1)}, u32[]{:S(2)}, u32[]{:S(2)}) collective-permute-start(bf16[4,2,2,128,384]{4,3,2,1,0:T(8,128)(2,1)S(1)} %all_to_all.20.a_ref), channel_id=1, source_target_pairs={{0,4},{4,0},{1,5},{5,1},{2,6},{6,2},{3,7},{7,3},{8,12},{12,8},{9,1... | collective-permute-start | bytes 4718600 | tf_op jit(solution)/shard_map/ppermute | solution.py:316
  72.3 30.9 %copy-start = (bf16[384,3072]{1,0:T(8,128)(2,1)S(1)}, bf16[384,3072]{1,0:T(8,128)(2,1)}, u32[]{:S(2)}) copy-start(bf16[384,3072]{1,0:T(8,128)(2,1)} %w_ref.1) | copy-start | bytes 7077892
  103.2 12.2 %copy-start.2 = (f32[768,64]{0,1:T(8,128)S(1)}, f32[768,64]{0,1:T(8,128)}, u32[]{:S(2)}) copy-start(f32[768,64]{0,1:T(8,128)} %param.24) | copy-start | bytes 589828
  103.2 12.2 %copy-start.3 = (bf16[48,768]{1,0:T(8,128)(2,1)S(1)}, bf16[48,768]{1,0:T(8,128)(2,1)}, u32[]{:S(2)}) copy-start(bf16[48,768]{1,0:T(8,128)(2,1)} %hidden_ref.1) | copy-start | bytes 221188
  103.2 12.2 %copy-start.6 = (f32[768]{0:T(1024)S(1)}, f32[768]{0:T(1024)}, u32[]{:S(2)}) copy-start(f32[768]{0:T(1024)} %param.23) | copy-start | bytes 9220
  103.2 12.2 %copy-start.7 = (f32[768]{0:T(1024)S(1)}, f32[768]{0:T(1024)}, u32[]{:S(2)}) copy-start(f32[768]{0:T(1024)} %param.22) | copy-start | bytes 9220
  103.3 20.9 %copy-start.4 = (f32[128,64]{0,1:T(8,128)S(1)}, f32[128,64]{0,1:T(8,128)}, u32[]{:S(2)}) copy-start(f32[128,64]{0,1:T(8,128)} %param.25) | copy-start | bytes 98308
  103.3 20.8 %copy-start.5 = (f32[128,64]{0,1:T(8,128)S(1)}, f32[128,64]{0,1:T(8,128)}, u32[]{:S(2)}) copy-start(f32[128,64]{0,1:T(8,128)} %param.26) | copy-start | bytes 98308
  103.3 20.8 %copy-start.8 = (s32[48]{0:T(128)S(1)}, s32[48]{0:T(128)}, u32[]{:S(2)}) copy-start(s32[48]{0:T(128)} %param.18) | copy-start | bytes 580

commit v5 on v4

--- a/solution.py
+++ b/solution.py
@@ -41,7 +41,9 @@
     return lax.broadcasted_iota(jnp.int32, (rows, cols), 0) == local
 
 
-def fill_kernel(count_ref, step_ref, pos_ref, new_ref, cache_ref, out_ref, row_ref):
+def fill_kernel(
+    count_ref, step_ref, pos_ref, q_ref, new_ref, cache_ref, out_ref, asked_ref, row_ref
+):
     rows, cols = cache_ref.shape[1], new_ref.shape[1]
     matched = one_hot(pos_ref, count_ref, rows, cols)
     pick = matched.astype(f32)
@@ -51,39 +53,27 @@
         placed = jnp.dot(pick, new_ref[s], preferred_element_type=f32)
         merged = jnp.where(keep, cache_ref[s].astype(f32), placed).astype(bf16)
         out_ref[s] = merged
+    for d in range(asked_ref.shape[0]):
+        asked_ref[d] = q_ref[...]
     row_ref[...] = jnp.broadcast_to(step_ref[...], row_ref.shape)
 
 
-def fill(count, step_size, pos, new_kv, cache_kv):
+def fill(count, step_size, pos, query, new_kv, cache_kv, copies):
     return pl.pallas_call(
         fill_kernel,
         out_shape=(
             pltpu.VMEM(cache_kv.shape, bf16),
+            pltpu.VMEM((copies,) + query.shape, bf16),
             pltpu.VMEM((8, 128), f32),
         ),
-        in_specs=[VM] * 5,
-        out_specs=(VM, VM),
+        in_specs=[VM] * 6,
+        out_specs=(VM, VM, VM),
         compiler_params=grant(8),
-    )(count, step_size, *remote(pos, new_kv, cache_kv))
-
-
-def spread_kernel(own_ref, other_ref, out_ref):
-    for d in range(out_ref.shape[0]):
-        out_ref[d, 0] = own_ref[...]
-        out_ref[d, 1] = other_ref[...]
-
-
-def spread(own, other, copies):
-    return pl.pallas_call(
-        spread_kernel,
-        out_shape=pltpu.VMEM((copies, 2) + own.shape, bf16),
-        in_specs=[VM] * 2,
-        out_specs=VM,
-        compiler_params=grant(8),
-    )(*local(own, other))
-
-
-def attend_kernel(q_ref, a_ref, b_ref, t_ref, out_ref, *, chunk, around):
+    )(count, step_size, *remote(pos, query, new_kv, cache_kv))
+
+
+def attend_kernel(q_ref, *refs, chunk, around):
+    *kv_refs, t_ref, out_ref = refs
     parts = out_ref.shape[0]
     slots = q_ref.shape[0] // parts
     heads = q_ref.shape[1] // HD
@@ -98,10 +88,10 @@
         eye = lane == slot + slots * (h % 2)
         base = 3 * (h // 2)
         keys, values = [], []
-        for ref in (a_ref, b_ref):
-            n = ref.shape[0] * ref.shape[1] * ref.shape[3]
-            keys.append(ref[:, :, 0, :, cols].reshape(n, HD))
-            values.append(ref[:, :, 1, :, cols].reshape(n, HD))
+        for ref in kv_refs:
+            n = ref.shape[0] * ref.shape[2]
+            keys.append(ref[:, 0, :, cols].reshape(n, HD))
+            values.append(ref[:, 1, :, cols].reshape(n, HD))
         keys.append(t_ref[0, own_text, cols])
         values.append(t_ref[1, own_text, cols])
         for start in range(0, q_ref.shape[0], chunk):
@@ -139,15 +129,15 @@
         out_ref[d, heads * slots : heads * slots + STAT, :] = stats[d].astype(bf16)
 
 
-def attend(parts, around, queries, near, far, text_kv, slots, chunk):
+def attend(parts, around, queries, blocks, text_kv, slots, chunk):
     heads = queries.shape[1] // HD
     return pl.pallas_call(
         functools.partial(attend_kernel, chunk=chunk, around=around),
         out_shape=pltpu.VMEM((parts, heads * slots + STAT, HD), bf16),
-        in_specs=[VM] * 4,
+        in_specs=[VM] * (len(blocks) + 2),
         out_specs=VM,
         compiler_params=grant(20),
-    )(*local(queries, near, far, text_kv))
+    )(*local(queries, *blocks, text_kv))
 
 
 def merge_kernel(got_ref, w_ref, out_ref):
@@ -309,12 +299,18 @@
 
     count = counts.reshape(1, 1)
     pos = active.reshape(1, slots)
-    filled, step_row = fill(count, step_size.reshape(1, 1), pos, new_kv, cache_kv)
-    pair = spread(filled, lax.ppermute(filled, "za", trade), lax.axis_size("y"))
-    near = lax.all_to_all(pair, "y", 0, 0, tiled=True)
-    gathered = lax.all_gather(query, "zb", axis=0, tiled=True)
-    far = lax.ppermute(near, "core", trade)
-    partial = attend(parts, "zb", gathered, near, far, text_kv, slots, 192)
+    filled, asked, step_row = fill(
+        count, step_size.reshape(1, 1), pos, query, new_kv, cache_kv, parts
+    )
+    other = lax.ppermute(filled, "za", trade)
+    gathered = lax.all_to_all(asked, "zb", 0, 0, tiled=True)
+    gathered = gathered.reshape(parts * slots, -1)
+    own = lax.all_gather(filled, "y", axis=0, tiled=False)
+    own_far = lax.ppermute(own, "core", trade)
+    other = lax.all_gather(other, "y", axis=0, tiled=False)
+    other_far = lax.ppermute(other, "core", trade)
+    blocks = (own, own_far, other, other_far)
+    partial = attend(parts, "zb", gathered, blocks, text_kv, slots, 192)
     returned = lax.all_to_all(partial, "zb", 0, 0, tiled=True)
     terms = merge(returned, w_out, groups)
     terms = lax.all_to_all(terms, "head", 0, 0, tiled=True)

time: 127 us -> 122 us (0.961)
  blocking collectives: 104 us -> 84.1 us
  starting transfers between devices: 5.74 us -> 21.8 us
  waiting for transfers between devices: 4.89 us -> 2.25 us
  local copies, waits for them, and re-layouts: 0.05 us -> 2.08 us
    all_to_all x1 -> x0, blocking collectives: 22.6 us -> none  [on_device(): near = lax.all_to_all(pair, 'y', 0, 0, tiled=True)]
    all_to_all x0 -> x1, starting transfers between devices: none -> 15.1 us  [on_device(): gathered = lax.all_to_all(asked, 'zb', 0, 0, tiled=True)]
    all_to_all x1, blocking collectives: 26.4 us -> 36 us  [on_device(): returned = lax.all_to_all(partial, 'zb', 0, 0, tiled=True)]
    all_gather x1 -> x2, blocking collectives: 35.8 us -> 28.9 us  [the longest x1 14.6 us: on_device(): other = lax.all_gather(other, 'y', axis=0, tiled=False)]
    ppermute x2 -> x3, waiting for transfers between devices: 4.89 us -> 2.25 us  [the longest x1 2.24 us: on_device(): other_far = lax.ppermute(other, 'core', trade)]
    unnamed x20 -> x22, local copies, waits for them, and re-layouts: 0.05 us -> 2.08 us
    ppermute x2 -> x3, starting transfers between devices: 5.74 us -> 6.73 us  [the longest x1 2.91 us: on_device(): other = lax.ppermute(filled, 'za', trade)]
  transfers between devices with their start and end apart: 2 -> 4, of which waited for: 1 -> 1; matrix products, arithmetic and copies ran while one was open for 0% -> 0% of each run, Pallas kernels for 0% -> 0%
where the time goes in v5:
time: 122 us; the launch traced here: 121 us
  blocking collectives  84.1 us (69%)
  starting transfers between devices  21.8 us (18%)
  Pallas kernels  8.77 us (7%)
  waiting for transfers between devices  2.25 us (2%)
  between operations  2.13 us (2%)
  local copies, waits for them, and re-layouts  2.08 us (2%)
    all_to_all x1, blocking collectives, on_device(): returned = lax.all_to_all(partial, 'zb', 0, 0, tiled=True)  36 us
    all_to_all x1, starting transfers between devices, on_device(): gathered = lax.all_to_all(asked, 'zb', 0, 0, tiled=True)  15.1 us
    all_gather x1, blocking collectives, on_device(): other = lax.all_gather(other, 'y', axis=0, tiled=False)  14.6 us
    all_gather x1, blocking collectives, on_device(): own = lax.all_gather(filled, 'y', axis=0, tiled=False)  14.3 us
    all_to_all x1, blocking collectives, on_device(): terms = lax.all_to_all(terms, 'head', 0, 0, tiled=True)  10.9 us
    all_to_all x1, blocking collectives, on_device(): stats = lax.all_to_all(stats, 'head', 0, 0, tiled=True)  8.27 us
    pallas_call x1, Pallas kernels, attend(): pl.pallas_call(functools.partial(attend_kernel, chunk=chunk, around=aroun...  4.56 us
    ppermute x1, starting transfers between devices, on_device(): other = lax.ppermute(filled, 'za', trade)  2.91 us
  transfers between devices with their start and end apart: 4, of which 1 were waited for; matrix products, arithmetic and copies ran while one was open for 0% of the time, Pallas kernels for 0%

profile of v5, /device:TPU:24, one launch (start us, length us, event | category | flops | bytes accessed | tf_op | source)
XLA Modules:
  0.0 121.2 jit_solution(8500786972550083555)
XLA Ops:
  0.6 0.0 copy-start.1
  2.0 1.9 %shard_map.149 = (bf16[2,128,384]{2,1,0:T(8,128)(2,1)S(1)}, bf16[8,48,384]{2,1,0:T(8,128)(2,1)}, f32[8,128]{1,0:T(8,128)S(1)}) custom-call(s32[1,1]{1,0:T(1,128)} %bitcast.13.count_ref, f32[1,1]{1,0:T(1,128)} %bitcast.15.step_ref, s32[1,48]{1,0:T(1,128)} %bitcast.26, bf16[48,384]{1,0:T(8,128)(2,1)} %q_ref.1, bf16[2,48,384]{2,1,0:T(8,128)(2,1)} %new_ref.1, ...), custom_call_target="tpu_custom_call" | custom-call | tf_op jit(solution)/shard_map/pallas_call | solution.py:62
  3.9 15.1 %all-to-all-start = ((bf16[8,48,384]{2,1,0:T(8,128)(2,1)}), bf16[8,48,384]{2,1,0:T(8,128)(2,1)S(1)}, u32[]{:S(2)}, u32[]{:S(2)}) async-start(bf16[8,48,384]{2,1,0:T(8,128)(2,1)} %get-tuple-element.8), calls=%async_computation | async-start | bytes 589824 | tf_op jit(solution)/shard_map/all_to_all | solution.py:306
  19.0 2.9 %collective-permute-start.1 = (bf16[2,128,384]{2,1,0:T(8,128)(2,1)S(1)}, bf16[2,128,384]{2,1,0:T(8,128)(2,1)S(1)}, u32[]{:S(2)}, u32[]{:S(2)}) collective-permute-start(bf16[2,128,384]{2,1,0:T(8,128)(2,1)S(1)} %get-tuple-element.9), channel_id=1, source_target_pairs={{0,32},{32,0},{1,33},{33,1},{2,34},{34,2},{3,35},{35,3},{4,36},{36... | collective-permute-start | bytes 589832 | tf_op jit(solution)/shard_map/ppermute | solution.py:305
  21.9 14.3 %all-gather = bf16[8,128,384]{2,1,0:T(8,128)(2,1)S(1)} all-gather(bf16[2,128,384]{2,1,0:T(8,128)(2,1)S(1)} %get-tuple-element.9), channel_id=2, replica_groups=mesh['zb'=8,'za'=2,'y'=4,'core'=2,'head'=4] {'y'}, dimensions={0}, use_global_device_ids=true | all-gather | bytes 983040 | tf_op jit(solution)/shard_map/all_gather | solution.py:308
  36.2 1.9 %collective-permute-start = (bf16[4,2,128,384]{3,2,1,0:T(8,128)(2,1)S(1)}, bf16[4,2,128,384]{3,2,1,0:T(8,128)(2,1)S(1)}, u32[]{:S(2)}, u32[]{:S(2)}) collective-permute-start(bf16[4,2,128,384]{3,2,1,0:T(8,128)(2,1)S(1)} %bitcast.16), channel_id=1, source_target_pairs={{0,4},{4,0},{1,5},{5,1},{2,6},{6,2},{3,7},{7,3},{8,12},{12,8},{9,1... | collective-permute-start | bytes 2359304 | tf_op jit(solution)/shard_map/ppermute | solution.py:309
  38.2 0.0 collective-permute-done.1
  38.2 14.6 %all-gather.1 = bf16[8,128,384]{2,1,0:T(8,128)(2,1)S(1)} all-gather(bf16[2,128,384]{2,1,0:T(8,128)(2,1)S(1)} %collective-permute-done.1), channel_id=3, replica_groups=mesh['zb'=8,'za'=2,'y'=4,'core'=2,'head'=4] {'y'}, dimensions={0}, use_global_device_ids=true | all-gather | bytes 983040 | tf_op jit(solution)/shard_map/all_gather | solution.py:310
  52.8 1.9 %collective-permute-start.2 = (bf16[4,2,128,384]{3,2,1,0:T(8,128)(2,1)S(1)}, bf16[4,2,128,384]{3,2,1,0:T(8,128)(2,1)S(1)}, u32[]{:S(2)}, u32[]{:S(2)}) collective-permute-start(bf16[4,2,128,384]{3,2,1,0:T(8,128)(2,1)S(1)} %bitcast.18), channel_id=1, source_target_pairs={{0,4},{4,0},{1,5},{5,1},{2,6},{6,2},{3,7},{7,3},{8,12},{12,8},{9,1... | collective-permute-start | bytes 2359304 | tf_op jit(solution)/shard_map/ppermute | solution.py:311
  54.7 0.0 collective-permute-done.refs_1_
  54.7 2.2 %collective-permute-done.2.refs_3_ = bf16[4,2,128,384]{3,2,1,0:T(8,128)(2,1)S(1)} collective-permute-done((bf16[4,2,128,384]{3,2,1,0:T(8,128)(2,1)S(1)}, bf16[4,2,128,384]{3,2,1,0:T(8,128)(2,1)S(1)}, u32[]{:S(2)}, u32[]{:S(2)}) %collective-permute-start.2) | collective-permute-done | bytes 786464 | tf_op jit(solution)/shard_map/ppermute | solution.py:311
  56.9 0.0 copy-start.2
  56.9 0.9 copy-done.2
  57.8 0.0 all-to-all-done
  57.8 0.0 copy-done.1
  57.8 0.0 copy-start.3
  57.8 1.1 copy-done.3
  59.0 0.0 copy-start
  59.0 4.6 %shard_map.150 = bf16[8,152,128]{2,1,0:T(8,128)(2,1)S(1)} custom-call(bf16[384,384]{1,0:T(8,128)(2,1)S(1)} %bitcast.20, bf16[4,2,128,384]{3,2,1,0:T(8,128)(2,1)S(1)} %bitcast.17, bf16[4,2,128,384]{3,2,1,0:T(8,128)(2,1)S(1)} %collective-permute-done.refs_1_, bf16[4,2,128,384]{3,2,1,0:T(8,128)(2,1)S(1)} %bitcast.19, bf16[4,2,128,384]{3,2,1,0:T(8,128)(2,1)S(1)} %copy-done.3, ...), custom_call_target="tpu_custom_call" | custom-call | tf_op jit(solution)/shard_map/pallas_call | solution.py:134
  63.5 0.0 copy-start.4
  63.6 0.0 copy-start.5
  63.6 0.0 copy-start.8
  63.6 0.0 copy-start.9
  63.6 36.0 %all_to_all.20.got_ref = bf16[8,152,128]{2,1,0:T(8,128)(2,1)S(1)} all-to-all(bf16[8,152,128]{2,1,0:T(8,128)(2,1)S(1)} %shard_map.150), channel_id=1, replica_groups=mesh['zb'=8,'za'=2,'y'=4,'core'=2,'head'=4] {'zb'}, dimensions={0} | all-to-all | bytes 622592 | tf_op jit(solution)/shard_map/all_to_all | solution.py:314
  99.6 0.0 copy-done
  99.6 0.0 copy-start.6
  99.6 0.0 copy-start.7
  99.6 0.0 copy-start.10
  99.6 0.8 shard_map.151
  100.4 10.9 %all_to_all.21.got_ref = bf16[4,48,768]{2,1,0:T(8,128)(2,1)S(1)} all-to-all(bf16[4,48,768]{2,1,0:T(8,128)(2,1)S(1)} %shard_map.151), channel_id=1, replica_groups=mesh['zb'=8,'za'=2,'y'=4,'core'=2,'head'=4] {'head'}, dimensions={0} | all-to-all | bytes 589824 | tf_op jit(solution)/shard_map/all_to_all | solution.py:316
  111.4 0.0 copy-done.4
  111.4 0.0 copy-done.5
  111.4 0.0 copy-done.8
  111.4 0.0 copy-done.9
  111.4 0.4 shard_map.152
  111.8 8.3 %all_to_all.22.got_ref = f32[4,56,128]{2,1,0:T(8,128)S(1)} all-to-all(f32[4,56,128]{2,1,0:T(8,128)S(1)} %shard_map.152), channel_id=1, replica_groups=mesh['zb'=8,'za'=2,'y'=4,'core'=2,'head'=4] {'head'}, dimensions={0} | all-to-all | bytes 229376 | tf_op jit(solution)/shard_map/all_to_all | solution.py:320
  120.1 0.0 copy-done.6
  120.1 0.0 copy-done.7
  120.1 0.0 copy-done.10
  120.1 1.1 shard_map.153
Async XLA Ops:
  0.6 57.2 %copy-start.1 = (bf16[2,512,384]{2,1,0:T(8,128)(2,1)S(1)}, bf16[2,512,384]{2,1,0:T(8,128)(2,1)}, u32[]{:S(2)}) copy-start(bf16[2,512,384]{2,1,0:T(8,128)(2,1)} %refs_4_.1) | copy-start | bytes 2359300
  3.9 53.9 %all-to-all-start = ((bf16[8,48,384]{2,1,0:T(8,128)(2,1)}), bf16[8,48,384]{2,1,0:T(8,128)(2,1)S(1)}, u32[]{:S(2)}, u32[]{:S(2)}) async-start(bf16[8,48,384]{2,1,0:T(8,128)(2,1)} %get-tuple-element.8), calls=%async_computation | async-start | bytes 589824 | tf_op jit(solution)/shard_map/all_to_all | solution.py:306
  19.0 19.2 %collective-permute-start.1 = (bf16[2,128,384]{2,1,0:T(8,128)(2,1)S(1)}, bf16[2,128,384]{2,1,0:T(8,128)(2,1)S(1)}, u32[]{:S(2)}, u32[]{:S(2)}) collective-permute-start(bf16[2,128,384]{2,1,0:T(8,128)(2,1)S(1)} %get-tuple-element.9), channel_id=1, source_target_pairs={{0,32},{32,0},{1,33},{33,1},{2,34},{34,2},{3,35},{35,3},{4,36},{36... | collective-permute-start | bytes 589832 | tf_op jit(solution)/shard_map/ppermute | solution.py:305
  36.2 18.4 %collective-permute-start = (bf16[4,2,128,384]{3,2,1,0:T(8,128)(2,1)S(1)}, bf16[4,2,128,384]{3,2,1,0:T(8,128)(2,1)S(1)}, u32[]{:S(2)}, u32[]{:S(2)}) collective-permute-start(bf16[4,2,128,384]{3,2,1,0:T(8,128)(2,1)S(1)} %bitcast.16), channel_id=1, source_target_pairs={{0,4},{4,0},{1,5},{5,1},{2,6},{6,2},{3,7},{7,3},{8,12},{12,8},{9,1... | collective-permute-start | bytes 2359304 | tf_op jit(solution)/shard_map/ppermute | solution.py:309
  52.8 4.2 %collective-permute-start.2 = (bf16[4,2,128,384]{3,2,1,0:T(8,128)(2,1)S(1)}, bf16[4,2,128,384]{3,2,1,0:T(8,128)(2,1)S(1)}, u32[]{:S(2)}, u32[]{:S(2)}) collective-permute-start(bf16[4,2,128,384]{3,2,1,0:T(8,128)(2,1)S(1)} %bitcast.18), channel_id=1, source_target_pairs={{0,4},{4,0},{1,5},{5,1},{2,6},{6,2},{3,7},{7,3},{8,12},{12,8},{9,1... | collective-permute-start | bytes 2359304 | tf_op jit(solution)/shard_map/ppermute | solution.py:311
  56.9 0.9 copy-start.2
  57.8 1.1 copy-start.3
  59.0 40.6 %copy-start = (bf16[384,3072]{1,0:T(8,128)(2,1)S(1)}, bf16[384,3072]{1,0:T(8,128)(2,1)}, u32[]{:S(2)}) copy-start(bf16[384,3072]{1,0:T(8,128)(2,1)} %w_ref.1) | copy-start | bytes 7077892
  63.5 47.8 %copy-start.4 = (f32[768,64]{0,1:T(8,128)S(1)}, f32[768,64]{0,1:T(8,128)}, u32[]{:S(2)}) copy-start(f32[768,64]{0,1:T(8,128)} %param.24) | copy-start | bytes 589828
  63.6 47.8 %copy-start.5 = (bf16[48,768]{1,0:T(8,128)(2,1)S(1)}, bf16[48,768]{1,0:T(8,128)(2,1)}, u32[]{:S(2)}) copy-start(bf16[48,768]{1,0:T(8,128)(2,1)} %hidden_ref.1) | copy-start | bytes 221188
  63.6 47.8 %copy-start.8 = (f32[768]{0:T(1024)S(1)}, f32[768]{0:T(1024)}, u32[]{:S(2)}) copy-start(f32[768]{0:T(1024)} %param.23) | copy-start | bytes 9220
  63.6 47.8 %copy-start.9 = (f32[768]{0:T(1024)S(1)}, f32[768]{0:T(1024)}, u32[]{:S(2)}) copy-start(f32[768]{0:T(1024)} %param.22) | copy-start | bytes 9220
  99.6 20.5 %copy-start.6 = (f32[128,64]{0,1:T(8,128)S(1)}, f32[128,64]{0,1:T(8,128)}, u32[]{:S(2)}) copy-start(f32[128,64]{0,1:T(8,128)} %param.25) | copy-start | bytes 98308
  99.6 20.5 %copy-start.7 = (f32[128,64]{0,1:T(8,128)S(1)}, f32[128,64]{0,1:T(8,128)}, u32[]{:S(2)}) copy-start(f32[128,64]{0,1:T(8,128)} %param.26) | copy-start | bytes 98308
  99.6 20.5 %copy-start.10 = (s32[48]{0:T(128)S(1)}, s32[48]{0:T(128)}, u32[]{:S(2)}) copy-start(s32[48]{0:T(128)} %param.18) | copy-start | bytes 580

commit v6 on v4

--- a/solution.py
+++ b/solution.py
@@ -13,7 +13,7 @@
 EPS = 1e-06
 LOG2E = 1.4426950408889634
 SCALE = HD ** (-0.5)
-SEQ = ("zb", "za", "y", "core")
+SEQ = ("zh", "zq", "za", "y", "core")
 STAT = 8
 
 
@@ -303,19 +303,22 @@
     step_size,
 ):
     groups = lax.axis_size("head")
-    parts = lax.axis_size("zb")
+    around = ("zh", "zq")
+    parts = lax.axis_size(around)
     slots = query.shape[0]
     trade = [(0, 1), (1, 0)]
 
     count = counts.reshape(1, 1)
     pos = active.reshape(1, slots)
     filled, step_row = fill(count, step_size.reshape(1, 1), pos, new_kv, cache_kv)
-    pair = spread(filled, lax.ppermute(filled, "za", trade), lax.axis_size("y"))
+    other = lax.ppermute(filled, "za", trade)
+    gathered = lax.all_gather(query, "zq", axis=0, tiled=True)
+    pair = spread(filled, other, lax.axis_size("y"))
     near = lax.all_to_all(pair, "y", 0, 0, tiled=True)
-    gathered = lax.all_gather(query, "zb", axis=0, tiled=True)
+    gathered = lax.all_gather(gathered, "zh", axis=0, tiled=True)
     far = lax.ppermute(near, "core", trade)
-    partial = attend(parts, "zb", gathered, near, far, text_kv, slots, 192)
-    returned = lax.all_to_all(partial, "zb", 0, 0, tiled=True)
+    partial = attend(parts, around, gathered, near, far, text_kv, slots, 192)
+    returned = lax.all_to_all(partial, around, 0, 0, tiled=True)
     terms = merge(returned, w_out, groups)
     terms = lax.all_to_all(terms, "head", 0, 0, tiled=True)
     stats = norm(
@@ -344,7 +347,7 @@
     )
     out_specs = (P(SEQ, None), P(SEQ, None))
     split = jax.sharding.Mesh(
-        mesh.devices.reshape(8, 2, 4, 2, mesh.shape["head"]), SEQ + ("head",)
+        mesh.devices.reshape(4, 2, 2, 4, 2, mesh.shape["head"]), SEQ + ("head",)
     )
 
     return jax.shard_map(

time: 127 us -> 125 us (0.984)
    all_gather x1 -> x2, blocking collectives: 35.8 us -> 34.4 us  [the longest x1 28.4 us: on_device(): gathered = lax.all_gather(gathered, 'zh', axis=0, tiled=True)]
where the time goes in v6:
time: 125 us; the launch traced here: 124 us
  blocking collectives  103 us (82%)
  Pallas kernels  8.21 us (7%)
  starting transfers between devices  5.74 us (5%)
  waiting for transfers between devices  4.89 us (4%)
  between operations  2.06 us (2%)
    all_gather x1, blocking collectives, on_device(): gathered = lax.all_gather(gathered, 'zh', axis=0, tiled=True)  28.4 us
    all_to_all x1, blocking collectives, on_device(): returned = lax.all_to_all(partial, around, 0, 0, tiled=True)  26 us
    all_to_all x1, blocking collectives, on_device(): near = lax.all_to_all(pair, 'y', 0, 0, tiled=True)  22.6 us
    all_to_all x1, blocking collectives, on_device(): terms = lax.all_to_all(terms, 'head', 0, 0, tiled=True)  11.6 us
    all_to_all x1, blocking collectives, on_device(): stats = lax.all_to_all(stats, 'head', 0, 0, tiled=True)  8.27 us
    all_gather x1, blocking collectives, on_device(): gathered = lax.all_gather(query, 'zq', axis=0, tiled=True)  6.06 us
    ppermute x1, waiting for transfers between devices, on_device(): other = lax.ppermute(filled, 'za', trade)  4.89 us
    pallas_call x1, Pallas kernels, attend(): pl.pallas_call(functools.partial(attend_kernel, chunk=chunk, around=aroun...  4.53 us
  transfers between devices with their start and end apart: 2, of which 1 were waited for; matrix products, arithmetic and copies ran while one was open for 0% of the time, Pallas kernels for 0%

profile of v6, /device:TPU:24, one launch (start us, length us, event | category | flops | bytes accessed | tf_op | source)
XLA Modules:
  0.0 123.8 jit_solution(17156807574862911396)
XLA Ops:
  1.9 1.2 shard_map.149
  3.2 3.8 %collective-permute-start = (bf16[2,128,384]{2,1,0:T(8,128)(2,1)S(1)}, bf16[2,128,384]{2,1,0:T(8,128)(2,1)S(1)}, u32[]{:S(2)}, u32[]{:S(2)}) collective-permute-start(bf16[2,128,384]{2,1,0:T(8,128)(2,1)S(1)} %get-tuple-element.7.own_ref), channel_id=1, source_target_pairs={{0,32},{32,0},{1,33},{33,1},{2,34},{34,2},{3,35},{35,3},{4,36},{36... | collective-permute-start | bytes 589832 | tf_op jit(solution)/shard_map/ppermute | solution.py:314
  7.0 4.9 %collective-permute-done.other_ref = bf16[2,128,384]{2,1,0:T(8,128)(2,1)S(1)} collective-permute-done((bf16[2,128,384]{2,1,0:T(8,128)(2,1)S(1)}, bf16[2,128,384]{2,1,0:T(8,128)(2,1)S(1)}, u32[]{:S(2)}, u32[]{:S(2)}) %collective-permute-start) | collective-permute-done | bytes 196640 | tf_op jit(solution)/shard_map/ppermute | solution.py:314
  11.9 0.1 shard_map.150
  12.0 0.0 copy-start.9
  12.0 0.0 copy-start.1
  12.0 22.6 %all_to_all.20.a_ref = bf16[4,2,2,128,384]{4,3,2,1,0:T(8,128)(2,1)S(1)} all-to-all(bf16[4,2,2,128,384]{4,3,2,1,0:T(8,128)(2,1)S(1)} %shard_map.150), channel_id=1, replica_groups=mesh['zh'=4,'zq'=2,'za'=2,'y'=4,'core'=2,'head'=4] {'y'}, dimensions={0} | all-to-all | bytes 3145728 | tf_op jit(solution)/shard_map/all_to_all | solution.py:317
  34.6 1.9 %collective-permute-start.1 = (bf16[4,2,2,128,384]{4,3,2,1,0:T(8,128)(2,1)S(1)}, bf16[4,2,2,128,384]{4,3,2,1,0:T(8,128)(2,1)S(1)}, u32[]{:S(2)}, u32[]{:S(2)}) collective-permute-start(bf16[4,2,2,128,384]{4,3,2,1,0:T(8,128)(2,1)S(1)} %all_to_all.20.a_ref), channel_id=1, source_target_pairs={{0,4},{4,0},{1,5},{5,1},{2,6},{6,2},{3,7},{7,3},{8,12},{12,8},{9,1... | collective-permute-start | bytes 4718600 | tf_op jit(solution)/shard_map/ppermute | solution.py:319
  36.6 0.0 copy-done.9
  36.6 6.1 %all_gather.6 = bf16[96,384]{1,0:T(8,128)(2,1)S(1)} all-gather(bf16[48,384]{1,0:T(8,128)(2,1)S(1)} %copy-done.9), channel_id=1, replica_groups=mesh['zh'=4,'zq'=2,'za'=2,'y'=4,'core'=2,'head'=4] {'zq'}, dimensions={0}, use_global_device_ids=true | all-gather | bytes 110592 | tf_op jit(solution)/shard_map/all_gather | solution.py:315
  42.6 28.4 %all_gather.7.q_ref = bf16[384,384]{1,0:T(8,128)(2,1)S(1)} all-gather(bf16[96,384]{1,0:T(8,128)(2,1)S(1)} %all_gather.6), channel_id=1, replica_groups=mesh['zh'=4,'zq'=2,'za'=2,'y'=4,'core'=2,'head'=4] {'zh'}, dimensions={0}, use_global_device_ids=true | all-gather | bytes 368640 | tf_op jit(solution)/shard_map/all_gather | solution.py:318
  71.0 0.0 copy-start
  71.0 0.0 collective-permute-done.1.b_ref
  71.0 0.0 copy-done.1
  71.0 4.5 %shard_map.151 = bf16[8,152,128]{2,1,0:T(8,128)(2,1)S(1)} custom-call(bf16[384,384]{1,0:T(8,128)(2,1)S(1)} %all_gather.7.q_ref, bf16[4,2,2,128,384]{4,3,2,1,0:T(8,128)(2,1)S(1)} %all_to_all.20.a_ref, bf16[4,2,2,128,384]{4,3,2,1,0:T(8,128)(2,1)S(1)} %collective-permute-done.1.b_ref, bf16[2,512,384]{2,1,0:T(8,128)(2,1)S(1)} %copy-done.1), custom_call_target="tpu_custom_call" | custom-call | tf_op jit(solution)/shard_map/pallas_call | solution.py:144
  75.5 26.0 %all_to_all.21.got_ref = bf16[8,152,128]{2,1,0:T(8,128)(2,1)S(1)} all-to-all(bf16[8,152,128]{2,1,0:T(8,128)(2,1)S(1)} %shard_map.151), channel_id=1, replica_groups=mesh['zh'=4,'zq'=2,'za'=2,'y'=4,'core'=2,'head'=4] {'zh','zq'}, dimensions={0} | all-to-all | bytes 622592 | tf_op jit(solution)/shard_map/all_to_all | solution.py:321
  101.5 0.0 copy-done
  101.5 0.0 copy-start.2
  101.5 0.0 copy-start.3
  101.5 0.0 copy-start.6
  101.5 0.0 copy-start.7
  101.5 0.0 copy-start.4
  101.6 0.0 copy-start.5
  101.6 0.0 copy-start.8
  101.6 0.8 shard_map.152
  102.4 11.6 %all_to_all.22.got_ref = bf16[4,48,768]{2,1,0:T(8,128)(2,1)S(1)} all-to-all(bf16[4,48,768]{2,1,0:T(8,128)(2,1)S(1)} %shard_map.152), channel_id=1, replica_groups=mesh['zh'=4,'zq'=2,'za'=2,'y'=4,'core'=2,'head'=4] {'head'}, dimensions={0} | all-to-all | bytes 589824 | tf_op jit(solution)/shard_map/all_to_all | solution.py:323
  114.0 0.0 copy-done.2
  114.0 0.0 copy-done.3
  114.0 0.0 copy-done.6
  114.0 0.0 copy-done.7
  114.0 0.4 shard_map.153
  114.4 8.3 %all_to_all.23.got_ref = f32[4,56,128]{2,1,0:T(8,128)S(1)} all-to-all(f32[4,56,128]{2,1,0:T(8,128)S(1)} %shard_map.153), channel_id=1, replica_groups=mesh['zh'=4,'zq'=2,'za'=2,'y'=4,'core'=2,'head'=4] {'head'}, dimensions={0} | all-to-all | bytes 229376 | tf_op jit(solution)/shard_map/all_to_all | solution.py:327
  122.7 0.0 copy-done.4
  122.7 0.0 copy-done.5
  122.7 0.0 copy-done.8
  122.7 1.1 shard_map.154
Async XLA Ops:
  3.2 8.7 %collective-permute-start = (bf16[2,128,384]{2,1,0:T(8,128)(2,1)S(1)}, bf16[2,128,384]{2,1,0:T(8,128)(2,1)S(1)}, u32[]{:S(2)}, u32[]{:S(2)}) collective-permute-start(bf16[2,128,384]{2,1,0:T(8,128)(2,1)S(1)} %get-tuple-element.7.own_ref), channel_id=1, source_target_pairs={{0,32},{32,0},{1,33},{33,1},{2,34},{34,2},{3,35},{35,3},{4,36},{36... | collective-permute-start | bytes 589832 | tf_op jit(solution)/shard_map/ppermute | solution.py:314
  12.0 24.5 %copy-start.9 = (bf16[48,384]{1,0:T(8,128)(2,1)S(1)}, bf16[48,384]{1,0:T(8,128)(2,1)}, u32[]{:S(2)}) copy-start(bf16[48,384]{1,0:T(8,128)(2,1)} %param.14) | copy-start | bytes 110596
  12.0 59.0 %copy-start.1 = (bf16[2,512,384]{2,1,0:T(8,128)(2,1)S(1)}, bf16[2,512,384]{2,1,0:T(8,128)(2,1)}, u32[]{:S(2)}) copy-start(bf16[2,512,384]{2,1,0:T(8,128)(2,1)} %t_ref.1) | copy-start | bytes 2359300
  34.6 36.4 %collective-permute-start.1 = (bf16[4,2,2,128,384]{4,3,2,1,0:T(8,128)(2,1)S(1)}, bf16[4,2,2,128,384]{4,3,2,1,0:T(8,128)(2,1)S(1)}, u32[]{:S(2)}, u32[]{:S(2)}) collective-permute-start(bf16[4,2,2,128,384]{4,3,2,1,0:T(8,128)(2,1)S(1)} %all_to_all.20.a_ref), channel_id=1, source_target_pairs={{0,4},{4,0},{1,5},{5,1},{2,6},{6,2},{3,7},{7,3},{8,12},{12,8},{9,1... | collective-permute-start | bytes 4718600 | tf_op jit(solution)/shard_map/ppermute | solution.py:319
  71.0 30.5 %copy-start = (bf16[384,3072]{1,0:T(8,128)(2,1)S(1)}, bf16[384,3072]{1,0:T(8,128)(2,1)}, u32[]{:S(2)}) copy-start(bf16[384,3072]{1,0:T(8,128)(2,1)} %w_ref.1) | copy-start | bytes 7077892
  101.5 12.5 %copy-start.2 = (f32[768,64]{0,1:T(8,128)S(1)}, f32[768,64]{0,1:T(8,128)}, u32[]{:S(2)}) copy-start(f32[768,64]{0,1:T(8,128)} %param.24) | copy-start | bytes 589828
  101.5 12.5 %copy-start.3 = (bf16[48,768]{1,0:T(8,128)(2,1)S(1)}, bf16[48,768]{1,0:T(8,128)(2,1)}, u32[]{:S(2)}) copy-start(bf16[48,768]{1,0:T(8,128)(2,1)} %hidden_ref.1) | copy-start | bytes 221188
  101.5 12.5 %copy-start.6 = (f32[768]{0:T(1024)S(1)}, f32[768]{0:T(1024)}, u32[]{:S(2)}) copy-start(f32[768]{0:T(1024)} %param.23) | copy-start | bytes 9220
  101.5 12.5 %copy-start.7 = (f32[768]{0:T(1024)S(1)}, f32[768]{0:T(1024)}, u32[]{:S(2)}) copy-start(f32[768]{0:T(1024)} %param.22) | copy-start | bytes 9220
  101.5 21.1 %copy-start.4 = (f32[128,64]{0,1:T(8,128)S(1)}, f32[128,64]{0,1:T(8,128)}, u32[]{:S(2)}) copy-start(f32[128,64]{0,1:T(8,128)} %param.25) | copy-start | bytes 98308
  101.6 21.1 %copy-start.5 = (f32[128,64]{0,1:T(8,128)S(1)}, f32[128,64]{0,1:T(8,128)}, u32[]{:S(2)}) copy-start(f32[128,64]{0,1:T(8,128)} %param.26) | copy-start | bytes 98308
  101.6 21.1 %copy-start.8 = (s32[48]{0:T(128)S(1)}, s32[48]{0:T(128)}, u32[]{:S(2)}) copy-start(s32[48]{0:T(128)} %param.18) | copy-start | bytes 580

commit v7 on v6

--- a/solution.py
+++ b/solution.py
@@ -85,6 +85,8 @@
 
 def attend_kernel(q_ref, a_ref, b_ref, t_ref, out_ref, *, chunk, around):
     parts = out_ref.shape[0]
+    inner = lax.axis_size(around[-1])
+    place = [d % inner * (parts // inner) + d // inner for d in range(parts)]
     slots = q_ref.shape[0] // parts
     heads = q_ref.shape[1] // HD
     share = t_ref.shape[1] // parts
@@ -126,7 +128,9 @@
             for i in range(chunk // slots):
                 d = start // slots + i
                 part = slice(i * slots, (i + 1) * slots)
-                out_ref[d, h * slots : (h + 1) * slots, :] = mixed[part].astype(bf16)
+                out_ref[place[d], h * slots : (h + 1) * slots, :] = mixed[part].astype(
+                    bf16
+                )
                 line = jnp.sum(
                     jnp.where(eye, level[part], 0.0), axis=0, keepdims=True
                 )
@@ -136,7 +140,9 @@
                 for p, piece in enumerate((first, second, third)):
                     stats[d] = jnp.where(row == base + p, stats[d] + piece, stats[d])
     for d in range(parts):
-        out_ref[d, heads * slots : heads * slots + STAT, :] = stats[d].astype(bf16)
+        out_ref[place[d], heads * slots : heads * slots + STAT, :] = stats[d].astype(
+            bf16
+        )
 
 
 def attend(parts, around, queries, near, far, text_kv, slots, chunk):
@@ -148,6 +154,49 @@
         out_specs=VM,
         compiler_params=grant(20),
     )(*local(queries, near, far, text_kv))
+
+
+def blend_kernel(got_ref, out_ref, *, slots):
+    dests, rows, _ = out_ref.shape
+    parts = got_ref.shape[0]
+    count = (rows - STAT) // slots
+    row = lax.broadcasted_iota(jnp.int32, (STAT, HD), 0)
+    stat = got_ref[:, rows - STAT : rows, :].astype(f32)
+    stats = [jnp.zeros((STAT, HD), f32)] * dests
+    shares = []
+    for base in range(0, 3 * ((count + 1) // 2), 3):
+        level = stat[:, base] + stat[:, base + 1] + stat[:, base + 2]
+        levels = [level[i : i + dests] for i in range(0, parts, dests)]
+        top = functools.reduce(jnp.maximum, levels)
+        joint = top + jnp.log(sum(jnp.exp(x - top) for x in levels))
+        pad = jnp.zeros((HD - parts, HD), f32)
+        share = jnp.concatenate([jnp.exp(x - joint) for x in levels] + [pad], axis=0)
+        shares.append(share.T)
+        first = joint.astype(bf16).astype(f32)
+        second = (joint - first).astype(bf16).astype(f32)
+        third = joint - first - second
+        for p, piece in enumerate((first, second, third)):
+            for d in range(dests):
+                stats[d] = jnp.where(row == base + p, piece[d : d + 1], stats[d])
+    for d in range(dests):
+        for h in range(count):
+            share = shares[h // 2][slots * (h % 2) : slots * (h % 2 + 1)]
+            total = jnp.zeros((slots, HD), f32)
+            for s in range(d, parts, dests):
+                block = got_ref[s, h * slots : (h + 1) * slots, :].astype(f32)
+                total += block * share[:, s : s + 1]
+            out_ref[d, h * slots : (h + 1) * slots, :] = total.astype(bf16)
+        out_ref[d, rows - STAT : rows, :] = stats[d].astype(bf16)
+
+
+def blend(got, dests, slots):
+    return pl.pallas_call(
+        functools.partial(blend_kernel, slots=slots),
+        out_shape=pltpu.VMEM((dests,) + got.shape[1:], bf16),
+        in_specs=[VM],
+        out_specs=VM,
+        compiler_params=grant(8),
+    )(*local(got))
 
 
 def merge_kernel(got_ref, w_ref, out_ref):
@@ -318,7 +367,9 @@
     gathered = lax.all_gather(gathered, "zh", axis=0, tiled=True)
     far = lax.ppermute(near, "core", trade)
     partial = attend(parts, around, gathered, near, far, text_kv, slots, 192)
-    returned = lax.all_to_all(partial, around, 0, 0, tiled=True)
+    partial = lax.all_to_all(partial, "zq", 0, 0, tiled=True)
+    partial = blend(partial, lax.axis_size("zh"), slots)
+    returned = lax.all_to_all(partial, "zh", 0, 0, tiled=True)
     terms = merge(returned, w_out, groups)
     terms = lax.all_to_all(terms, "head", 0, 0, tiled=True)
     stats = norm(

time: 125 us -> 130 us (1.040)
  blocking collectives: 103 us -> 107 us
    all_to_all x1 -> x2, blocking collectives: 26 us -> 30.6 us  [the longest x1 20.2 us: on_device(): returned = lax.all_to_all(partial, 'zh', 0, 0, tiled=True)]
where the time goes in v7:
time: 130 us; the launch traced here: 129 us
  blocking collectives  107 us (82%)
  Pallas kernels  8.55 us (7%)
  starting transfers between devices  5.74 us (4%)
  waiting for transfers between devices  4.89 us (4%)
  between operations  2.06 us (2%)
    all_gather x1, blocking collectives, on_device(): gathered = lax.all_gather(gathered, 'zh', axis=0, tiled=True)  28.4 us
    all_to_all x1, blocking collectives, on_device(): near = lax.all_to_all(pair, 'y', 0, 0, tiled=True)  22.6 us
    all_to_all x1, blocking collectives, on_device(): returned = lax.all_to_all(partial, 'zh', 0, 0, tiled=True)  20.2 us
    all_to_all x1, blocking collectives, on_device(): terms = lax.all_to_all(terms, 'head', 0, 0, tiled=True)  11.5 us
    all_to_all x1, blocking collectives, on_device(): partial = lax.all_to_all(partial, 'zq', 0, 0, tiled=True)  10.4 us
    all_to_all x1, blocking collectives, on_device(): stats = lax.all_to_all(stats, 'head', 0, 0, tiled=True)  8.27 us
    all_gather x1, blocking collectives, on_device(): gathered = lax.all_gather(query, 'zq', axis=0, tiled=True)  6.06 us
    ppermute x1, waiting for transfers between devices, on_device(): other = lax.ppermute(filled, 'za', trade)  4.89 us
  transfers between devices with their start and end apart: 2, of which 1 were waited for; matrix products, arithmetic and copies ran while one was open for 0% of the time, Pallas kernels for 0%

profile of v7, /device:TPU:24, one launch (start us, length us, event | category | flops | bytes accessed | tf_op | source)
XLA Modules:
  0.0 128.7 jit_solution(7384183485963427440)
XLA Ops:
  1.9 1.2 shard_map.149
  3.2 3.8 %collective-permute-start = (bf16[2,128,384]{2,1,0:T(8,128)(2,1)S(1)}, bf16[2,128,384]{2,1,0:T(8,128)(2,1)S(1)}, u32[]{:S(2)}, u32[]{:S(2)}) collective-permute-start(bf16[2,128,384]{2,1,0:T(8,128)(2,1)S(1)} %get-tuple-element.7.own_ref), channel_id=1, source_target_pairs={{0,32},{32,0},{1,33},{33,1},{2,34},{34,2},{3,35},{35,3},{4,36},{36... | collective-permute-start | bytes 589832 | tf_op jit(solution)/shard_map/ppermute | solution.py:363
  7.0 4.9 %collective-permute-done.other_ref = bf16[2,128,384]{2,1,0:T(8,128)(2,1)S(1)} collective-permute-done((bf16[2,128,384]{2,1,0:T(8,128)(2,1)S(1)}, bf16[2,128,384]{2,1,0:T(8,128)(2,1)S(1)}, u32[]{:S(2)}, u32[]{:S(2)}) %collective-permute-start) | collective-permute-done | bytes 196640 | tf_op jit(solution)/shard_map/ppermute | solution.py:363
  11.9 0.1 shard_map.150
  12.0 0.0 copy-start.9
  12.0 0.0 copy-start.1
  12.0 22.6 %all_to_all.25.a_ref = bf16[4,2,2,128,384]{4,3,2,1,0:T(8,128)(2,1)S(1)} all-to-all(bf16[4,2,2,128,384]{4,3,2,1,0:T(8,128)(2,1)S(1)} %shard_map.150), channel_id=1, replica_groups=mesh['zh'=4,'zq'=2,'za'=2,'y'=4,'core'=2,'head'=4] {'y'}, dimensions={0} | all-to-all | bytes 3145728 | tf_op jit(solution)/shard_map/all_to_all | solution.py:366
  34.6 1.9 %collective-permute-start.1 = (bf16[4,2,2,128,384]{4,3,2,1,0:T(8,128)(2,1)S(1)}, bf16[4,2,2,128,384]{4,3,2,1,0:T(8,128)(2,1)S(1)}, u32[]{:S(2)}, u32[]{:S(2)}) collective-permute-start(bf16[4,2,2,128,384]{4,3,2,1,0:T(8,128)(2,1)S(1)} %all_to_all.25.a_ref), channel_id=1, source_target_pairs={{0,4},{4,0},{1,5},{5,1},{2,6},{6,2},{3,7},{7,3},{8,12},{12,8},{9,1... | collective-permute-start | bytes 4718600 | tf_op jit(solution)/shard_map/ppermute | solution.py:368
  36.6 0.0 copy-done.9
  36.6 6.1 %all_gather.6 = bf16[96,384]{1,0:T(8,128)(2,1)S(1)} all-gather(bf16[48,384]{1,0:T(8,128)(2,1)S(1)} %copy-done.9), channel_id=1, replica_groups=mesh['zh'=4,'zq'=2,'za'=2,'y'=4,'core'=2,'head'=4] {'zq'}, dimensions={0}, use_global_device_ids=true | all-gather | bytes 110592 | tf_op jit(solution)/shard_map/all_gather | solution.py:364
  42.6 28.4 %all_gather.7.q_ref = bf16[384,384]{1,0:T(8,128)(2,1)S(1)} all-gather(bf16[96,384]{1,0:T(8,128)(2,1)S(1)} %all_gather.6), channel_id=1, replica_groups=mesh['zh'=4,'zq'=2,'za'=2,'y'=4,'core'=2,'head'=4] {'zh'}, dimensions={0}, use_global_device_ids=true | all-gather | bytes 368640 | tf_op jit(solution)/shard_map/all_gather | solution.py:367
  71.0 0.0 collective-permute-done.1.b_ref
  71.0 0.0 copy-done.1
  71.0 0.0 copy-start
  71.0 4.5 %shard_map.151 = bf16[8,152,128]{2,1,0:T(8,128)(2,1)S(1)} custom-call(bf16[384,384]{1,0:T(8,128)(2,1)S(1)} %all_gather.7.q_ref, bf16[4,2,2,128,384]{4,3,2,1,0:T(8,128)(2,1)S(1)} %all_to_all.25.a_ref, bf16[4,2,2,128,384]{4,3,2,1,0:T(8,128)(2,1)S(1)} %collective-permute-done.1.b_ref, bf16[2,512,384]{2,1,0:T(8,128)(2,1)S(1)} %copy-done.1), custom_call_target="tpu_custom_call" | custom-call | tf_op jit(solution)/shard_map/pallas_call | solution.py:150
  75.5 10.4 %all_to_all.26.got_ref = bf16[8,152,128]{2,1,0:T(8,128)(2,1)S(1)} all-to-all(bf16[8,152,128]{2,1,0:T(8,128)(2,1)S(1)} %shard_map.151), channel_id=1, replica_groups=mesh['zh'=4,'zq'=2,'za'=2,'y'=4,'core'=2,'head'=4] {'zq'}, dimensions={0} | all-to-all | bytes 622592 | tf_op jit(solution)/shard_map/all_to_all | solution.py:370
  85.9 0.4 shard_map.152
  86.3 20.2 %all_to_all.27.got_ref = bf16[4,152,128]{2,1,0:T(8,128)(2,1)S(1)} all-to-all(bf16[4,152,128]{2,1,0:T(8,128)(2,1)S(1)} %shard_map.152), channel_id=1, replica_groups=mesh['zh'=4,'zq'=2,'za'=2,'y'=4,'core'=2,'head'=4] {'zh'}, dimensions={0} | all-to-all | bytes 311296 | tf_op jit(solution)/shard_map/all_to_all | solution.py:372
  106.5 0.0 copy-done
  106.5 0.0 copy-start.2
  106.5 0.0 copy-start.3
  106.5 0.0 copy-start.6
  106.5 0.0 copy-start.7
  106.5 0.0 copy-start.4
  106.6 0.0 copy-start.5
  106.6 0.0 copy-start.8
  106.6 0.8 shard_map.153
  107.3 11.5 %all_to_all.28.got_ref = bf16[4,48,768]{2,1,0:T(8,128)(2,1)S(1)} all-to-all(bf16[4,48,768]{2,1,0:T(8,128)(2,1)S(1)} %shard_map.153), channel_id=1, replica_groups=mesh['zh'=4,'zq'=2,'za'=2,'y'=4,'core'=2,'head'=4] {'head'}, dimensions={0} | all-to-all | bytes 589824 | tf_op jit(solution)/shard_map/all_to_all | solution.py:374
  118.9 0.0 copy-done.2
  118.9 0.0 copy-done.3
  118.9 0.0 copy-done.6
  118.9 0.0 copy-done.7
  118.9 0.4 shard_map.154
  119.3 8.3 %all_to_all.29.got_ref = f32[4,56,128]{2,1,0:T(8,128)S(1)} all-to-all(f32[4,56,128]{2,1,0:T(8,128)S(1)} %shard_map.154), channel_id=1, replica_groups=mesh['zh'=4,'zq'=2,'za'=2,'y'=4,'core'=2,'head'=4] {'head'}, dimensions={0} | all-to-all | bytes 229376 | tf_op jit(solution)/shard_map/all_to_all | solution.py:378
  127.6 0.0 copy-done.4
  127.6 0.0 copy-done.5
  127.6 0.0 copy-done.8
  127.6 1.1 shard_map.155
Async XLA Ops:
  3.2 8.7 %collective-permute-start = (bf16[2,128,384]{2,1,0:T(8,128)(2,1)S(1)}, bf16[2,128,384]{2,1,0:T(8,128)(2,1)S(1)}, u32[]{:S(2)}, u32[]{:S(2)}) collective-permute-start(bf16[2,128,384]{2,1,0:T(8,128)(2,1)S(1)} %get-tuple-element.7.own_ref), channel_id=1, source_target_pairs={{0,32},{32,0},{1,33},{33,1},{2,34},{34,2},{3,35},{35,3},{4,36},{36... | collective-permute-start | bytes 589832 | tf_op jit(solution)/shard_map/ppermute | solution.py:363
  12.0 24.5 %copy-start.9 = (bf16[48,384]{1,0:T(8,128)(2,1)S(1)}, bf16[48,384]{1,0:T(8,128)(2,1)}, u32[]{:S(2)}) copy-start(bf16[48,384]{1,0:T(8,128)(2,1)} %param.14) | copy-start | bytes 110596
  12.0 59.0 %copy-start.1 = (bf16[2,512,384]{2,1,0:T(8,128)(2,1)S(1)}, bf16[2,512,384]{2,1,0:T(8,128)(2,1)}, u32[]{:S(2)}) copy-start(bf16[2,512,384]{2,1,0:T(8,128)(2,1)} %t_ref.1) | copy-start | bytes 2359300
  34.6 36.4 %collective-permute-start.1 = (bf16[4,2,2,128,384]{4,3,2,1,0:T(8,128)(2,1)S(1)}, bf16[4,2,2,128,384]{4,3,2,1,0:T(8,128)(2,1)S(1)}, u32[]{:S(2)}, u32[]{:S(2)}) collective-permute-start(bf16[4,2,2,128,384]{4,3,2,1,0:T(8,128)(2,1)S(1)} %all_to_all.25.a_ref), channel_id=1, source_target_pairs={{0,4},{4,0},{1,5},{5,1},{2,6},{6,2},{3,7},{7,3},{8,12},{12,8},{9,1... | collective-permute-start | bytes 4718600 | tf_op jit(solution)/shard_map/ppermute | solution.py:368
  71.0 35.5 %copy-start = (bf16[384,3072]{1,0:T(8,128)(2,1)S(1)}, bf16[384,3072]{1,0:T(8,128)(2,1)}, u32[]{:S(2)}) copy-start(bf16[384,3072]{1,0:T(8,128)(2,1)} %w_ref.1) | copy-start | bytes 7077892
  106.5 12.4 %copy-start.2 = (f32[768,64]{0,1:T(8,128)S(1)}, f32[768,64]{0,1:T(8,128)}, u32[]{:S(2)}) copy-start(f32[768,64]{0,1:T(8,128)} %param.24) | copy-start | bytes 589828
  106.5 12.4 %copy-start.3 = (bf16[48,768]{1,0:T(8,128)(2,1)S(1)}, bf16[48,768]{1,0:T(8,128)(2,1)}, u32[]{:S(2)}) copy-start(bf16[48,768]{1,0:T(8,128)(2,1)} %hidden_ref.1) | copy-start | bytes 221188
  106.5 12.4 %copy-start.6 = (f32[768]{0:T(1024)S(1)}, f32[768]{0:T(1024)}, u32[]{:S(2)}) copy-start(f32[768]{0:T(1024)} %param.23) | copy-start | bytes 9220
  106.5 12.4 %copy-start.7 = (f32[768]{0:T(1024)S(1)}, f32[768]{0:T(1024)}, u32[]{:S(2)}) copy-start(f32[768]{0:T(1024)} %param.22) | copy-start | bytes 9220
  106.5 21.0 %copy-start.4 = (f32[128,64]{0,1:T(8,128)S(1)}, f32[128,64]{0,1:T(8,128)}, u32[]{:S(2)}) copy-start(f32[128,64]{0,1:T(8,128)} %param.25) | copy-start | bytes 98308
  106.6 21.0 %copy-start.5 = (f32[128,64]{0,1:T(8,128)S(1)}, f32[128,64]{0,1:T(8,128)}, u32[]{:S(2)}) copy-start(f32[128,64]{0,1:T(8,128)} %param.26) | copy-start | bytes 98308
  106.6 21.0 %copy-start.8 = (s32[48]{0:T(128)S(1)}, s32[48]{0:T(128)}, u32[]{:S(2)}) copy-start(s32[48]{0:T(128)} %param.18) | copy-start | bytes 580

commit v8 on v6

--- a/solution.py
+++ b/solution.py
@@ -83,12 +83,65 @@
     )(*local(own, other))
 
 
-def attend_kernel(q_ref, a_ref, b_ref, t_ref, out_ref, *, chunk, around):
+def attend_part(q, keys, values):
+    scores = [
+        lax.dot_general(q, k, (((1,), (1,)), ((), ())), preferred_element_type=f32)
+        for k in keys
+    ]
+    top = functools.reduce(
+        jnp.maximum, [jnp.max(s, axis=1, keepdims=True) for s in scores]
+    )
+    weights = [jnp.exp2((s - top) * (SCALE * LOG2E)) for s in scores]
+    total = sum(jnp.sum(w, axis=1, keepdims=True) for w in weights)
+    mixed = sum(
+        jnp.dot(w.astype(bf16), v, preferred_element_type=f32)
+        for w, v in zip(weights, values)
+    )
+    return top, total, mixed
+
+
+def flat_keys(ref, side, cols):
+    n = ref.shape[0] * ref.shape[1] * ref.shape[3]
+    return ref[:, :, side, :, cols].reshape(n, HD)
+
+
+def near_kernel(q_ref, a_ref, t_ref, mixed_ref, stat_ref, *, chunk, parts, around):
+    share = t_ref.shape[1] // parts
+    own_text = pl.ds(pl.multiple_of(lax.axis_index(around) * share, share), share)
+    lane = lax.broadcasted_iota(jnp.int32, (chunk, HD), 1)
+    heads = q_ref.shape[1] // HD
+    for start in range(0, q_ref.shape[0], chunk):
+        rows = pl.ds(start, chunk)
+        stat = jnp.zeros((chunk, HD), f32)
+        for h in range(heads):
+            cols = slice(h * HD, (h + 1) * HD)
+            top, total, mixed = attend_part(
+                q_ref[rows, cols],
+                [flat_keys(a_ref, 0, cols), t_ref[0, own_text, cols]],
+                [flat_keys(a_ref, 1, cols), t_ref[1, own_text, cols]],
+            )
+            mixed_ref[rows, cols] = mixed
+            stat = jnp.where(lane == h, top, jnp.where(lane == heads + h, total, stat))
+        stat_ref[rows, :] = stat
+
+
+def attend_near(parts, around, queries, near, text_kv, chunk):
+    return pl.pallas_call(
+        functools.partial(near_kernel, chunk=chunk, parts=parts, around=around),
+        out_shape=(
+            pltpu.VMEM(queries.shape, f32),
+            pltpu.VMEM((queries.shape[0], HD), f32),
+        ),
+        in_specs=[VM] * 3,
+        out_specs=(VM, VM),
+        compiler_params=grant(20),
+    )(*local(queries, near, text_kv))
+
+
+def far_kernel(q_ref, b_ref, mixed_ref, stat_ref, out_ref, *, chunk):
     parts = out_ref.shape[0]
     slots = q_ref.shape[0] // parts
     heads = q_ref.shape[1] // HD
-    share = t_ref.shape[1] // parts
-    own_text = pl.ds(pl.multiple_of(lax.axis_index(around) * share, share), share)
     lane = lax.broadcasted_iota(jnp.int32, (slots, HD), 1)
     slot = lax.broadcasted_iota(jnp.int32, (slots, HD), 0)
     row = lax.broadcasted_iota(jnp.int32, (STAT, HD), 0)
@@ -97,31 +150,22 @@
         cols = slice(h * HD, (h + 1) * HD)
         eye = lane == slot + slots * (h % 2)
         base = 3 * (h // 2)
-        keys, values = [], []
-        for ref in (a_ref, b_ref):
-            n = ref.shape[0] * ref.shape[1] * ref.shape[3]
-            keys.append(ref[:, :, 0, :, cols].reshape(n, HD))
-            values.append(ref[:, :, 1, :, cols].reshape(n, HD))
-        keys.append(t_ref[0, own_text, cols])
-        values.append(t_ref[1, own_text, cols])
         for start in range(0, q_ref.shape[0], chunk):
-            q = q_ref[pl.ds(start, chunk), cols]
-            scores = [
-                lax.dot_general(
-                    q, k, (((1,), (1,)), ((), ())), preferred_element_type=f32
-                )
-                for k in keys
-            ]
-            top = functools.reduce(
-                jnp.maximum, [jnp.max(s, axis=1, keepdims=True) for s in scores]
+            rows = pl.ds(start, chunk)
+            far_top, far_total, mixed = attend_part(
+                q_ref[rows, cols],
+                [flat_keys(b_ref, 0, cols)],
+                [flat_keys(b_ref, 1, cols)],
             )
-            weights = [jnp.exp2((s - top) * (SCALE * LOG2E)) for s in scores]
-            total = sum(jnp.sum(w, axis=1, keepdims=True) for w in weights)
-            mixed = sum(
-                jnp.dot(w.astype(bf16), v, preferred_element_type=f32)
-                for w, v in zip(weights, values)
+            near_top = stat_ref[rows, h : h + 1]
+            near_total = stat_ref[rows, heads + h : heads + h + 1]
+            top = jnp.maximum(near_top, far_top)
+            near_scale = jnp.exp2((near_top - top) * (SCALE * LOG2E))
+            far_scale = jnp.exp2((far_top - top) * (SCALE * LOG2E))
+            total = near_total * near_scale + far_total * far_scale
+            mixed = mixed_ref[rows, cols] * (near_scale / total) + mixed * (
+                far_scale / total
             )
-            mixed = mixed / total
             level = top * SCALE + jnp.log(total)
             for i in range(chunk // slots):
                 d = start // slots + i
@@ -139,15 +183,15 @@
         out_ref[d, heads * slots : heads * slots + STAT, :] = stats[d].astype(bf16)
 
 
-def attend(parts, around, queries, near, far, text_kv, slots, chunk):
+def attend_far(parts, queries, far, mixed, stat, slots, chunk):
     heads = queries.shape[1] // HD
     return pl.pallas_call(
-        functools.partial(attend_kernel, chunk=chunk, around=around),
+        functools.partial(far_kernel, chunk=chunk),
         out_shape=pltpu.VMEM((parts, heads * slots + STAT, HD), bf16),
         in_specs=[VM] * 4,
         out_specs=VM,
         compiler_params=grant(20),
-    )(*local(queries, near, far, text_kv))
+    )(*local(queries, far, mixed, stat))
 
 
 def merge_kernel(got_ref, w_ref, out_ref):
@@ -317,7 +361,8 @@
     near = lax.all_to_all(pair, "y", 0, 0, tiled=True)
     gathered = lax.all_gather(gathered, "zh", axis=0, tiled=True)
     far = lax.ppermute(near, "core", trade)
-    partial = attend(parts, around, gathered, near, far, text_kv, slots, 192)
+    mixed, stat = attend_near(parts, around, gathered, near, text_kv, 192)
+    partial = attend_far(parts, gathered, far, mixed, stat, slots, 192)
     returned = lax.all_to_all(partial, around, 0, 0, tiled=True)
     terms = merge(returned, w_out, groups)
     terms = lax.all_to_all(terms, "head", 0, 0, tiled=True)

time: 125 us -> 128 us (1.024)
  Pallas kernels: 8.21 us -> 11.1 us
    pallas_call x1 -> x2, Pallas kernels: 4.53 us -> 7.46 us  [the longest x1 4.59 us: attend_far(): pl.pallas_call(functools.partial(far_kernel, chunk=chunk), out_shape=pltp...]
  transfers between devices with their start and end apart: 2 -> 2, of which waited for: 1 -> 1; matrix products, arithmetic and copies ran while one was open for 0% -> 0% of each run, Pallas kernels for 0% -> 2%
where the time goes in v8:
time: 128 us; the launch traced here: 127 us
  blocking collectives  103 us (80%)
  Pallas kernels  11.1 us (9%)
  starting transfers between devices  5.74 us (4%)
  waiting for transfers between devices  4.89 us (4%)
  between operations  2.08 us (2%)
    all_gather x1, blocking collectives, on_device(): gathered = lax.all_gather(gathered, 'zh', axis=0, tiled=True)  28.4 us
    all_to_all x1, blocking collectives, on_device(): returned = lax.all_to_all(partial, around, 0, 0, tiled=True)  26 us
    all_to_all x1, blocking collectives, on_device(): near = lax.all_to_all(pair, 'y', 0, 0, tiled=True)  22.6 us
    all_to_all x1, blocking collectives, on_device(): terms = lax.all_to_all(terms, 'head', 0, 0, tiled=True)  11.6 us
    all_to_all x1, blocking collectives, on_device(): stats = lax.all_to_all(stats, 'head', 0, 0, tiled=True)  8.27 us
    all_gather x1, blocking collectives, on_device(): gathered = lax.all_gather(query, 'zq', axis=0, tiled=True)  6.06 us
    ppermute x1, waiting for transfers between devices, on_device(): other = lax.ppermute(filled, 'za', trade)  4.89 us
    pallas_call x1, Pallas kernels, attend_far(): pl.pallas_call(functools.partial(far_kernel, chunk=chunk), out_shape=pltp...  4.59 us
  transfers between devices with their start and end apart: 2, of which 1 were waited for; matrix products, arithmetic and copies ran while one was open for 0% of the time, Pallas kernels for 2%

profile of v8, /device:TPU:24, one launch (start us, length us, event | category | flops | bytes accessed | tf_op | source)
XLA Modules:
  0.0 126.7 jit_solution(223169440428206589)
XLA Ops:
  1.9 1.2 shard_map.149
  3.2 3.8 %collective-permute-start = (bf16[2,128,384]{2,1,0:T(8,128)(2,1)S(1)}, bf16[2,128,384]{2,1,0:T(8,128)(2,1)S(1)}, u32[]{:S(2)}, u32[]{:S(2)}) collective-permute-start(bf16[2,128,384]{2,1,0:T(8,128)(2,1)S(1)} %get-tuple-element.9.own_ref), channel_id=1, source_target_pairs={{0,32},{32,0},{1,33},{33,1},{2,34},{34,2},{3,35},{35,3},{4,36},{36... | collective-permute-start | bytes 589832 | tf_op jit(solution)/shard_map/ppermute | solution.py:358
  7.0 4.9 %collective-permute-done.other_ref = bf16[2,128,384]{2,1,0:T(8,128)(2,1)S(1)} collective-permute-done((bf16[2,128,384]{2,1,0:T(8,128)(2,1)S(1)}, bf16[2,128,384]{2,1,0:T(8,128)(2,1)S(1)}, u32[]{:S(2)}, u32[]{:S(2)}) %collective-permute-start) | collective-permute-done | bytes 196640 | tf_op jit(solution)/shard_map/ppermute | solution.py:358
  11.9 0.1 shard_map.150
  12.0 0.0 copy-start.9
  12.0 0.0 copy-start.1
  12.0 22.6 %all_to_all.20.a_ref = bf16[4,2,2,128,384]{4,3,2,1,0:T(8,128)(2,1)S(1)} all-to-all(bf16[4,2,2,128,384]{4,3,2,1,0:T(8,128)(2,1)S(1)} %shard_map.150), channel_id=1, replica_groups=mesh['zh'=4,'zq'=2,'za'=2,'y'=4,'core'=2,'head'=4] {'y'}, dimensions={0} | all-to-all | bytes 3145728 | tf_op jit(solution)/shard_map/all_to_all | solution.py:361
  34.6 1.9 %collective-permute-start.1 = (bf16[4,2,2,128,384]{4,3,2,1,0:T(8,128)(2,1)S(1)}, bf16[4,2,2,128,384]{4,3,2,1,0:T(8,128)(2,1)S(1)}, u32[]{:S(2)}, u32[]{:S(2)}) collective-permute-start(bf16[4,2,2,128,384]{4,3,2,1,0:T(8,128)(2,1)S(1)} %all_to_all.20.a_ref), channel_id=1, source_target_pairs={{0,4},{4,0},{1,5},{5,1},{2,6},{6,2},{3,7},{7,3},{8,12},{12,8},{9,1... | collective-permute-start | bytes 4718600 | tf_op jit(solution)/shard_map/ppermute | solution.py:363
  36.6 0.0 copy-done.9
  36.6 6.1 %all_gather.6 = bf16[96,384]{1,0:T(8,128)(2,1)S(1)} all-gather(bf16[48,384]{1,0:T(8,128)(2,1)S(1)} %copy-done.9), channel_id=1, replica_groups=mesh['zh'=4,'zq'=2,'za'=2,'y'=4,'core'=2,'head'=4] {'zq'}, dimensions={0}, use_global_device_ids=true | all-gather | bytes 110592 | tf_op jit(solution)/shard_map/all_gather | solution.py:359
  42.6 28.4 %all_gather.7.q_ref = bf16[384,384]{1,0:T(8,128)(2,1)S(1)} all-gather(bf16[96,384]{1,0:T(8,128)(2,1)S(1)} %all_gather.6), channel_id=1, replica_groups=mesh['zh'=4,'zq'=2,'za'=2,'y'=4,'core'=2,'head'=4] {'zh'}, dimensions={0}, use_global_device_ids=true | all-gather | bytes 368640 | tf_op jit(solution)/shard_map/all_gather | solution.py:362
  71.0 0.0 copy-done.1
  71.0 2.9 %shard_map.151 = (f32[384,384]{1,0:T(8,128)S(1)}, f32[384,128]{1,0:T(8,128)S(1)}) custom-call(bf16[384,384]{1,0:T(8,128)(2,1)S(1)} %all_gather.7.q_ref, bf16[4,2,2,128,384]{4,3,2,1,0:T(8,128)(2,1)S(1)} %all_to_all.20.a_ref, bf16[2,512,384]{2,1,0:T(8,128)(2,1)S(1)} %copy-done.1), custom_call_target="tpu_custom_call" | custom-call | tf_op jit(solution)/shard_map/pallas_call | solution.py:129
  73.9 0.0 collective-permute-done.1.b_ref
  73.9 0.0 copy-start
  73.9 4.6 %shard_map.152 = bf16[8,152,128]{2,1,0:T(8,128)(2,1)S(1)} custom-call(bf16[384,384]{1,0:T(8,128)(2,1)S(1)} %all_gather.7.q_ref, bf16[4,2,2,128,384]{4,3,2,1,0:T(8,128)(2,1)S(1)} %collective-permute-done.1.b_ref, f32[384,384]{1,0:T(8,128)S(1)} %get-tuple-element.10.mixed_ref, f32[384,128]{1,0:T(8,128)S(1)} %get-tuple-element.11.stat_ref), custom_call_target="tpu_custom_call" | custom-call | tf_op jit(solution)/shard_map/pallas_call | solution.py:188
  78.5 26.0 %all_to_all.21.got_ref = bf16[8,152,128]{2,1,0:T(8,128)(2,1)S(1)} all-to-all(bf16[8,152,128]{2,1,0:T(8,128)(2,1)S(1)} %shard_map.152), channel_id=1, replica_groups=mesh['zh'=4,'zq'=2,'za'=2,'y'=4,'core'=2,'head'=4] {'zh','zq'}, dimensions={0} | all-to-all | bytes 622592 | tf_op jit(solution)/shard_map/all_to_all | solution.py:366
  104.5 0.0 copy-done
  104.5 0.0 copy-start.2
  104.5 0.0 copy-start.3
  104.5 0.0 copy-start.6
  104.5 0.0 copy-start.7
  104.5 0.0 copy-start.4
  104.5 0.0 copy-start.5
  104.5 0.0 copy-start.8
  104.5 0.8 shard_map.153
  105.4 11.6 %all_to_all.22.got_ref = bf16[4,48,768]{2,1,0:T(8,128)(2,1)S(1)} all-to-all(bf16[4,48,768]{2,1,0:T(8,128)(2,1)S(1)} %shard_map.153), channel_id=1, replica_groups=mesh['zh'=4,'zq'=2,'za'=2,'y'=4,'core'=2,'head'=4] {'head'}, dimensions={0} | all-to-all | bytes 589824 | tf_op jit(solution)/shard_map/all_to_all | solution.py:368
  116.9 0.0 copy-done.2
  116.9 0.0 copy-done.3
  116.9 0.0 copy-done.6
  117.0 0.0 copy-done.7
  117.0 0.4 shard_map.154
  117.4 8.3 %all_to_all.23.got_ref = f32[4,56,128]{2,1,0:T(8,128)S(1)} all-to-all(f32[4,56,128]{2,1,0:T(8,128)S(1)} %shard_map.154), channel_id=1, replica_groups=mesh['zh'=4,'zq'=2,'za'=2,'y'=4,'core'=2,'head'=4] {'head'}, dimensions={0} | all-to-all | bytes 229376 | tf_op jit(solution)/shard_map/all_to_all | solution.py:372
  125.6 0.0 copy-done.4
  125.6 0.0 copy-done.5
  125.6 0.0 copy-done.8
  125.6 1.1 shard_map.155
Async XLA Ops:
  3.2 8.7 %collective-permute-start = (bf16[2,128,384]{2,1,0:T(8,128)(2,1)S(1)}, bf16[2,128,384]{2,1,0:T(8,128)(2,1)S(1)}, u32[]{:S(2)}, u32[]{:S(2)}) collective-permute-start(bf16[2,128,384]{2,1,0:T(8,128)(2,1)S(1)} %get-tuple-element.9.own_ref), channel_id=1, source_target_pairs={{0,32},{32,0},{1,33},{33,1},{2,34},{34,2},{3,35},{35,3},{4,36},{36... | collective-permute-start | bytes 589832 | tf_op jit(solution)/shard_map/ppermute | solution.py:358
  12.0 24.5 %copy-start.9 = (bf16[48,384]{1,0:T(8,128)(2,1)S(1)}, bf16[48,384]{1,0:T(8,128)(2,1)}, u32[]{:S(2)}) copy-start(bf16[48,384]{1,0:T(8,128)(2,1)} %param.14) | copy-start | bytes 110596
  12.0 59.0 %copy-start.1 = (bf16[2,512,384]{2,1,0:T(8,128)(2,1)S(1)}, bf16[2,512,384]{2,1,0:T(8,128)(2,1)}, u32[]{:S(2)}) copy-start(bf16[2,512,384]{2,1,0:T(8,128)(2,1)} %t_ref.1) | copy-start | bytes 2359300
  34.6 39.2 %collective-permute-start.1 = (bf16[4,2,2,128,384]{4,3,2,1,0:T(8,128)(2,1)S(1)}, bf16[4,2,2,128,384]{4,3,2,1,0:T(8,128)(2,1)S(1)}, u32[]{:S(2)}, u32[]{:S(2)}) collective-permute-start(bf16[4,2,2,128,384]{4,3,2,1,0:T(8,128)(2,1)S(1)} %all_to_all.20.a_ref), channel_id=1, source_target_pairs={{0,4},{4,0},{1,5},{5,1},{2,6},{6,2},{3,7},{7,3},{8,12},{12,8},{9,1... | collective-permute-start | bytes 4718600 | tf_op jit(solution)/shard_map/ppermute | solution.py:363
  73.9 30.6 %copy-start = (bf16[384,3072]{1,0:T(8,128)(2,1)S(1)}, bf16[384,3072]{1,0:T(8,128)(2,1)}, u32[]{:S(2)}) copy-start(bf16[384,3072]{1,0:T(8,128)(2,1)} %w_ref.1) | copy-start | bytes 7077892
  104.5 12.5 %copy-start.2 = (f32[768,64]{0,1:T(8,128)S(1)}, f32[768,64]{0,1:T(8,128)}, u32[]{:S(2)}) copy-start(f32[768,64]{0,1:T(8,128)} %param.24) | copy-start | bytes 589828
  104.5 12.5 %copy-start.3 = (bf16[48,768]{1,0:T(8,128)(2,1)S(1)}, bf16[48,768]{1,0:T(8,128)(2,1)}, u32[]{:S(2)}) copy-start(bf16[48,768]{1,0:T(8,128)(2,1)} %hidden_ref.1) | copy-start | bytes 221188
  104.5 12.5 %copy-start.6 = (f32[768]{0:T(1024)S(1)}, f32[768]{0:T(1024)}, u32[]{:S(2)}) copy-start(f32[768]{0:T(1024)} %param.23) | copy-start | bytes 9220
  104.5 12.5 %copy-start.7 = (f32[768]{0:T(1024)S(1)}, f32[768]{0:T(1024)}, u32[]{:S(2)}) copy-start(f32[768]{0:T(1024)} %param.22) | copy-start | bytes 9220
  104.5 21.1 %copy-start.4 = (f32[128,64]{0,1:T(8,128)S(1)}, f32[128,64]{0,1:T(8,128)}, u32[]{:S(2)}) copy-start(f32[128,64]{0,1:T(8,128)} %param.25) | copy-start | bytes 98308
  104.5 21.1 %copy-start.5 = (f32[128,64]{0,1:T(8,128)S(1)}, f32[128,64]{0,1:T(8,128)}, u32[]{:S(2)}) copy-start(f32[128,64]{0,1:T(8,128)} %param.26) | copy-start | bytes 98308
  104.5 21.1 %copy-start.8 = (s32[48]{0:T(128)S(1)}, s32[48]{0:T(128)}, u32[]{:S(2)}) copy-start(s32[48]{0:T(128)} %param.18) | copy-start | bytes 580

commit v9 on v8

--- a/solution.py
+++ b/solution.py
@@ -108,11 +108,9 @@
 def near_kernel(q_ref, a_ref, t_ref, mixed_ref, stat_ref, *, chunk, parts, around):
     share = t_ref.shape[1] // parts
     own_text = pl.ds(pl.multiple_of(lax.axis_index(around) * share, share), share)
-    lane = lax.broadcasted_iota(jnp.int32, (chunk, HD), 1)
     heads = q_ref.shape[1] // HD
     for start in range(0, q_ref.shape[0], chunk):
         rows = pl.ds(start, chunk)
-        stat = jnp.zeros((chunk, HD), f32)
         for h in range(heads):
             cols = slice(h * HD, (h + 1) * HD)
             top, total, mixed = attend_part(
@@ -121,8 +119,8 @@
                 [flat_keys(a_ref, 1, cols), t_ref[1, own_text, cols]],
             )
             mixed_ref[rows, cols] = mixed
-            stat = jnp.where(lane == h, top, jnp.where(lane == heads + h, total, stat))
-        stat_ref[rows, :] = stat
+            stat_ref[0, rows, cols] = jnp.broadcast_to(top, (chunk, HD))
+            stat_ref[1, rows, cols] = jnp.broadcast_to(total, (chunk, HD))
 
 
 def attend_near(parts, around, queries, near, text_kv, chunk):
@@ -130,7 +128,7 @@
         functools.partial(near_kernel, chunk=chunk, parts=parts, around=around),
         out_shape=(
             pltpu.VMEM(queries.shape, f32),
-            pltpu.VMEM((queries.shape[0], HD), f32),
+            pltpu.VMEM((2,) + queries.shape, f32),
         ),
         in_specs=[VM] * 3,
         out_specs=(VM, VM),
@@ -157,15 +155,15 @@
                 [flat_keys(b_ref, 0, cols)],
                 [flat_keys(b_ref, 1, cols)],
             )
-            near_top = stat_ref[rows, h : h + 1]
-            near_total = stat_ref[rows, heads + h : heads + h + 1]
+            near_top = stat_ref[0, rows, cols]
+            near_total = stat_ref[1, rows, cols]
+            far_top = jnp.broadcast_to(far_top, (chunk, HD))
             top = jnp.maximum(near_top, far_top)
             near_scale = jnp.exp2((near_top - top) * (SCALE * LOG2E))
             far_scale = jnp.exp2((far_top - top) * (SCALE * LOG2E))
             total = near_total * near_scale + far_total * far_scale
-            mixed = mixed_ref[rows, cols] * (near_scale / total) + mixed * (
-                far_scale / total
-            )
+            mixed = mixed_ref[rows, cols] * near_scale + mixed * far_scale
+            mixed = mixed / total
             level = top * SCALE + jnp.log(total)
             for i in range(chunk // slots):
                 d = start // slots + i
@@ -361,8 +359,10 @@
     near = lax.all_to_all(pair, "y", 0, 0, tiled=True)
     gathered = lax.all_gather(gathered, "zh", axis=0, tiled=True)
     far = lax.ppermute(near, "core", trade)
-    mixed, stat = attend_near(parts, around, gathered, near, text_kv, 192)
-    partial = attend_far(parts, gathered, far, mixed, stat, slots, 192)
+    mixed, stat = attend_near(parts, around, gathered, near, text_kv, gathered.shape[0])
+    partial = attend_far(
+        parts, gathered, far, mixed, stat, slots, gathered.shape[0]
+    )
     returned = lax.all_to_all(partial, around, 0, 0, tiled=True)
     terms = merge(returned, w_out, groups)
     terms = lax.all_to_all(terms, "head", 0, 0, tiled=True)

time: 128 us -> 125 us (0.977)
  Pallas kernels: 11.1 us -> 8.54 us
    pallas_call x1, Pallas kernels: 4.59 us -> 2.31 us  [attend_far(): pl.pallas_call(functools.partial(far_kernel, chunk=chunk), out_shape=pltp...]
where the time goes in v9:
time: 125 us; the launch traced here: 124 us
  blocking collectives  103 us (82%)
  Pallas kernels  8.54 us (7%)
  starting transfers between devices  5.74 us (5%)
  waiting for transfers between devices  4.89 us (4%)
  between operations  2.08 us (2%)
    all_gather x1, blocking collectives, on_device(): gathered = lax.all_gather(gathered, 'zh', axis=0, tiled=True)  28.4 us
    all_to_all x1, blocking collectives, on_device(): returned = lax.all_to_all(partial, around, 0, 0, tiled=True)  26 us
    all_to_all x1, blocking collectives, on_device(): near = lax.all_to_all(pair, 'y', 0, 0, tiled=True)  22.6 us
    all_to_all x1, blocking collectives, on_device(): terms = lax.all_to_all(terms, 'head', 0, 0, tiled=True)  11.6 us
    all_to_all x1, blocking collectives, on_device(): stats = lax.all_to_all(stats, 'head', 0, 0, tiled=True)  8.27 us
    all_gather x1, blocking collectives, on_device(): gathered = lax.all_gather(query, 'zq', axis=0, tiled=True)  6.06 us
    ppermute x1, waiting for transfers between devices, on_device(): other = lax.ppermute(filled, 'za', trade)  4.89 us
    ppermute x1, starting transfers between devices, on_device(): other = lax.ppermute(filled, 'za', trade)  3.83 us
  transfers between devices with their start and end apart: 2, of which 1 were waited for; matrix products, arithmetic and copies ran while one was open for 0% of the time, Pallas kernels for 2%

profile of v9, /device:TPU:24, one launch (start us, length us, event | category | flops | bytes accessed | tf_op | source)
XLA Modules:
  0.0 124.1 jit_solution(2459138511137650375)
XLA Ops:
  1.9 1.2 shard_map.149
  3.2 3.8 %collective-permute-start = (bf16[2,128,384]{2,1,0:T(8,128)(2,1)S(1)}, bf16[2,128,384]{2,1,0:T(8,128)(2,1)S(1)}, u32[]{:S(2)}, u32[]{:S(2)}) collective-permute-start(bf16[2,128,384]{2,1,0:T(8,128)(2,1)S(1)} %get-tuple-element.9.own_ref), channel_id=1, source_target_pairs={{0,32},{32,0},{1,33},{33,1},{2,34},{34,2},{3,35},{35,3},{4,36},{36... | collective-permute-start | bytes 589832 | tf_op jit(solution)/shard_map/ppermute | solution.py:356
  7.0 4.9 %collective-permute-done.other_ref = bf16[2,128,384]{2,1,0:T(8,128)(2,1)S(1)} collective-permute-done((bf16[2,128,384]{2,1,0:T(8,128)(2,1)S(1)}, bf16[2,128,384]{2,1,0:T(8,128)(2,1)S(1)}, u32[]{:S(2)}, u32[]{:S(2)}) %collective-permute-start) | collective-permute-done | bytes 196640 | tf_op jit(solution)/shard_map/ppermute | solution.py:356
  11.9 0.1 shard_map.150
  12.0 0.0 copy-start.9
  12.0 0.0 copy-start.1
  12.0 22.6 %all_to_all.20.a_ref = bf16[4,2,2,128,384]{4,3,2,1,0:T(8,128)(2,1)S(1)} all-to-all(bf16[4,2,2,128,384]{4,3,2,1,0:T(8,128)(2,1)S(1)} %shard_map.150), channel_id=1, replica_groups=mesh['zh'=4,'zq'=2,'za'=2,'y'=4,'core'=2,'head'=4] {'y'}, dimensions={0} | all-to-all | bytes 3145728 | tf_op jit(solution)/shard_map/all_to_all | solution.py:359
  34.6 1.9 %collective-permute-start.1 = (bf16[4,2,2,128,384]{4,3,2,1,0:T(8,128)(2,1)S(1)}, bf16[4,2,2,128,384]{4,3,2,1,0:T(8,128)(2,1)S(1)}, u32[]{:S(2)}, u32[]{:S(2)}) collective-permute-start(bf16[4,2,2,128,384]{4,3,2,1,0:T(8,128)(2,1)S(1)} %all_to_all.20.a_ref), channel_id=1, source_target_pairs={{0,4},{4,0},{1,5},{5,1},{2,6},{6,2},{3,7},{7,3},{8,12},{12,8},{9,1... | collective-permute-start | bytes 4718600 | tf_op jit(solution)/shard_map/ppermute | solution.py:361
  36.6 0.0 copy-done.9
  36.6 6.1 %all_gather.6 = bf16[96,384]{1,0:T(8,128)(2,1)S(1)} all-gather(bf16[48,384]{1,0:T(8,128)(2,1)S(1)} %copy-done.9), channel_id=1, replica_groups=mesh['zh'=4,'zq'=2,'za'=2,'y'=4,'core'=2,'head'=4] {'zq'}, dimensions={0}, use_global_device_ids=true | all-gather | bytes 110592 | tf_op jit(solution)/shard_map/all_gather | solution.py:357
  42.6 28.4 %all_gather.7.q_ref = bf16[384,384]{1,0:T(8,128)(2,1)S(1)} all-gather(bf16[96,384]{1,0:T(8,128)(2,1)S(1)} %all_gather.6), channel_id=1, replica_groups=mesh['zh'=4,'zq'=2,'za'=2,'y'=4,'core'=2,'head'=4] {'zh'}, dimensions={0}, use_global_device_ids=true | all-gather | bytes 368640 | tf_op jit(solution)/shard_map/all_gather | solution.py:360
  71.0 0.0 copy-done.1
  71.0 2.5 %shard_map.151 = (f32[384,384]{1,0:T(8,128)S(1)}, f32[2,384,384]{2,1,0:T(8,128)S(1)}) custom-call(bf16[384,384]{1,0:T(8,128)(2,1)S(1)} %all_gather.7.q_ref, bf16[4,2,2,128,384]{4,3,2,1,0:T(8,128)(2,1)S(1)} %all_to_all.20.a_ref, bf16[2,512,384]{2,1,0:T(8,128)(2,1)S(1)} %copy-done.1), custom_call_target="tpu_custom_call" | custom-call | tf_op jit(solution)/shard_map/pallas_call | solution.py:127
  73.5 0.0 collective-permute-done.1.b_ref
  73.5 0.0 copy-start
  73.6 2.3 %shard_map.152 = bf16[8,152,128]{2,1,0:T(8,128)(2,1)S(1)} custom-call(bf16[384,384]{1,0:T(8,128)(2,1)S(1)} %all_gather.7.q_ref, bf16[4,2,2,128,384]{4,3,2,1,0:T(8,128)(2,1)S(1)} %collective-permute-done.1.b_ref, f32[384,384]{1,0:T(8,128)S(1)} %get-tuple-element.10.mixed_ref, f32[2,384,384]{2,1,0:T(8,128)S(1)} %get-tuple-element.11.stat_ref), custom_call_target="tpu_custom_call" | custom-call | tf_op jit(solution)/shard_map/pallas_call | solution.py:186
  75.9 26.0 %all_to_all.21.got_ref = bf16[8,152,128]{2,1,0:T(8,128)(2,1)S(1)} all-to-all(bf16[8,152,128]{2,1,0:T(8,128)(2,1)S(1)} %shard_map.152), channel_id=1, replica_groups=mesh['zh'=4,'zq'=2,'za'=2,'y'=4,'core'=2,'head'=4] {'zh','zq'}, dimensions={0} | all-to-all | bytes 622592 | tf_op jit(solution)/shard_map/all_to_all | solution.py:366
  101.9 0.0 copy-done
  101.9 0.0 copy-start.2
  101.9 0.0 copy-start.3
  101.9 0.0 copy-start.6
  101.9 0.0 copy-start.7
  101.9 0.0 copy-start.4
  101.9 0.0 copy-start.5
  101.9 0.0 copy-start.8
  101.9 0.8 shard_map.153
  102.8 11.6 %all_to_all.22.got_ref = bf16[4,48,768]{2,1,0:T(8,128)(2,1)S(1)} all-to-all(bf16[4,48,768]{2,1,0:T(8,128)(2,1)S(1)} %shard_map.153), channel_id=1, replica_groups=mesh['zh'=4,'zq'=2,'za'=2,'y'=4,'core'=2,'head'=4] {'head'}, dimensions={0} | all-to-all | bytes 589824 | tf_op jit(solution)/shard_map/all_to_all | solution.py:368
  114.3 0.0 copy-done.2
  114.3 0.0 copy-done.3
  114.3 0.0 copy-done.6
  114.3 0.0 copy-done.7
  114.3 0.4 shard_map.154
  114.7 8.3 %all_to_all.23.got_ref = f32[4,56,128]{2,1,0:T(8,128)S(1)} all-to-all(f32[4,56,128]{2,1,0:T(8,128)S(1)} %shard_map.154), channel_id=1, replica_groups=mesh['zh'=4,'zq'=2,'za'=2,'y'=4,'core'=2,'head'=4] {'head'}, dimensions={0} | all-to-all | bytes 229376 | tf_op jit(solution)/shard_map/all_to_all | solution.py:372
  123.0 0.0 copy-done.4
  123.0 0.0 copy-done.5
  123.0 0.0 copy-done.8
  123.0 1.1 shard_map.155
Async XLA Ops:
  3.2 8.7 %collective-permute-start = (bf16[2,128,384]{2,1,0:T(8,128)(2,1)S(1)}, bf16[2,128,384]{2,1,0:T(8,128)(2,1)S(1)}, u32[]{:S(2)}, u32[]{:S(2)}) collective-permute-start(bf16[2,128,384]{2,1,0:T(8,128)(2,1)S(1)} %get-tuple-element.9.own_ref), channel_id=1, source_target_pairs={{0,32},{32,0},{1,33},{33,1},{2,34},{34,2},{3,35},{35,3},{4,36},{36... | collective-permute-start | bytes 589832 | tf_op jit(solution)/shard_map/ppermute | solution.py:356
  12.0 24.5 %copy-start.9 = (bf16[48,384]{1,0:T(8,128)(2,1)S(1)}, bf16[48,384]{1,0:T(8,128)(2,1)}, u32[]{:S(2)}) copy-start(bf16[48,384]{1,0:T(8,128)(2,1)} %param.14) | copy-start | bytes 110596
  12.0 59.0 %copy-start.1 = (bf16[2,512,384]{2,1,0:T(8,128)(2,1)S(1)}, bf16[2,512,384]{2,1,0:T(8,128)(2,1)}, u32[]{:S(2)}) copy-start(bf16[2,512,384]{2,1,0:T(8,128)(2,1)} %t_ref.1) | copy-start | bytes 2359300
  34.6 38.9 %collective-permute-start.1 = (bf16[4,2,2,128,384]{4,3,2,1,0:T(8,128)(2,1)S(1)}, bf16[4,2,2,128,384]{4,3,2,1,0:T(8,128)(2,1)S(1)}, u32[]{:S(2)}, u32[]{:S(2)}) collective-permute-start(bf16[4,2,2,128,384]{4,3,2,1,0:T(8,128)(2,1)S(1)} %all_to_all.20.a_ref), channel_id=1, source_target_pairs={{0,4},{4,0},{1,5},{5,1},{2,6},{6,2},{3,7},{7,3},{8,12},{12,8},{9,1... | collective-permute-start | bytes 4718600 | tf_op jit(solution)/shard_map/ppermute | solution.py:361
  73.5 28.3 %copy-start = (bf16[384,3072]{1,0:T(8,128)(2,1)S(1)}, bf16[384,3072]{1,0:T(8,128)(2,1)}, u32[]{:S(2)}) copy-start(bf16[384,3072]{1,0:T(8,128)(2,1)} %w_ref.1) | copy-start | bytes 7077892
  101.9 12.5 %copy-start.2 = (f32[768,64]{0,1:T(8,128)S(1)}, f32[768,64]{0,1:T(8,128)}, u32[]{:S(2)}) copy-start(f32[768,64]{0,1:T(8,128)} %param.24) | copy-start | bytes 589828
  101.9 12.5 %copy-start.3 = (bf16[48,768]{1,0:T(8,128)(2,1)S(1)}, bf16[48,768]{1,0:T(8,128)(2,1)}, u32[]{:S(2)}) copy-start(bf16[48,768]{1,0:T(8,128)(2,1)} %hidden_ref.1) | copy-start | bytes 221188
  101.9 12.5 %copy-start.6 = (f32[768]{0:T(1024)S(1)}, f32[768]{0:T(1024)}, u32[]{:S(2)}) copy-start(f32[768]{0:T(1024)} %param.23) | copy-start | bytes 9220
  101.9 12.5 %copy-start.7 = (f32[768]{0:T(1024)S(1)}, f32[768]{0:T(1024)}, u32[]{:S(2)}) copy-start(f32[768]{0:T(1024)} %param.22) | copy-start | bytes 9220
  101.9 21.1 %copy-start.4 = (f32[128,64]{0,1:T(8,128)S(1)}, f32[128,64]{0,1:T(8,128)}, u32[]{:S(2)}) copy-start(f32[128,64]{0,1:T(8,128)} %param.25) | copy-start | bytes 98308
  101.9 21.1 %copy-start.5 = (f32[128,64]{0,1:T(8,128)S(1)}, f32[128,64]{0,1:T(8,128)}, u32[]{:S(2)}) copy-start(f32[128,64]{0,1:T(8,128)} %param.26) | copy-start | bytes 98308
  101.9 21.1 %copy-start.8 = (s32[48]{0:T(128)S(1)}, s32[48]{0:T(128)}, u32[]{:S(2)}) copy-start(s32[48]{0:T(128)} %param.18) | copy-start | bytes 580

commit v10 on v9

--- a/solution.py
+++ b/solution.py
@@ -67,18 +67,24 @@
     )(count, step_size, *remote(pos, new_kv, cache_kv))
 
 
-def spread_kernel(own_ref, other_ref, out_ref):
+def spread_kernel(own_ref, other_ref, out_ref, sems):
+    copies = []
     for d in range(out_ref.shape[0]):
-        out_ref[d, 0] = own_ref[...]
-        out_ref[d, 1] = other_ref[...]
+        for i, ref in enumerate((own_ref, other_ref)):
+            copies.append(pltpu.make_async_copy(ref, out_ref.at[d, i], sems.at[d, i]))
+    for copy in copies:
+        copy.start()
+    for copy in copies:
+        copy.wait()
 
 
 def spread(own, other, copies):
     return pl.pallas_call(
         spread_kernel,
-        out_shape=pltpu.VMEM((copies, 2) + own.shape, bf16),
+        out_shape=pltpu.HBM((copies, 2) + own.shape, bf16),
         in_specs=[VM] * 2,
-        out_specs=VM,
+        out_specs=pl.BlockSpec(memory_space=pltpu.HBM),
+        scratch_shapes=[pltpu.SemaphoreType.DMA((copies, 2))],
         compiler_params=grant(8),
     )(*local(own, other))
 

time: 125 us -> 127 us (1.016)
  Pallas kernels: 8.54 us -> 9.95 us
where the time goes in v10:
time: 127 us; the launch traced here: 126 us
  blocking collectives  103 us (81%)
  Pallas kernels  9.95 us (8%)
  starting transfers between devices  5.74 us (5%)
  waiting for transfers between devices  4.89 us (4%)
  between operations  2.08 us (2%)
    all_gather x1, blocking collectives, on_device(): gathered = lax.all_gather(gathered, 'zh', axis=0, tiled=True)  28.4 us
    all_to_all x1, blocking collectives, on_device(): returned = lax.all_to_all(partial, around, 0, 0, tiled=True)  26 us
    all_to_all x1, blocking collectives, on_device(): near = lax.all_to_all(pair, 'y', 0, 0, tiled=True)  22.8 us
    all_to_all x1, blocking collectives, on_device(): terms = lax.all_to_all(terms, 'head', 0, 0, tiled=True)  11.6 us
    all_to_all x1, blocking collectives, on_device(): stats = lax.all_to_all(stats, 'head', 0, 0, tiled=True)  8.27 us
    all_gather x1, blocking collectives, on_device(): gathered = lax.all_gather(query, 'zq', axis=0, tiled=True)  6.06 us
    ppermute x1, waiting for transfers between devices, on_device(): other = lax.ppermute(filled, 'za', trade)  4.89 us
    ppermute x1, starting transfers between devices, on_device(): other = lax.ppermute(filled, 'za', trade)  3.83 us
  transfers between devices with their start and end apart: 2, of which 1 were waited for; matrix products, arithmetic and copies ran while one was open for 0% of the time, Pallas kernels for 2%

profile of v10, /device:TPU:24, one launch (start us, length us, event | category | flops | bytes accessed | tf_op | source)
XLA Modules:
  0.0 125.7 jit_solution(13434353522902803107)
XLA Ops:
  1.9 1.2 shard_map.149
  3.2 3.8 %collective-permute-start = (bf16[2,128,384]{2,1,0:T(8,128)(2,1)S(1)}, bf16[2,128,384]{2,1,0:T(8,128)(2,1)S(1)}, u32[]{:S(2)}, u32[]{:S(2)}) collective-permute-start(bf16[2,128,384]{2,1,0:T(8,128)(2,1)S(1)} %get-tuple-element.9.own_ref), channel_id=1, source_target_pairs={{0,32},{32,0},{1,33},{33,1},{2,34},{34,2},{3,35},{35,3},{4,36},{36... | collective-permute-start | bytes 589832 | tf_op jit(solution)/shard_map/ppermute | solution.py:362
  7.0 4.9 %collective-permute-done.other_ref = bf16[2,128,384]{2,1,0:T(8,128)(2,1)S(1)} collective-permute-done((bf16[2,128,384]{2,1,0:T(8,128)(2,1)S(1)}, bf16[2,128,384]{2,1,0:T(8,128)(2,1)S(1)}, u32[]{:S(2)}, u32[]{:S(2)}) %collective-permute-start) | collective-permute-done | bytes 196640 | tf_op jit(solution)/shard_map/ppermute | solution.py:362
  11.9 1.2 shard_map.150
  13.1 0.0 copy-start.9
  13.1 0.0 copy-start.1
  13.2 22.8 %all_to_all.20.a_ref = bf16[4,2,2,128,384]{4,3,2,1,0:T(8,128)(2,1)S(1)} all-to-all(bf16[4,2,2,128,384]{4,3,2,1,0:T(8,128)(2,1)} %shard_map.150), channel_id=1, replica_groups=mesh['zh'=4,'zq'=2,'za'=2,'y'=4,'core'=2,'head'=4] {'y'}, dimensions={0} | all-to-all | bytes 3145728 | tf_op jit(solution)/shard_map/all_to_all | solution.py:365
  36.0 1.9 %collective-permute-start.1 = (bf16[4,2,2,128,384]{4,3,2,1,0:T(8,128)(2,1)S(1)}, bf16[4,2,2,128,384]{4,3,2,1,0:T(8,128)(2,1)S(1)}, u32[]{:S(2)}, u32[]{:S(2)}) collective-permute-start(bf16[4,2,2,128,384]{4,3,2,1,0:T(8,128)(2,1)S(1)} %all_to_all.20.a_ref), channel_id=1, source_target_pairs={{0,4},{4,0},{1,5},{5,1},{2,6},{6,2},{3,7},{7,3},{8,12},{12,8},{9,1... | collective-permute-start | bytes 4718600 | tf_op jit(solution)/shard_map/ppermute | solution.py:367
  37.9 0.0 copy-done.9
  37.9 6.1 %all_gather.6 = bf16[96,384]{1,0:T(8,128)(2,1)S(1)} all-gather(bf16[48,384]{1,0:T(8,128)(2,1)S(1)} %copy-done.9), channel_id=1, replica_groups=mesh['zh'=4,'zq'=2,'za'=2,'y'=4,'core'=2,'head'=4] {'zq'}, dimensions={0}, use_global_device_ids=true | all-gather | bytes 110592 | tf_op jit(solution)/shard_map/all_gather | solution.py:363
  43.9 28.4 %all_gather.7.q_ref = bf16[384,384]{1,0:T(8,128)(2,1)S(1)} all-gather(bf16[96,384]{1,0:T(8,128)(2,1)S(1)} %all_gather.6), channel_id=1, replica_groups=mesh['zh'=4,'zq'=2,'za'=2,'y'=4,'core'=2,'head'=4] {'zh'}, dimensions={0}, use_global_device_ids=true | all-gather | bytes 368640 | tf_op jit(solution)/shard_map/all_gather | solution.py:366
  72.3 0.0 copy-done.1
  72.3 2.7 %shard_map.151 = (f32[384,384]{1,0:T(8,128)S(1)}, f32[2,384,384]{2,1,0:T(8,128)S(1)}) custom-call(bf16[384,384]{1,0:T(8,128)(2,1)S(1)} %all_gather.7.q_ref, bf16[4,2,2,128,384]{4,3,2,1,0:T(8,128)(2,1)S(1)} %all_to_all.20.a_ref, bf16[2,512,384]{2,1,0:T(8,128)(2,1)S(1)} %copy-done.1), custom_call_target="tpu_custom_call" | custom-call | tf_op jit(solution)/shard_map/pallas_call | solution.py:133
  75.0 0.0 collective-permute-done.1.b_ref
  75.0 0.0 copy-start
  75.0 2.5 %shard_map.152 = bf16[8,152,128]{2,1,0:T(8,128)(2,1)S(1)} custom-call(bf16[384,384]{1,0:T(8,128)(2,1)S(1)} %all_gather.7.q_ref, bf16[4,2,2,128,384]{4,3,2,1,0:T(8,128)(2,1)S(1)} %collective-permute-done.1.b_ref, f32[384,384]{1,0:T(8,128)S(1)} %get-tuple-element.10.mixed_ref, f32[2,384,384]{2,1,0:T(8,128)S(1)} %get-tuple-element.11.stat_ref), custom_call_target="tpu_custom_call" | custom-call | tf_op jit(solution)/shard_map/pallas_call | solution.py:192
  77.5 26.0 %all_to_all.21.got_ref = bf16[8,152,128]{2,1,0:T(8,128)(2,1)S(1)} all-to-all(bf16[8,152,128]{2,1,0:T(8,128)(2,1)S(1)} %shard_map.152), channel_id=1, replica_groups=mesh['zh'=4,'zq'=2,'za'=2,'y'=4,'core'=2,'head'=4] {'zh','zq'}, dimensions={0} | all-to-all | bytes 622592 | tf_op jit(solution)/shard_map/all_to_all | solution.py:372
  103.5 0.0 copy-done
  103.5 0.0 copy-start.2
  103.5 0.0 copy-start.3
  103.5 0.0 copy-start.6
  103.5 0.0 copy-start.7
  103.5 0.0 copy-start.4
  103.5 0.0 copy-start.5
  103.5 0.0 copy-start.8
  103.5 0.8 shard_map.153
  104.4 11.6 %all_to_all.22.got_ref = bf16[4,48,768]{2,1,0:T(8,128)(2,1)S(1)} all-to-all(bf16[4,48,768]{2,1,0:T(8,128)(2,1)S(1)} %shard_map.153), channel_id=1, replica_groups=mesh['zh'=4,'zq'=2,'za'=2,'y'=4,'core'=2,'head'=4] {'head'}, dimensions={0} | all-to-all | bytes 589824 | tf_op jit(solution)/shard_map/all_to_all | solution.py:374
  116.0 0.0 copy-done.2
  116.0 0.0 copy-done.3
  116.0 0.0 copy-done.6
  116.0 0.0 copy-done.7
  116.0 0.4 shard_map.154
  116.4 8.3 %all_to_all.23.got_ref = f32[4,56,128]{2,1,0:T(8,128)S(1)} all-to-all(f32[4,56,128]{2,1,0:T(8,128)S(1)} %shard_map.154), channel_id=1, replica_groups=mesh['zh'=4,'zq'=2,'za'=2,'y'=4,'core'=2,'head'=4] {'head'}, dimensions={0} | all-to-all | bytes 229376 | tf_op jit(solution)/shard_map/all_to_all | solution.py:378
  124.6 0.0 copy-done.4
  124.6 0.0 copy-done.5
  124.7 0.0 copy-done.8
  124.7 1.1 shard_map.155
Async XLA Ops:
  3.2 8.7 %collective-permute-start = (bf16[2,128,384]{2,1,0:T(8,128)(2,1)S(1)}, bf16[2,128,384]{2,1,0:T(8,128)(2,1)S(1)}, u32[]{:S(2)}, u32[]{:S(2)}) collective-permute-start(bf16[2,128,384]{2,1,0:T(8,128)(2,1)S(1)} %get-tuple-element.9.own_ref), channel_id=1, source_target_pairs={{0,32},{32,0},{1,33},{33,1},{2,34},{34,2},{3,35},{35,3},{4,36},{36... | collective-permute-start | bytes 589832 | tf_op jit(solution)/shard_map/ppermute | solution.py:362
  13.1 24.7 %copy-start.9 = (bf16[48,384]{1,0:T(8,128)(2,1)S(1)}, bf16[48,384]{1,0:T(8,128)(2,1)}, u32[]{:S(2)}) copy-start(bf16[48,384]{1,0:T(8,128)(2,1)} %param.14) | copy-start | bytes 110596
  13.1 59.2 %copy-start.1 = (bf16[2,512,384]{2,1,0:T(8,128)(2,1)S(1)}, bf16[2,512,384]{2,1,0:T(8,128)(2,1)}, u32[]{:S(2)}) copy-start(bf16[2,512,384]{2,1,0:T(8,128)(2,1)} %t_ref.1) | copy-start | bytes 2359300
  36.0 39.1 %collective-permute-start.1 = (bf16[4,2,2,128,384]{4,3,2,1,0:T(8,128)(2,1)S(1)}, bf16[4,2,2,128,384]{4,3,2,1,0:T(8,128)(2,1)S(1)}, u32[]{:S(2)}, u32[]{:S(2)}) collective-permute-start(bf16[4,2,2,128,384]{4,3,2,1,0:T(8,128)(2,1)S(1)} %all_to_all.20.a_ref), channel_id=1, source_target_pairs={{0,4},{4,0},{1,5},{5,1},{2,6},{6,2},{3,7},{7,3},{8,12},{12,8},{9,1... | collective-permute-start | bytes 4718600 | tf_op jit(solution)/shard_map/ppermute | solution.py:367
  75.0 28.5 %copy-start = (bf16[384,3072]{1,0:T(8,128)(2,1)S(1)}, bf16[384,3072]{1,0:T(8,128)(2,1)}, u32[]{:S(2)}) copy-start(bf16[384,3072]{1,0:T(8,128)(2,1)} %w_ref.1) | copy-start | bytes 7077892
  103.5 12.5 %copy-start.2 = (f32[768,64]{0,1:T(8,128)S(1)}, f32[768,64]{0,1:T(8,128)}, u32[]{:S(2)}) copy-start(f32[768,64]{0,1:T(8,128)} %param.24) | copy-start | bytes 589828
  103.5 12.5 %copy-start.3 = (bf16[48,768]{1,0:T(8,128)(2,1)S(1)}, bf16[48,768]{1,0:T(8,128)(2,1)}, u32[]{:S(2)}) copy-start(bf16[48,768]{1,0:T(8,128)(2,1)} %hidden_ref.1) | copy-start | bytes 221188
  103.5 12.5 %copy-start.6 = (f32[768]{0:T(1024)S(1)}, f32[768]{0:T(1024)}, u32[]{:S(2)}) copy-start(f32[768]{0:T(1024)} %param.23) | copy-start | bytes 9220
  103.5 12.5 %copy-start.7 = (f32[768]{0:T(1024)S(1)}, f32[768]{0:T(1024)}, u32[]{:S(2)}) copy-start(f32[768]{0:T(1024)} %param.22) | copy-start | bytes 9220
  103.5 21.1 %copy-start.4 = (f32[128,64]{0,1:T(8,128)S(1)}, f32[128,64]{0,1:T(8,128)}, u32[]{:S(2)}) copy-start(f32[128,64]{0,1:T(8,128)} %param.25) | copy-start | bytes 98308
  103.5 21.1 %copy-start.5 = (f32[128,64]{0,1:T(8,128)S(1)}, f32[128,64]{0,1:T(8,128)}, u32[]{:S(2)}) copy-start(f32[128,64]{0,1:T(8,128)} %param.26) | copy-start | bytes 98308
  103.5 21.1 %copy-start.8 = (s32[48]{0:T(128)S(1)}, s32[48]{0:T(128)}, u32[]{:S(2)}) copy-start(s32[48]{0:T(128)} %param.18) | copy-start | bytes 580
